TPU v7x, 32 devices: a whole 2x2x4 slice. The times are simulated.
32 devices in a mesh: ctx: 32 (over z, y, x, core).
Axes of the slice: x: 2, y: 2, z: 4, core: 2. Of those that a mesh axis runs over, the one named last changes fastest.
Arguments:
- layer_input: bfloat16 [24576, 768], P('ctx'), may hold values from -6 to 6
- out_grad: bfloat16 [24576, 768], P('ctx'), may hold values from -6 to 6
- doc_starts: int32 [24], replicated, may hold values from 0 to 24576, as said below
- rand_blocks: int32 [384, 12, 3], P('ctx'), may hold values from 0 to 383, as said below
- query_weight: float32 [768, 768], P('ctx'), may hold values from -0.21875 to 0.21875
- query_bias: float32 [768], P('ctx'), may hold values from -1.8 to 1.8
- key_weight: float32 [768, 768], P('ctx'), may hold values from -0.21875 to 0.21875
- value_weight: float32 [768, 768], P('ctx'), may hold values from -0.21875 to 0.21875
- value_bias: float32 [768], P('ctx'), may hold values from -0.12 to 0.12
- output_weight: float32 [768, 768], P('ctx'), may hold values from -2.5 to 2.5
- output_bias: float32 [768], P('ctx'), may hold values from -1.2 to 1.2
- first_gain: float32 [768], P('ctx'), may hold values from 0.5 to 1.5
- first_shift: float32 [768], P('ctx'), may hold values from -1.2 to 1.2
- inner_weight: float32 [768, 3072], P('ctx'), may hold values from -0.21875 to 0.21875
- inner_bias: float32 [3072], P('ctx'), may hold values from -1.2 to 1.2
- outer_weight: float32 [3072, 768], P('ctx'), may hold values from -0.109375 to 0.109375
- outer_bias: float32 [768], P('ctx'), may hold values from -1.2 to 1.2
- second_gain: float32 [768], P('ctx'), may hold values from 0.5 to 1.5
- second_shift: float32 [768], P('ctx'), may hold values from -1.2 to 1.2
Outputs:
- layer_out: bfloat16 [24576, 768], P('ctx')
- grad_input: float32 [24576, 768], P('ctx')
- grad_query_weight: float32 [768, 768], P('ctx')
- grad_query_bias: float32 [768], P('ctx')
- grad_key_weight: float32 [768, 768], P('ctx')
- grad_value_weight: float32 [768, 768], P('ctx')
- grad_value_bias: float32 [768], P('ctx')
- grad_output_weight: float32 [768, 768], P('ctx')
- grad_output_bias: float32 [768], P('ctx')
- grad_first_gain: float32 [768], P('ctx')
- grad_first_shift: float32 [768], P('ctx')
- grad_inner_weight: float32 [768, 3072], P('ctx')
- grad_inner_bias: float32 [3072], P('ctx')
- grad_outer_weight: float32 [3072, 768], P('ctx')
- grad_outer_bias: float32 [768], P('ctx')
- grad_second_gain: float32 [768], P('ctx')
- grad_second_shift: float32 [768], P('ctx')
Inputs may be any that keep to these rules, and one draw needn't show every extreme that they name: `doc_starts`: ascending multiples of 64, the first 0. The entries below 24576 cut the stream into documents of 16 to 32 blocks, one of exactly 32 and one of exactly 16 blocks; every remaining entry at the end equals 24576. rand_blocks[b, h, :] are 3 different blocks of the document of block b, none within one block of b and none among the document's first two blocks. Rows of a document's first two blocks are not read.
All inputs are finite; a program needn't handle non-finite values.
Results may differ from a plain program's by a relative error of at most 0.014.
The roundings to bfloat16 on the way count: a program that leaves them out, or rounds other values in their place, can miss the bound.
Values may be sent and summed in bfloat16 or wider, within the bound.
A program may use at most 144 MiB of HBM per device.

v0:
```python
import math

import jax
import jax.numpy as jnp
from jax import lax
from jax.sharding import PartitionSpec as P

BLOCK = 64
DOC_MIN = 16
DOC_MAX = 32


norm_eps = 1e-06
masked_score = -1e30


def passed_along(value, axis, steps):
    count = lax.axis_size(axis)
    first, last = (max(0, -steps), min(count, count - steps))
    return lax.ppermute(value, axis, [(source, source + steps) for source in range(first, last)])


def layer_norm(hidden, scale_gain, shift_vec):
    row_mean = jnp.mean(hidden, axis=-1, keepdims=True)
    centred = hidden - row_mean
    variance = jnp.mean(centred * centred, axis=-1, keepdims=True)
    return centred * lax.rsqrt(variance + norm_eps) * scale_gain + shift_vec


def gelu_exact(inner_pre):
    return jax.nn.gelu(inner_pre, approximate=False)


def plain_dot(left, right):
    return jnp.dot(left, right, preferred_element_type=jnp.float32)


def rows_dot(left, right):
    return lax.dot_general(
        left, right, (((0,), (0,)), ((), ())), preferred_element_type=jnp.float32
    )


def cols_dot(left, right):
    return lax.dot_general(
        left, right, (((1,), (1,)), ((), ())), preferred_element_type=jnp.float32
    )


def edge_rows(distance, own_blocks):
    return BLOCK * min(own_blocks, DOC_MAX - 1 - (distance - 1) * own_blocks)


def doc_layout(doc_starts, block_ids):
    start_blocks = doc_starts // BLOCK
    before = start_blocks[None, :] <= block_ids[:, None]
    doc_ids = jnp.sum(before.astype(jnp.int32), axis=1) - 1
    first_block = jnp.max(jnp.where(before, start_blocks[None, :], -1), axis=1)
    return (doc_ids, first_block)


def masked_scores(query_rows, key_matrix, allowed, score_scale):
    scores = (
        jnp.einsum("nae,nwe->naw", query_rows, key_matrix, preferred_element_type=jnp.float32)
        * score_scale
    )
    return jnp.where(allowed[:, None, :], scores, masked_score)


def attend_forward(query_rows, key_matrix, value_matrix, allowed, score_scale):
    scores = masked_scores(query_rows, key_matrix, allowed, score_scale)
    row_max = jnp.max(scores, axis=-1, keepdims=True)
    weights = jnp.exp(scores - row_max)
    row_sum = jnp.sum(weights, axis=-1, keepdims=True)
    attention_probability = (weights / row_sum).astype(jnp.bfloat16)
    context_rows = jnp.einsum(
        "acw,awi->aci", attention_probability, value_matrix, preferred_element_type=jnp.float32
    )
    return (context_rows.astype(jnp.bfloat16), row_max + jnp.log(row_sum))


def attend_backward(
    query_rows, key_matrix, value_matrix, allowed, log_total, context_gradient, score_scale
):
    scores = masked_scores(query_rows, key_matrix, allowed, score_scale)
    attention_probability = jnp.exp(scores - log_total)
    grad_prob = jnp.einsum(
        "nae,nwe->naw", context_gradient, value_matrix, preferred_element_type=jnp.float32
    )
    score_gradient = attention_probability * (
        grad_prob - jnp.sum(attention_probability * grad_prob, axis=-1, keepdims=True)
    )
    score_gradient = score_gradient.astype(jnp.bfloat16)
    grad_query = (
        jnp.einsum("acw,awi->aci", score_gradient, key_matrix, preferred_element_type=jnp.float32)
        * score_scale
    )
    grad_key = (
        jnp.einsum("avm,avi->ami", score_gradient, query_rows, preferred_element_type=jnp.float32)
        * score_scale
    )
    grad_value = jnp.einsum(
        "avm,avi->ami",
        attention_probability.astype(jnp.bfloat16),
        context_gradient,
        preferred_element_type=jnp.float32,
    )
    return (grad_query, grad_key, grad_value)


def gather_heads(head_rows, slot_local, glob_start, span_blocks):
    regular = head_rows[slot_local].reshape(slot_local.shape[0], -1, head_rows.shape[2])
    leading = jax.vmap(
        lambda start_at: lax.dynamic_slice_in_dim(head_rows, start_at, span_blocks, 0)
    )(glob_start)
    return (regular, leading.reshape(glob_start.shape[0], -1, head_rows.shape[2]))


def scatter_heads(buf_blocks, slot_local, glob_range, regular, leading):
    head_dim = regular.shape[2]
    block_len = head_dim * 0 + BLOCK
    summed = jnp.zeros((buf_blocks, block_len, head_dim), jnp.float32)
    summed = summed.at[slot_local.reshape(-1)].add(regular.reshape(-1, block_len, head_dim))
    return summed.at[glob_range.reshape(-1)].add(leading.reshape(-1, block_len, head_dim))


def on_device(
    layer_input,
    out_grad,
    doc_starts,
    rand_blocks,
    query_weight,
    query_bias,
    key_weight,
    value_weight,
    value_bias,
    output_weight,
    output_bias,
    first_gain,
    first_shift,
    inner_weight,
    inner_bias,
    outer_weight,
    outer_bias,
    second_gain,
    second_shift,
):
    row_count, model_width = layer_input.shape
    head_count = rand_blocks.shape[1]
    head_dim = model_width // head_count
    own_blocks = row_count // BLOCK
    reach_shards = (DOC_MAX - 2 + own_blocks) // own_blocks
    buf_blocks = (2 * reach_shards + 1) * own_blocks
    span_blocks = DOC_MAX + 1
    score_scale = 1.0 / math.sqrt(head_dim)
    own_first = lax.axis_index("ctx") * own_blocks
    buf_first = own_first - reach_shards * own_blocks
    block_total = own_blocks * lax.axis_size("ctx")
    own_ids = own_first + jnp.arange(own_blocks, dtype=jnp.int32)
    buf_ids = buf_first + jnp.arange(buf_blocks, dtype=jnp.int32)
    own_doc, own_start = doc_layout(doc_starts, own_ids)
    buf_doc = doc_layout(doc_starts, buf_ids)[0]
    buf_doc = jnp.where((buf_ids >= 0) & (buf_ids < block_total), buf_doc, -1)
    glob_own = own_ids - own_start < 2
    window = own_ids[:, None] + jnp.arange(-1, 2, dtype=jnp.int32)[None, :]
    leading_ids = own_start[:, None] + jnp.arange(2, dtype=jnp.int32)[None, :]
    slot_blocks = jnp.concatenate(
        [
            jnp.broadcast_to(window[:, None, :], (own_blocks, head_count, 3)),
            jnp.broadcast_to(leading_ids[:, None, :], (own_blocks, head_count, 2)),
            rand_blocks,
        ],
        axis=2,
    )
    slot_local = jnp.clip(slot_blocks - buf_first, 0, buf_blocks - 1)
    window_ok = buf_doc[slot_local[:, :, :3]] == own_doc[:, None, None]
    leading_ok = jnp.broadcast_to(
        (jnp.abs(leading_ids - own_ids[:, None]) > 1)[:, None, :], (own_blocks, head_count, 2)
    )
    random_ok = jnp.ones(rand_blocks.shape, dtype=bool)
    slot_ok = jnp.repeat(jnp.concatenate([window_ok, leading_ok, random_ok], axis=2), BLOCK, axis=2)
    glob_cap = 2 * ((own_blocks - 1) // DOC_MIN + 1) + 1
    glob_rank = jnp.cumsum(glob_own.astype(jnp.int32)) - 1
    picked = glob_own[None, :] & (
        glob_rank[None, :] == jnp.arange(glob_cap, dtype=jnp.int32)[:, None]
    )
    positions = jnp.arange(own_blocks, dtype=jnp.int32)
    glob_index = jnp.where(
        jnp.any(picked, axis=1),
        jnp.sum(jnp.where(picked, positions[None, :], 0), axis=1),
        own_blocks,
    )
    glob_safe = jnp.minimum(glob_index, own_blocks - 1)
    glob_start = own_ids[glob_safe] - 1 - buf_first
    glob_range = glob_start[:, None] + jnp.arange(span_blocks, dtype=jnp.int32)[None, :]
    glob_ok = jnp.repeat(buf_doc[glob_range] == own_doc[glob_safe][:, None], BLOCK, axis=1)

    def fetch_weights():
        return (
            lax.all_gather(query_weight.astype(jnp.bfloat16), "ctx", axis=0, tiled=True),
            lax.all_gather(query_bias.astype(jnp.bfloat16), "ctx", axis=0, tiled=True),
            lax.all_gather(key_weight.astype(jnp.bfloat16), "ctx", axis=0, tiled=True),
            lax.all_gather(value_weight.astype(jnp.bfloat16), "ctx", axis=0, tiled=True),
            lax.all_gather(value_bias.astype(jnp.bfloat16), "ctx", axis=0, tiled=True),
            lax.all_gather(output_weight.astype(jnp.bfloat16), "ctx", axis=0, tiled=True),
            lax.all_gather(output_bias.astype(jnp.bfloat16), "ctx", axis=0, tiled=True),
            lax.all_gather(first_gain.astype(jnp.bfloat16), "ctx", axis=0, tiled=True),
            lax.all_gather(first_shift.astype(jnp.bfloat16), "ctx", axis=0, tiled=True),
            lax.all_gather(inner_weight.astype(jnp.bfloat16), "ctx", axis=0, tiled=True),
            lax.all_gather(inner_bias.astype(jnp.bfloat16), "ctx", axis=0, tiled=True),
            lax.all_gather(outer_weight.astype(jnp.bfloat16), "ctx", axis=0, tiled=True),
            lax.all_gather(outer_bias.astype(jnp.bfloat16), "ctx", axis=0, tiled=True),
            lax.all_gather(second_gain.astype(jnp.bfloat16), "ctx", axis=0, tiled=True),
            lax.all_gather(second_shift.astype(jnp.bfloat16), "ctx", axis=0, tiled=True),
        )

    def project(weights_all):
        w_query, b_query, w_key, w_value, b_value = weights_all[:5]
        query_rows = (plain_dot(layer_input, w_query) + b_query.astype(jnp.float32)).astype(
            jnp.bfloat16
        )
        key_own = plain_dot(layer_input, w_key).astype(jnp.bfloat16)
        value_own = (plain_dot(layer_input, w_value) + b_value.astype(jnp.float32)).astype(
            jnp.bfloat16
        )
        return (query_rows, key_own, value_own)

    def fetch_near(key_own, value_own):
        key_parts = []
        value_parts = []
        for offset in range(-reach_shards, reach_shards + 1):
            if offset == 0:
                key_parts.append(key_own)
                value_parts.append(value_own)
            else:
                span_rows = edge_rows(abs(offset), own_blocks)
                start_at = 0 if offset > 0 else row_count - span_rows
                far_key, far_value = passed_along(
                    (
                        key_own[start_at : start_at + span_rows],
                        value_own[start_at : start_at + span_rows],
                    ),
                    "ctx",
                    -offset,
                )
                filler = jnp.zeros((row_count - span_rows, model_width), jnp.bfloat16)
                if offset > 0:
                    key_parts.append(jnp.concatenate([far_key, filler], axis=0))
                    value_parts.append(jnp.concatenate([far_value, filler], axis=0))
                else:
                    key_parts.append(jnp.concatenate([filler, far_key], axis=0))
                    value_parts.append(jnp.concatenate([filler, far_value], axis=0))
        return (jnp.concatenate(key_parts, axis=0), jnp.concatenate(value_parts, axis=0))

    def head_slices(query_rows, key_buf, value_buf, head_index):
        column = head_index * head_dim
        query_head = lax.dynamic_slice_in_dim(query_rows, column, head_dim, 1).reshape(
            own_blocks, BLOCK, head_dim
        )
        key_head = lax.dynamic_slice_in_dim(key_buf, column, head_dim, 1).reshape(
            buf_blocks, BLOCK, head_dim
        )
        value_head = lax.dynamic_slice_in_dim(value_buf, column, head_dim, 1).reshape(
            buf_blocks, BLOCK, head_dim
        )
        local_head = jnp.take(slot_local, head_index, axis=1)
        key_reg, key_lead = gather_heads(key_head, local_head, glob_start, span_blocks)
        value_reg, value_lead = gather_heads(value_head, local_head, glob_start, span_blocks)
        return (query_head, key_reg, key_lead, value_reg, value_lead, local_head)

    weights_all = fetch_weights()
    query_rows, key_own, value_own = project(weights_all)
    key_buf, value_buf = fetch_near(key_own, value_own)

    def head_forward(head_index):
        query_head, key_reg, key_lead, value_reg, value_lead, local_head = head_slices(
            query_rows, key_buf, value_buf, head_index
        )
        ok_head = jnp.take(slot_ok, head_index, axis=1)
        context_reg, lse_reg = attend_forward(query_head, key_reg, value_reg, ok_head, score_scale)
        context_lead, lse_lead = attend_forward(
            query_head[glob_safe], key_lead, value_lead, glob_ok, score_scale
        )
        context_head = context_reg.at[glob_index].set(context_lead, mode="drop")
        return (context_head.reshape(row_count, head_dim), lse_reg, lse_lead)

    context_stack, lse_regs, lse_leads = lax.map(
        head_forward, jnp.arange(head_count, dtype=jnp.int32)
    )
    context_rows = jnp.transpose(context_stack, (1, 0, 2)).reshape(row_count, model_width)
    w_output, b_output, g_first, s_first = weights_all[5:9]
    w_inner, b_inner, w_outer, b_outer, g_second, s_second = weights_all[9:]
    input_float = layer_input.astype(jnp.float32)
    resid_one = input_float + plain_dot(context_rows, w_output) + b_output.astype(jnp.float32)
    normed_one, first_pull = jax.vjp(
        layer_norm, resid_one, g_first.astype(jnp.float32), s_first.astype(jnp.float32)
    )
    normed_low = normed_one.astype(jnp.bfloat16)
    ffn_rows = math.gcd(512, row_count)
    ffn_blocks = row_count // ffn_rows

    def ffn_forward(rows_in):
        inner_pre = plain_dot(rows_in, w_inner) + b_inner.astype(jnp.float32)
        active = gelu_exact(inner_pre).astype(jnp.bfloat16)
        return plain_dot(active, w_outer) + b_outer.astype(jnp.float32)

    branch_two = lax.map(
        ffn_forward, normed_low.reshape(ffn_blocks, ffn_rows, model_width)
    ).reshape(row_count, model_width)
    resid_two = normed_one + branch_two
    normed_two, second_pull = jax.vjp(
        layer_norm, resid_two, g_second.astype(jnp.float32), s_second.astype(jnp.float32)
    )
    layer_out = normed_two.astype(jnp.bfloat16)
    weights_back = fetch_weights()
    query_rows, key_own, value_own = project(weights_back)
    key_buf, value_buf = fetch_near(key_own, value_own)
    w_query, b_query, w_key, w_value, b_value, w_output = weights_back[:6]
    w_inner, b_inner, w_outer = weights_back[9:12]
    grad_two, grad_second_gain, grad_second_shift = second_pull(out_grad.astype(jnp.float32))
    grad_two_low = grad_two.astype(jnp.bfloat16)
    grad_outer_bias = jnp.sum(grad_two_low.astype(jnp.float32), axis=0)

    def ffn_backward(carry, block_in):
        acc_inner, acc_outer = carry
        rows_in, grad_rows = block_in
        inner_pre = plain_dot(rows_in, w_inner) + b_inner.astype(jnp.float32)
        active_f, gelu_pull = jax.vjp(gelu_exact, inner_pre)
        active = active_f.astype(jnp.bfloat16)
        grad_active = cols_dot(grad_rows, w_outer)
        grad_inner = gelu_pull(grad_active)[0].astype(jnp.bfloat16)
        acc_outer = acc_outer + rows_dot(active, grad_rows)
        acc_inner = acc_inner + rows_dot(rows_in, grad_inner)
        return (
            (acc_inner, acc_outer),
            (cols_dot(grad_inner, w_inner), jnp.sum(grad_inner.astype(jnp.float32), axis=0)),
        )

    ffn_init = (jnp.zeros(w_inner.shape, jnp.float32), jnp.zeros(w_outer.shape, jnp.float32))
    ffn_inputs = (
        normed_low.reshape(ffn_blocks, ffn_rows, model_width),
        grad_two_low.reshape(ffn_blocks, ffn_rows, model_width),
    )
    (grad_inner_weight, grad_outer_weight), (grad_from_ffn, bias_parts) = lax.scan(
        ffn_backward, ffn_init, ffn_inputs
    )
    grad_inner_bias = jnp.sum(bias_parts, axis=0)
    grad_one = grad_two + grad_from_ffn.reshape(row_count, model_width)
    grad_resid_one, grad_first_gain, grad_first_shift = first_pull(grad_one)
    grad_one_low = grad_resid_one.astype(jnp.bfloat16)
    grad_output_bias = jnp.sum(grad_one_low.astype(jnp.float32), axis=0)
    grad_output_weight = rows_dot(context_rows, grad_one_low)
    context_gradient = cols_dot(grad_one_low, w_output).astype(jnp.bfloat16)

    def head_backward(head_index, carry):
        grad_queries, grad_keys, grad_values = carry
        query_head, key_reg, key_lead, value_reg, value_lead, local_head = head_slices(
            query_rows, key_buf, value_buf, head_index
        )
        ok_head = jnp.take(slot_ok, head_index, axis=1)
        column = head_index * head_dim
        grad_head = lax.dynamic_slice_in_dim(context_gradient, column, head_dim, 1).reshape(
            own_blocks, BLOCK, head_dim
        )
        grad_reg = jnp.where(glob_own[:, None, None], jnp.zeros_like(grad_head), grad_head)
        grad_lead = jnp.take(grad_head, glob_index, axis=0, mode="fill", fill_value=0)
        dq_reg, dk_reg, dv_reg = attend_backward(
            query_head, key_reg, value_reg, ok_head, lse_regs[head_index], grad_reg, score_scale
        )
        dq_lead, dk_lead, dv_lead = attend_backward(
            query_head[glob_safe],
            key_lead,
            value_lead,
            glob_ok,
            lse_leads[head_index],
            grad_lead,
            score_scale,
        )
        dq_head = dq_reg.at[glob_index].add(dq_lead, mode="drop").reshape(row_count, head_dim)
        dk_head = scatter_heads(buf_blocks, local_head, glob_range, dk_reg, dk_lead).reshape(
            -1, head_dim
        )
        dv_head = scatter_heads(buf_blocks, local_head, glob_range, dv_reg, dv_lead).reshape(
            -1, head_dim
        )
        grad_queries = lax.dynamic_update_slice_in_dim(grad_queries, dq_head, column, 1)
        grad_keys = lax.dynamic_update_slice_in_dim(grad_keys, dk_head, column, 1)
        grad_values = lax.dynamic_update_slice_in_dim(grad_values, dv_head, column, 1)
        return (grad_queries, grad_keys, grad_values)

    attn_init = (
        jnp.zeros((row_count, model_width), jnp.float32),
        jnp.zeros((buf_blocks * BLOCK, model_width), jnp.float32),
        jnp.zeros((buf_blocks * BLOCK, model_width), jnp.float32),
    )
    grad_queries, grad_key_buf, grad_value_buf = lax.fori_loop(
        0, head_count, head_backward, attn_init
    )
    own_lower = reach_shards * row_count
    key_total = grad_key_buf[own_lower : own_lower + row_count]
    value_total = grad_value_buf[own_lower : own_lower + row_count]
    for offset in range(-reach_shards, reach_shards + 1):
        if offset != 0:
            lower = (offset + reach_shards) * row_count
            span_rows = edge_rows(abs(offset), own_blocks)
            target = 0 if offset > 0 else row_count - span_rows
            start_at = lower + target
            got_key, got_value = (
                passed_along(
                    grad_key_buf[start_at : start_at + span_rows].astype(jnp.bfloat16),
                    "ctx",
                    offset,
                ).astype(jnp.float32),
                passed_along(
                    grad_value_buf[start_at : start_at + span_rows].astype(jnp.bfloat16),
                    "ctx",
                    offset,
                ).astype(jnp.float32),
            )
            key_total = key_total.at[target : target + span_rows].add(got_key)
            value_total = value_total.at[target : target + span_rows].add(got_value)
    query_low = grad_queries.astype(jnp.bfloat16)
    key_low = key_total.astype(jnp.bfloat16)
    value_low = value_total.astype(jnp.bfloat16)
    grad_query_weight = rows_dot(layer_input, query_low)
    grad_query_bias = jnp.sum(query_low.astype(jnp.float32), axis=0)
    grad_key_weight = rows_dot(layer_input, key_low)
    grad_value_weight = rows_dot(layer_input, value_low)
    grad_value_bias = jnp.sum(value_low.astype(jnp.float32), axis=0)
    grad_input = (
        grad_resid_one
        + cols_dot(query_low, w_query)
        + cols_dot(key_low, w_key)
        + cols_dot(value_low, w_value)
    )
    reduced = (
        lax.psum_scatter(grad_query_weight, "ctx", scatter_dimension=0, tiled=True),
        lax.psum_scatter(grad_query_bias, "ctx", scatter_dimension=0, tiled=True),
        lax.psum_scatter(grad_key_weight, "ctx", scatter_dimension=0, tiled=True),
        lax.psum_scatter(grad_value_weight, "ctx", scatter_dimension=0, tiled=True),
        lax.psum_scatter(grad_value_bias, "ctx", scatter_dimension=0, tiled=True),
        lax.psum_scatter(grad_output_weight, "ctx", scatter_dimension=0, tiled=True),
        lax.psum_scatter(grad_output_bias, "ctx", scatter_dimension=0, tiled=True),
        lax.psum_scatter(grad_first_gain, "ctx", scatter_dimension=0, tiled=True),
        lax.psum_scatter(grad_first_shift, "ctx", scatter_dimension=0, tiled=True),
        lax.psum_scatter(grad_inner_weight, "ctx", scatter_dimension=0, tiled=True),
        lax.psum_scatter(grad_inner_bias, "ctx", scatter_dimension=0, tiled=True),
        lax.psum_scatter(grad_outer_weight, "ctx", scatter_dimension=0, tiled=True),
        lax.psum_scatter(grad_outer_bias, "ctx", scatter_dimension=0, tiled=True),
        lax.psum_scatter(grad_second_gain, "ctx", scatter_dimension=0, tiled=True),
        lax.psum_scatter(grad_second_shift, "ctx", scatter_dimension=0, tiled=True),
    )
    return (layer_out, grad_input) + tuple(reduced)


def solution(mesh):
    in_specs = (
        P("ctx", None),
        P("ctx", None),
        P(),
        P("ctx", None, None),
        P("ctx", None),
        P("ctx"),
        P("ctx", None),
        P("ctx", None),
        P("ctx"),
        P("ctx", None),
        P("ctx"),
        P("ctx"),
        P("ctx"),
        P("ctx", None),
        P("ctx"),
        P("ctx", None),
        P("ctx"),
        P("ctx"),
        P("ctx"),
    )
    out_specs = (
        P("ctx", None),
        P("ctx", None),
        P("ctx", None),
        P("ctx"),
        P("ctx", None),
        P("ctx", None),
        P("ctx"),
        P("ctx", None),
        P("ctx"),
        P("ctx"),
        P("ctx"),
        P("ctx", None),
        P("ctx"),
        P("ctx", None),
        P("ctx"),
        P("ctx"),
        P("ctx"),
    )
    return jax.shard_map(
        on_device, mesh=mesh, in_specs=in_specs, out_specs=out_specs, check_vma=False
    )
```

profile of v0, /device:TPU:6, one launch (start us, length us, event | category | flops | bytes accessed | tf_op | source)
XLA Modules:
  0.0 3203.5 jit_solution(16193227365697337893)
XLA Ops:
  27.8 41.4 %all-reduce.21 = (bf16[768]{0:T(1024)(128)(2,1)}, bf16[768]{0:T(1024)(128)(2,1)S(1)}, bf16[768]{0:T(1024)(128)(2,1)}, bf16[768]{0:T(1024)(128)(2,1)}, bf16[768]{...) all-reduce(bf16[768]{0:T(1024)(128)(2,1)S(1)} %dynamic-update-slice, ...), channel_id=1, replica_groups=mesh['ctx'=32] {'ctx'}, use_global_device_ids=true, to_apply=%add.2 | all-reduce | flops 9216 | bytes 36864
  81.0 42.0 %all-gather.11.cloned.1.call-done = bf16[768,768]{1,0:T(8,128)(2,1)} async-done(((bf16[24,768]{1,0:T(8,128)(2,1)}), bf16[768,768]{1,0:T(8,128)(2,1)}) %all-gather.11.cloned.1.call-update) | async-done | bytes 1179664 | tf_op jit(solution)/shard_map/all_gather | solution.py:203
  159.2 23.3 collective-permute-done.6
  182.6 31.6 collective-permute-start.1
  214.1 33.5 %all-gather.7.cloned.1.call-done = bf16[768,768]{1,0:T(8,128)(2,1)} async-done(((bf16[24,768]{1,0:T(8,128)(2,1)}), bf16[768,768]{1,0:T(8,128)(2,1)}) %all-gather.7.cloned.1.call-update) | async-done | bytes 1179664 | tf_op jit(solution)/shard_map/all_gather | solution.py:200
  278.7 18.1 collective-permute-start.5
  300.2 32.9 %collective-permute-done.4 = bf16[768,768]{1,0:T(8,128)(2,1)S(1)} collective-permute-done((bf16[768,768]{1,0:T(8,128)(2,1)S(1)}, bf16[768,768]{1,0:T(8,128)(2,1)S(1)}, u32[]{:S(2)}, u32[]{:S(2)}) %collective-permute-start.4) | collective-permute-done | bytes 1179680 | tf_op jit(solution)/shard_map/ppermute | solution.py:20
  337.0 365.8 %while.86 = (s32[]{:T(128)}, bf16[12,768,64]{1,2,0:T(8,128)(2,1)}, f32[12,12,64,1]{2,1,3,0:T(8,128)}, f32[12,3,64,1]{2,1,3,0:T(4,128)}, s32[12]{0:T(128)S(1)}, /...) while((s32[]{:T(128)}, bf16[12,768,64]{1,2,0:T(8,128)(2,1)}, ...), condition=%wide.region_12.13_spmd.clone, body=%wide.region_6.12_spmd.clone.sunk | while | flops 210931184 | bytes 29264896 | solution.py:287
  710.1 47.0 %while.85 = (s32[]{:T(128)}, f32[3,256,768]{2,1,0:T(8,128)}, bf16[3,256,768]{2,1,0:T(8,128)(2,1)S(1)}, bf16[768,3072]{1,0:T(8,128)(2,1)}, bf16[3072]{0:T(1024)(1...) while((s32[]{:T(128)}, f32[3,256,768]{2,1,0:T(8,128)}, ...), condition=%wide.region_16.17_spmd, body=%wide.region_15.16_spmd.sunk | while | flops 2468024064 | bytes 10657373 | solution.py:307
  768.1 121.0 %while.87 = (s32[]{:T(128)}, f32[768,3072]{1,0:T(8,128)}, f32[3072,768]{1,0:T(8,128)}, f32[3,256,768]{2,1,0:T(8,128)}, f32[3,3072]{1,0:T(4,128)}, /*index=5*/bf1...) while((s32[]{:T(128)}, f32[768,3072]{1,0:T(8,128)}, ...), condition=%wide.region_23.24_spmd.clone, body=%wide.region_21.23_spmd.clone.sunk | while | flops 6159335424 | bytes 184879472 | solution.py:344
  916.4 1629.6 %while.88 = (s32[]{:T(128)}, bf16[768,768]{1,0:T(8,128)(2,1)}, f32[5376,768]{1,0:T(8,128)}, f32[5376,768]{1,0:T(8,128)}, pred[12,12,512]{2,0,1:T(8,128)(4,1)}, /...) while((s32[]{:T(128)}, bf16[768,768]{1,0:T(8,128)(2,1)}, ...), condition=%wide.region_34.35_spmd.clone.clone, body=%wide.region_26.34_spmd.clone.clone.sunk | while | flops 520922272 | bytes 125673192 | solution.py:396
  988.3 17.9 scatter_fusion.5
  1122.2 17.8 scatter_fusion.5
  1260.4 17.8 scatter_fusion.5
  1394.2 17.8 scatter_fusion.5
  1532.5 17.8 scatter_fusion.5
  1666.3 17.8 scatter_fusion.5
  1804.6 17.8 scatter_fusion.5
  1938.4 17.8 scatter_fusion.5
  2076.9 17.8 scatter_fusion.5
  2210.9 17.8 scatter_fusion.5
  2348.6 17.8 scatter_fusion.5
  2577.5 24.9 collective-permute-done.18
  2602.4 21.8 collective-permute-start.23
  2625.7 19.6 collective-permute-done.21
  2670.8 19.7 collective-permute-start.16
  2700.0 34.2 %collective-permute-done.12 = bf16[448,768]{1,0:T(8,128)(2,1)S(1)} collective-permute-done((bf16[448,768]{1,0:T(8,128)(2,1)S(1)}, bf16[448,768]{1,0:T(8,128)(2,1)S(1)}, u32[]{:S(2)}, u32[]{:S(2)}) %collective-permute-start.12) | collective-permute-done | bytes 688160 | tf_op jit(solution)/shard_map/ppermute | solution.py:20
  2746.7 20.1 collective-permute-done.15
  2786.0 64.2 %all-reduce.20 = (f32[768]{0:T(1024)}, f32[768]{0:T(1024)}, f32[768]{0:T(1024)}, f32[768]{0:T(1024)}, f32[768]{0:T(1024)}, /*index=5*/f32[3072]{0:T(1024)}, f32[768]{0:T(1024)}, f32[768]{0:T(1024)}, f32[768]{0:T(1024)}) all-reduce(f32[768]{0:T(1024)} %convert_reduce_fusion.5, ...), channel_id=3, replica_groups=mesh['ctx'=32] {'ctx'}, use_global_device_ids=true, to_apply=%region_37.38.clone | all-reduce | flops 9216 | bytes 73728
  2867.9 45.7 %reduce-scatter.21.cloned.1.call-done = f32[24,768]{1,0:T(8,128)} async-done(((f32[768,768]{1,0:T(8,128)}), f32[24,768]{1,0:T(8,128)}) %reduce-scatter.21.cloned.1.call-update) | async-done | bytes 73744
  2913.6 141.3 %reduce-scatter.15.cloned.1.call-done = f32[24,3072]{1,0:T(8,128)} async-done(((f32[768,3072]{1,0:T(8,128)}), f32[24,3072]{1,0:T(8,128)}) %reduce-scatter.15.cloned.1.call-update) | async-done | bytes 294928 | tf_op jit(solution)/shard_map/reduce_scatter | solution.py:446
  3054.9 141.5 %reduce-scatter.17.cloned.1.call-done = f32[96,768]{1,0:T(8,128)} async-done(((f32[3072,768]{1,0:T(8,128)}), f32[96,768]{1,0:T(8,128)}) %reduce-scatter.17.cloned.1.call-update) | async-done | bytes 294928 | tf_op jit(solution)/shard_map/reduce_scatter | solution.py:448
  (2054 shorter events, 2197.3 us)
Async XLA Ops:
  7.2 68.0 %all-gather.9.cloned.1.call-start = ((), (), s32[]{:S(2)}) async-start(), calls=%async_computation.7 | async-start | bytes 1216512 | tf_op jit(solution)/shard_map/all_gather | solution.py:202
  8.8 114.2 %all-gather.11.cloned.1.call-start = ((), (), s32[]{:S(2)}) async-start(), calls=%async_computation.8 | async-start | bytes 1216512 | tf_op jit(solution)/shard_map/all_gather | solution.py:203
  10.4 237.3 %all-gather.7.cloned.1.call-start = ((), (), s32[]{:S(2)}) async-start(), calls=%async_computation.6 | async-start | bytes 1216512 | tf_op jit(solution)/shard_map/all_gather | solution.py:200
  11.9 690.8 %all-gather.13.cloned.1.call-start = ((), (), s32[]{:S(2)}) async-start(), calls=%async_computation.9 | async-start | bytes 1216512 | tf_op jit(solution)/shard_map/all_gather | solution.py:205
  13.5 695.0 %all-gather.15.cloned.1.call-start = ((), (), s32[]{:S(2)}) async-start(), calls=%async_computation.10 | async-start | bytes 4866048 | tf_op jit(solution)/shard_map/all_gather | solution.py:209
  15.2 693.3 %all-gather.17.cloned.1.call-start = ((), (), s32[]{:S(2)}) async-start(), calls=%async_computation.11 | async-start | bytes 4866048 | tf_op jit(solution)/shard_map/all_gather | solution.py:211
  16.9 2850.9 %reduce-scatter.13.cloned.1.call-start = ((), (), s32[]{:S(2)}) async-start(), calls=%async_computation.12 | async-start | bytes 2433024 | tf_op jit(solution)/shard_map/reduce_scatter | solution.py:442
  78.7 75.6 %collective-permute-start = (bf16[448,768]{1,0:T(8,128)(2,1)}, bf16[448,768]{1,0:T(8,128)(2,1)}, u32[]{:S(2)}, u32[]{:S(2)}) collective-permute-start(bf16[448,768]{1,0:T(8,128)(2,1)} %get-tuple-element.1239), channel_id=1, source_target_pairs={{0,3},{1,4},{2,5},{3,6},{4,7},{5,8},{6,9},{7,10},{8,11},{9,12},{10... | collective-permute-start | bytes 2064392 | tf_op jit(solution)/shard_map/ppermute | solution.py:20
  125.8 127.9 %collective-permute-start.10 = (bf16[768,768]{1,0:T(8,128)(2,1)S(1)}, bf16[768,768]{1,0:T(8,128)(2,1)S(1)}, u32[]{:S(2)}, u32[]{:S(2)}) collective-permute-start(bf16[768,768]{1,0:T(8,128)(2,1)S(1)} %add_convert_fusion.2), channel_id=1, source_target_pairs={{2,0},{3,1},{4,2},{5,3},{6,4},{7,5},{8,6},{9,7},{10,8},{11,9},{12,... | collective-permute-start | bytes 3538952 | tf_op jit(solution)/shard_map/ppermute | solution.py:20
  129.2 127.7 %collective-permute-start.7 = (bf16[768,768]{1,0:T(8,128)(2,1)S(1)}, bf16[768,768]{1,0:T(8,128)(2,1)}, u32[]{:S(2)}, u32[]{:S(2)}) collective-permute-start(bf16[768,768]{1,0:T(8,128)(2,1)S(1)} %add_convert_fusion.2), channel_id=1, source_target_pairs={{0,2},{1,3},{2,4},{3,5},{4,6},{5,7},{6,8},{7,9},{8,10},{9,11},{10,... | collective-permute-start | bytes 3538952 | tf_op jit(solution)/shard_map/ppermute | solution.py:20
  134.6 48.0 %collective-permute-start.6 = (bf16[448,768]{1,0:T(8,128)(2,1)}, bf16[448,768]{1,0:T(8,128)(2,1)}, u32[]{:S(2)}, u32[]{:S(2)}) collective-permute-start(bf16[448,768]{1,0:T(8,128)(2,1)} %get-tuple-element.1237), channel_id=1, source_target_pairs={{0,3},{1,4},{2,5},{3,6},{4,7},{5,8},{6,9},{7,10},{8,11},{9,12},{10... | collective-permute-start | bytes 2064392 | tf_op jit(solution)/shard_map/ppermute | solution.py:20
  150.8 112.8 %collective-permute-start.8 = (bf16[768,768]{1,0:T(8,128)(2,1)S(1)}, bf16[768,768]{1,0:T(8,128)(2,1)}, u32[]{:S(2)}, u32[]{:S(2)}) collective-permute-start(bf16[768,768]{1,0:T(8,128)(2,1)S(1)} %add_convert_fusion.2), channel_id=1, source_target_pairs={{0,1},{1,2},{2,3},{3,4},{4,5},{5,6},{6,7},{7,8},{8,9},{9,10},{10,1... | collective-permute-start | bytes 3538952 | tf_op jit(solution)/shard_map/ppermute | solution.py:20
  154.3 113.7 %collective-permute-start.9 = (bf16[768,768]{1,0:T(8,128)(2,1)S(1)}, bf16[768,768]{1,0:T(8,128)(2,1)}, u32[]{:S(2)}, u32[]{:S(2)}) collective-permute-start(bf16[768,768]{1,0:T(8,128)(2,1)S(1)} %add_convert_fusion.2), channel_id=1, source_target_pairs={{1,0},{2,1},{3,2},{4,3},{5,4},{6,5},{7,6},{8,7},{9,8},{10,9},{11,1... | collective-permute-start | bytes 3538952 | tf_op jit(solution)/shard_map/ppermute | solution.py:20
  182.6 115.1 %collective-permute-start.1 = (bf16[768,768]{1,0:T(8,128)(2,1)S(1)}, bf16[768,768]{1,0:T(8,128)(2,1)}, u32[]{:S(2)}, u32[]{:S(2)}) collective-permute-start(bf16[768,768]{1,0:T(8,128)(2,1)S(1)} %convolution_convert_fusion.3), channel_id=1, source_target_pairs={{0,2},{1,3},{2,4},{3,5},{4,6},{5,7},{6,8},{7,9},{8,10},{9,11},{10,... | collective-permute-start | bytes 3538952 | tf_op jit(solution)/shard_map/ppermute | solution.py:20
  253.6 46.3 %collective-permute-start.2 = (bf16[768,768]{1,0:T(8,128)(2,1)S(1)}, bf16[768,768]{1,0:T(8,128)(2,1)S(1)}, u32[]{:S(2)}, u32[]{:S(2)}) collective-permute-start(bf16[768,768]{1,0:T(8,128)(2,1)S(1)} %convolution_convert_fusion.3), channel_id=1, source_target_pairs={{0,1},{1,2},{2,3},{3,4},{4,5},{5,6},{6,7},{7,8},{8,9},{9,10},{10,1... | collective-permute-start | bytes 3538952 | tf_op jit(solution)/shard_map/ppermute | solution.py:20
  267.9 65.2 %collective-permute-start.4 = (bf16[768,768]{1,0:T(8,128)(2,1)S(1)}, bf16[768,768]{1,0:T(8,128)(2,1)S(1)}, u32[]{:S(2)}, u32[]{:S(2)}) collective-permute-start(bf16[768,768]{1,0:T(8,128)(2,1)S(1)} %convolution_convert_fusion.3), channel_id=1, source_target_pairs={{2,0},{3,1},{4,2},{5,3},{6,4},{7,5},{8,6},{9,7},{10,8},{11,9},{12,... | collective-permute-start | bytes 3538952 | tf_op jit(solution)/shard_map/ppermute | solution.py:20
  278.7 54.9 %collective-permute-start.5 = (bf16[448,768]{1,0:T(8,128)(2,1)S(1)}, bf16[448,768]{1,0:T(8,128)(2,1)S(1)}, u32[]{:S(2)}, u32[]{:S(2)}) collective-permute-start(bf16[448,768]{1,0:T(8,128)(2,1)S(1)} %copy-done.30), channel_id=1, source_target_pairs={{3,0},{4,1},{5,2},{6,3},{7,4},{8,5},{9,6},{10,7},{11,8},{12,9},{13... | collective-permute-start | bytes 2064392 | tf_op jit(solution)/shard_map/ppermute | solution.py:20
  901.7 1966.2 %reduce-scatter.19.cloned.1.call-start = ((), (), s32[]{:S(2)}) async-start(), calls=%async_computation.15 | async-start | bytes 2433024
  2550.8 317.1 %reduce-scatter.23.cloned.1.call-start = ((), (), s32[]{:S(2)}) async-start(), calls=%async_computation.17 | async-start | bytes 2433024
  2557.5 68.2 %collective-permute-start.19 = (bf16[768,768]{1,0:T(8,128)(2,1)S(1)}, bf16[768,768]{1,0:T(8,128)(2,1)S(1)}, u32[]{:S(2)}, u32[]{:S(2)}) collective-permute-start(bf16[768,768]{1,0:T(8,128)(2,1)S(1)} %get-tuple-element.1225), channel_id=1, source_target_pairs={{2,0},{3,1},{4,2},{5,3},{6,4},{7,5},{8,6},{9,7},{10,8},{11,9},{12,... | collective-permute-start | bytes 3538952 | tf_op jit(solution)/shard_map/ppermute | solution.py:20
  2559.4 66.3 %collective-permute-start.22 = (bf16[768,768]{1,0:T(8,128)(2,1)S(1)}, bf16[768,768]{1,0:T(8,128)(2,1)S(1)}, u32[]{:S(2)}, u32[]{:S(2)}) collective-permute-start(bf16[768,768]{1,0:T(8,128)(2,1)S(1)} %get-tuple-element.1226), channel_id=1, source_target_pairs={{0,2},{1,3},{2,4},{3,5},{4,6},{5,7},{6,8},{7,9},{8,10},{9,11},{10,... | collective-permute-start | bytes 3538952 | tf_op jit(solution)/shard_map/ppermute | solution.py:20
  2567.6 77.8 %collective-permute-start.21 = (bf16[768,768]{1,0:T(8,128)(2,1)S(1)}, bf16[768,768]{1,0:T(8,128)(2,1)S(1)}, u32[]{:S(2)}, u32[]{:S(2)}) collective-permute-start(bf16[768,768]{1,0:T(8,128)(2,1)S(1)} %get-tuple-element.1227), channel_id=1, source_target_pairs={{0,1},{1,2},{2,3},{3,4},{4,5},{5,6},{6,7},{7,8},{8,9},{9,10},{10,1... | collective-permute-start | bytes 3538952 | tf_op jit(solution)/shard_map/ppermute | solution.py:20
  2570.2 75.2 %collective-permute-start.20 = (bf16[768,768]{1,0:T(8,128)(2,1)S(1)}, bf16[768,768]{1,0:T(8,128)(2,1)S(1)}, u32[]{:S(2)}, u32[]{:S(2)}) collective-permute-start(bf16[768,768]{1,0:T(8,128)(2,1)S(1)} %get-tuple-element.1228), channel_id=1, source_target_pairs={{1,0},{2,1},{3,2},{4,3},{5,4},{6,5},{7,6},{8,7},{9,8},{10,9},{11,1... | collective-permute-start | bytes 3538952 | tf_op jit(solution)/shard_map/ppermute | solution.py:20
  2602.4 53.9 %collective-permute-start.23 = (bf16[448,768]{1,0:T(8,128)(2,1)S(1)}, bf16[448,768]{1,0:T(8,128)(2,1)S(1)}, u32[]{:S(2)}, u32[]{:S(2)}) collective-permute-start(bf16[448,768]{1,0:T(8,128)(2,1)S(1)} %get-tuple-element.1223), channel_id=1, source_target_pairs={{0,3},{1,4},{2,5},{3,6},{4,7},{5,8},{6,9},{7,10},{8,11},{9,12},{10... | collective-permute-start | bytes 2064392 | tf_op jit(solution)/shard_map/ppermute | solution.py:20
  2662.2 251.4 %reduce-scatter.21.cloned.1.call-start = ((), (), s32[]{:S(2)}) async-start(), calls=%async_computation.16 | async-start | bytes 2433024
  2668.9 77.7 %collective-permute-start.13 = (bf16[768,768]{1,0:T(8,128)(2,1)S(1)}, bf16[768,768]{1,0:T(8,128)(2,1)S(1)}, u32[]{:S(2)}, u32[]{:S(2)}) collective-permute-start(bf16[768,768]{1,0:T(8,128)(2,1)S(1)} %get-tuple-element.1231), channel_id=1, source_target_pairs={{2,0},{3,1},{4,2},{5,3},{6,4},{7,5},{8,6},{9,7},{10,8},{11,9},{12,... | collective-permute-start | bytes 3538952 | tf_op jit(solution)/shard_map/ppermute | solution.py:20
  2670.8 75.8 %collective-permute-start.16 = (bf16[768,768]{1,0:T(8,128)(2,1)S(1)}, bf16[768,768]{1,0:T(8,128)(2,1)S(1)}, u32[]{:S(2)}, u32[]{:S(2)}) collective-permute-start(bf16[768,768]{1,0:T(8,128)(2,1)S(1)} %get-tuple-element.1232), channel_id=1, source_target_pairs={{0,2},{1,3},{2,4},{3,5},{4,6},{5,7},{6,8},{7,9},{8,10},{9,11},{10,... | collective-permute-start | bytes 3538952 | tf_op jit(solution)/shard_map/ppermute | solution.py:20
  2690.5 76.2 %collective-permute-start.15 = (bf16[768,768]{1,0:T(8,128)(2,1)S(1)}, bf16[768,768]{1,0:T(8,128)(2,1)S(1)}, u32[]{:S(2)}, u32[]{:S(2)}) collective-permute-start(bf16[768,768]{1,0:T(8,128)(2,1)S(1)} %get-tuple-element.1233), channel_id=1, source_target_pairs={{0,1},{1,2},{2,3},{3,4},{4,5},{5,6},{6,7},{7,8},{8,9},{9,10},{10,1... | collective-permute-start | bytes 3538952 | tf_op jit(solution)/shard_map/ppermute | solution.py:20
  2692.4 74.3 %collective-permute-start.14 = (bf16[768,768]{1,0:T(8,128)(2,1)S(1)}, bf16[768,768]{1,0:T(8,128)(2,1)S(1)}, u32[]{:S(2)}, u32[]{:S(2)}) collective-permute-start(bf16[768,768]{1,0:T(8,128)(2,1)S(1)} %get-tuple-element.1234), channel_id=1, source_target_pairs={{1,0},{2,1},{3,2},{4,3},{5,4},{6,5},{7,6},{8,7},{9,8},{10,9},{11,1... | collective-permute-start | bytes 3538952 | tf_op jit(solution)/shard_map/ppermute | solution.py:20
  2696.2 38.0 %collective-permute-start.12 = (bf16[448,768]{1,0:T(8,128)(2,1)S(1)}, bf16[448,768]{1,0:T(8,128)(2,1)S(1)}, u32[]{:S(2)}, u32[]{:S(2)}) collective-permute-start(bf16[448,768]{1,0:T(8,128)(2,1)S(1)} %get-tuple-element.1230), channel_id=1, source_target_pairs={{3,0},{4,1},{5,2},{6,3},{7,4},{8,5},{9,6},{10,7},{11,8},{12,9},{13... | collective-permute-start | bytes 2064392 | tf_op jit(solution)/shard_map/ppermute | solution.py:20
  2778.4 276.5 %reduce-scatter.15.cloned.1.call-start = ((), (), s32[]{:S(2)}) async-start(), calls=%async_computation.13 | async-start | bytes 9732096 | tf_op jit(solution)/shard_map/reduce_scatter | solution.py:446
  2779.2 417.3 %reduce-scatter.17.cloned.1.call-start = ((), (), s32[]{:S(2)}) async-start(), calls=%async_computation.14 | async-start | bytes 9732096 | tf_op jit(solution)/shard_map/reduce_scatter | solution.py:448
  (386 other events, 3974.5 us)
Sparse Core Ops, SparseCore 0:
  11.5 54.2 all-gather.8
  69.3 53.7 all-gather.10
  126.5 121.1 all-gather.6
  250.4 92.7 all-gather.12
  346.5 61.8 all-gather.14
  411.2 61.9 all-gather.16
  901.8 103.1 reduce-scatter.12
  2550.9 128.9 reduce-scatter.18
  2685.8 123.4 reduce-scatter.22
  2815.0 98.6 reduce-scatter.20
  2920.1 134.7 reduce-scatter.14
  3061.3 135.1 reduce-scatter.16
where the time goes:
time: 3250 us; the launch traced here: 3200 us
  local copies, waits for them, and re-layouts  1030 us (32%)
  other arithmetic  766 us (24%)
  waiting for transfers between devices  577 us (18%)
  matrix products  515 us (16%)
  starting transfers between devices  159 us (5%)
  blocking collectives  106 us (3%)
  loops' own time  38.6 us (1%)
    scatter-add x24, other arithmetic, scatter_heads(): summed.at[glob_range.reshape(-1)]  355 us
    scatter-add x24, other arithmetic, scatter_heads(): summed.at[slot_local.reshape(-1)]  247 us
    dynamic_update_slice x12, local copies, waits for them, and re-layouts, head_backward(): lax.dynamic_update_slice_in_dim(grad_values, dv_head, column, 1)  191 us
    dynamic_update_slice x12, local copies, waits for them, and re-layouts, head_backward(): grad_keys = lax.dynamic_update_slice_in_dim(grad_keys, dk_head, column, 1)  185 us
    ppermute x24, waiting for transfers between devices, passed_along(): lax.ppermute(value, axis, [(source, source + steps) for source in range(f...  172 us
    ppermute x24, starting transfers between devices, passed_along(): lax.ppermute(value, axis, [(source, source + steps) for source in range(f...  159 us
    reduce_scatter x1, waiting for transfers between devices, on_device(): lax.psum_scatter(grad_outer_weight, 'ctx', scatter_dimension=0, tiled=True)  142 us
    reduce_scatter x1, waiting for transfers between devices, on_device(): lax.psum_scatter(grad_inner_weight, 'ctx', scatter_dimension=0, tiled=True)  141 us
  transfers between devices with their start and end apart: 36, of which 15 were waited for; matrix products, arithmetic and copies ran while one was open for 64% of the time, Pallas kernels for 0%

commit v1 on v0

v1 whole, which is shorter than its diff:
```python
import functools
import math

import jax
import jax.numpy as jnp
from jax import lax
from jax.experimental import pallas as pl
from jax.experimental.pallas import tpu as pltpu
from jax.sharding import PartitionSpec as P

BLOCK = 64
DOC_MAX = 32
REACH = DOC_MAX - 1
SLOTS = 8
WIDE = SLOTS * BLOCK
CHUNKS = DOC_MAX // SLOTS
LANES = 128

norm_eps = 1e-06
masked_score = -1e30
BF = jnp.bfloat16
F32 = jnp.float32


def passed_along(value, axis, steps):
    count = lax.axis_size(axis)
    first, last = (max(0, -steps), min(count, count - steps))
    return lax.ppermute(value, axis, [(source, source + steps) for source in range(first, last)])


def layer_norm(hidden, scale_gain, shift_vec):
    row_mean = jnp.mean(hidden, axis=-1, keepdims=True)
    centred = hidden - row_mean
    variance = jnp.mean(centred * centred, axis=-1, keepdims=True)
    return centred * lax.rsqrt(variance + norm_eps) * scale_gain + shift_vec


def gelu_exact(inner_pre):
    return jax.nn.gelu(inner_pre, approximate=False)


def plain_dot(left, right):
    return jnp.dot(left, right, preferred_element_type=F32)


def rows_dot(left, right):
    return lax.dot_general(left, right, (((0,), (0,)), ((), ())), preferred_element_type=F32)


def cols_dot(left, right):
    return lax.dot_general(left, right, (((1,), (1,)), ((), ())), preferred_element_type=F32)


def edge_rows(distance, own_blocks):
    return BLOCK * min(own_blocks, DOC_MAX - 1 - (distance - 1) * own_blocks)


def doc_layout(doc_starts, block_ids):
    start_blocks = doc_starts // BLOCK
    before = start_blocks[None, :] <= block_ids[:, None]
    doc_ids = jnp.sum(before.astype(jnp.int32), axis=1) - 1
    first_block = jnp.max(jnp.where(before, start_blocks[None, :], -1), axis=1)
    return (doc_ids, first_block)


def low_half():
    return lax.broadcasted_iota(jnp.int32, (BLOCK, LANES), 1) < LANES // 2


def split_pair(rows):
    half = low_half()
    zero = jnp.zeros_like(rows)
    return jnp.concatenate([jnp.where(half, rows, zero), jnp.where(half, zero, rows)], axis=0)


def join_pair(rows):
    return jnp.where(low_half(), rows[:BLOCK], rows[BLOCK:])


def block_at(ref, position):
    return ref[pl.ds(pl.multiple_of(position * BLOCK, BLOCK), BLOCK), :]


def slots_of(near_ref, rand_ref, block, pair, heads):
    shared = [near_ref[block * 8 + i] for i in range(5)]
    at = (block * heads + 2 * pair) * 3
    chosen = [(rand_ref[at + i], rand_ref[at + 3 + i]) for i in range(3)]
    return shared, chosen


def slot_rows(ref, shared, chosen):
    half = low_half()
    parts = [block_at(ref, i) for i in shared]
    parts += [jnp.where(half, block_at(ref, a), block_at(ref, b)) for a, b in chosen]
    return jnp.concatenate(parts, axis=0)


def slot_bias(near_ref, block):
    after = jnp.where(near_ref[block * 8 + 5] > 0, 0.0, masked_score).astype(F32)
    lead = jnp.where(near_ref[block * 8 + 6] > 0, 0.0, masked_score).astype(F32)
    return after, lead


def forward_kernel(heads, own_blocks, near_ref, rand_ref, glob_ref, q_ref, k_ref, v_ref, o_ref, s_ref):
    pair = pl.program_id(0)
    slot_id = lax.broadcasted_iota(jnp.int32, (1, WIDE), 1) // BLOCK

    def regular(block, carry):
        rows = pl.ds(pl.multiple_of(block * BLOCK, BLOCK), BLOCK)
        shared, chosen = slots_of(near_ref, rand_ref, block, pair, heads)
        queries = split_pair(q_ref[rows, :] * 0.125)
        scores = cols_dot(queries, slot_rows(k_ref, shared, chosen))
        after, lead = slot_bias(near_ref, block)
        scores = scores + jnp.where(slot_id == 2, after, jnp.where(slot_id == 4, lead, 0.0))
        weights = jnp.exp(scores - jnp.max(scores, axis=1, keepdims=True))
        probs = weights * (1.0 / jnp.sum(weights, axis=1, keepdims=True))
        mixed = plain_dot(probs.astype(BF), slot_rows(v_ref, shared, chosen))
        o_ref[rows, :] = join_pair(mixed).astype(BF)
        return carry

    lax.fori_loop(0, own_blocks, regular, 0, unroll=4)

    def whole(block, carry):
        @pl.when(glob_ref[block * 4] > 0)
        def _():
            rows = pl.ds(pl.multiple_of(block * BLOCK, BLOCK), BLOCK)
            first = glob_ref[block * 4 + 1]
            length = glob_ref[block * 4 + 2]
            chunks = (length + SLOTS - 1) // SLOTS
            queries = split_pair(q_ref[rows, :] * 0.125)

            def score(step, top):
                at = pl.ds(pl.multiple_of((first + step * SLOTS) * BLOCK, BLOCK), WIDE)
                scores = cols_dot(queries, k_ref[at, :])
                scores = jnp.where(slot_id < length - step * SLOTS, scores, masked_score)
                s_ref[step] = scores
                return jnp.maximum(top, jnp.max(scores, axis=1, keepdims=True))

            top = lax.fori_loop(0, chunks, score, jnp.full((LANES, 1), masked_score, F32))

            def mix(step, kept):
                total, acc = kept
                at = pl.ds(pl.multiple_of((first + step * SLOTS) * BLOCK, BLOCK), WIDE)
                weights = jnp.exp(s_ref[step] - top)
                return (
                    total + jnp.sum(weights, axis=1, keepdims=True),
                    acc + plain_dot(weights.astype(BF), v_ref[at, :]),
                )

            total, acc = lax.fori_loop(
                0, chunks, mix, (jnp.zeros((LANES, 1), F32), jnp.zeros((LANES, LANES), F32))
            )
            o_ref[rows, :] = join_pair(acc * (1.0 / total)).astype(BF)

        return carry

    lax.fori_loop(0, own_blocks, whole, 0)


def backward_kernel(
    heads, own_blocks, near_ref, rand_ref, glob_ref, q_ref, k_ref, v_ref, c_ref,
    dq_ref, dk_ref, dv_ref, dk_acc, dv_acc, s_ref, p_ref,
):
    pair = pl.program_id(0)
    dk_acc[...] = jnp.zeros_like(dk_acc)
    dv_acc[...] = jnp.zeros_like(dv_acc)
    half = low_half()

    def add_rows(acc, shared, chosen, update):
        for i, position in enumerate(shared):
            at = pl.ds(pl.multiple_of(position * BLOCK, BLOCK), BLOCK)
            acc[at, :] += update[i * BLOCK : (i + 1) * BLOCK]
        for i, (one, two) in enumerate(chosen):
            piece = update[(5 + i) * BLOCK : (6 + i) * BLOCK]
            at = pl.ds(pl.multiple_of(one * BLOCK, BLOCK), BLOCK)
            acc[at, :] += jnp.where(half, piece, 0.0)
            at = pl.ds(pl.multiple_of(two * BLOCK, BLOCK), BLOCK)
            acc[at, :] += jnp.where(half, 0.0, piece)

    def regular(block, carry):
        rows = pl.ds(pl.multiple_of(block * BLOCK, BLOCK), BLOCK)
        shared, chosen = slots_of(near_ref, rand_ref, block, pair, heads)
        queries = split_pair(q_ref[rows, :] * 0.125)
        slope = c_ref[rows, :]
        slope = split_pair(jnp.where(glob_ref[block * 4] > 0, jnp.zeros_like(slope), slope))
        keys = slot_rows(k_ref, shared, chosen)
        scores = cols_dot(keys, queries)
        after, lead = slot_bias(near_ref, block)
        scores = jnp.concatenate(
            [
                scores[: 2 * BLOCK],
                scores[2 * BLOCK : 3 * BLOCK] + after,
                scores[3 * BLOCK : 4 * BLOCK],
                scores[4 * BLOCK : 5 * BLOCK] + lead,
                scores[5 * BLOCK :],
            ],
            axis=0,
        )
        weights = jnp.exp(scores - jnp.max(scores, axis=0, keepdims=True))
        probs = weights * (1.0 / jnp.sum(weights, axis=0, keepdims=True))
        dprobs = cols_dot(slot_rows(v_ref, shared, chosen), slope)
        inner = jnp.sum(probs * dprobs, axis=0, keepdims=True)
        dscores = (probs * (dprobs - inner)).astype(BF)
        dq_ref[rows, :] = (join_pair(rows_dot(dscores, keys)) * 0.125).astype(BF)
        add_rows(dk_acc, shared, chosen, plain_dot(dscores, queries))
        add_rows(dv_acc, shared, chosen, plain_dot(probs.astype(BF), slope))
        return carry

    lax.fori_loop(0, own_blocks, regular, 0, unroll=2)

    def whole(block, carry):
        @pl.when(glob_ref[block * 4] > 0)
        def _():
            rows = pl.ds(pl.multiple_of(block * BLOCK, BLOCK), BLOCK)
            first = glob_ref[block * 4 + 1]
            length = glob_ref[block * 4 + 2]
            chunks = (length + SLOTS - 1) // SLOTS
            queries = split_pair(q_ref[rows, :] * 0.125)
            slope = split_pair(c_ref[rows, :])
            slot_id = lax.broadcasted_iota(jnp.int32, (WIDE, LANES), 0) // BLOCK

            def score(step, top):
                at = pl.ds(pl.multiple_of((first + step * SLOTS) * BLOCK, BLOCK), WIDE)
                scores = cols_dot(k_ref[at, :], queries)
                scores = jnp.where(slot_id < length - step * SLOTS, scores, masked_score)
                s_ref[step] = scores
                p_ref[step] = cols_dot(v_ref[at, :], slope)
                return jnp.maximum(top, jnp.max(scores, axis=0, keepdims=True))

            top = lax.fori_loop(0, chunks, score, jnp.full((1, LANES), masked_score, F32))

            def weigh(step, kept):
                total, inner = kept
                weights = jnp.exp(s_ref[step] - top)
                s_ref[step] = weights
                return (
                    total + jnp.sum(weights, axis=0, keepdims=True),
                    inner + jnp.sum(weights * p_ref[step], axis=0, keepdims=True),
                )

            zero_row = jnp.zeros((1, LANES), F32)
            total, inner = lax.fori_loop(0, chunks, weigh, (zero_row, zero_row))
            scale = 1.0 / total
            inner = inner * scale

            def spread(step, dq_sum):
                at = pl.ds(pl.multiple_of((first + step * SLOTS) * BLOCK, BLOCK), WIDE)
                probs = s_ref[step] * scale
                dscores = (probs * (p_ref[step] - inner)).astype(BF)
                dk_acc[at, :] += plain_dot(dscores, queries)
                dv_acc[at, :] += plain_dot(probs.astype(BF), slope)
                return dq_sum + rows_dot(dscores, k_ref[at, :])

            dq_sum = lax.fori_loop(0, chunks, spread, jnp.zeros((LANES, LANES), F32))
            dq_ref[rows, :] = (join_pair(dq_sum) * 0.125).astype(BF)

        return carry

    lax.fori_loop(0, own_blocks, whole, 0)
    dk_ref[...] = dk_acc[...].astype(BF)
    dv_ref[...] = dv_acc[...].astype(BF)


def attention_calls(row_count, model_width, heads, buf_rows):
    own_blocks = row_count // BLOCK
    pairs = heads // 2
    own = lambda: pl.BlockSpec((row_count, LANES), lambda p, *_: (0, p))
    keys = lambda: pl.BlockSpec((buf_rows, LANES), lambda p, *_: (0, p))
    values = lambda: pl.BlockSpec((buf_rows, LANES), lambda p, *_: (0, p + pairs))
    params = lambda: pltpu.CompilerParams(vmem_limit_bytes=48 * 1024 * 1024)
    forward = pl.pallas_call(
        functools.partial(forward_kernel, heads, own_blocks),
        out_shape=jax.ShapeDtypeStruct((row_count, model_width), BF),
        grid_spec=pltpu.PrefetchScalarGridSpec(
            num_scalar_prefetch=3,
            grid=(pairs,),
            in_specs=[own(), keys(), values()],
            out_specs=own(),
            scratch_shapes=[pltpu.VMEM((CHUNKS, LANES, WIDE), F32)],
        ),
        compiler_params=params(),
        cost_estimate=pl.CostEstimate(
            flops=4 * row_count * WIDE * 2 * model_width, bytes_accessed=4 * buf_rows * model_width,
            transcendentals=row_count * WIDE * heads,
        ),
        name="attend_forward",
    )
    backward = pl.pallas_call(
        functools.partial(backward_kernel, heads, own_blocks),
        out_shape=(
            jax.ShapeDtypeStruct((row_count, model_width), BF),
            jax.ShapeDtypeStruct((buf_rows, model_width), BF),
            jax.ShapeDtypeStruct((buf_rows, model_width), BF),
        ),
        grid_spec=pltpu.PrefetchScalarGridSpec(
            num_scalar_prefetch=3,
            grid=(pairs,),
            in_specs=[own(), keys(), values(), own()],
            out_specs=[own(), keys(), keys()],
            scratch_shapes=[
                pltpu.VMEM((buf_rows, LANES), F32),
                pltpu.VMEM((buf_rows, LANES), F32),
                pltpu.VMEM((CHUNKS, WIDE, LANES), F32),
                pltpu.VMEM((CHUNKS, WIDE, LANES), F32),
            ],
        ),
        compiler_params=params(),
        cost_estimate=pl.CostEstimate(
            flops=10 * row_count * WIDE * 2 * model_width, bytes_accessed=8 * buf_rows * model_width,
            transcendentals=row_count * WIDE * heads,
        ),
        name="attend_backward",
    )
    return forward, backward


def on_device(
    layer_input, out_grad, doc_starts, rand_blocks, query_weight, query_bias, key_weight, value_weight,
    value_bias, output_weight, output_bias, first_gain, first_shift, inner_weight, inner_bias,
    outer_weight, outer_bias, second_gain, second_shift,
):
    row_count, model_width = layer_input.shape
    head_count = rand_blocks.shape[1]
    devices = lax.axis_size("ctx")
    own_blocks = row_count // BLOCK
    reach_shards = (REACH - 1 + own_blocks) // own_blocks
    buf_blocks = 2 * REACH + own_blocks
    own_first = lax.axis_index("ctx") * own_blocks
    buf_first = own_first - REACH
    block_total = own_blocks * devices
    own_ids = own_first + jnp.arange(own_blocks, dtype=jnp.int32)
    own_doc, own_start = doc_layout(doc_starts, own_ids)
    next_doc = doc_layout(doc_starts, own_ids + 1)[0]
    start_blocks = doc_starts // BLOCK
    later = start_blocks[None, :] > own_ids[:, None]
    doc_end = jnp.min(jnp.where(later, start_blocks[None, :], block_total), axis=1)
    glob_own = own_ids - own_start < 2

    def local(ids):
        return jnp.clip(ids - buf_first, 0, buf_blocks - 1).astype(jnp.int32)

    near = jnp.stack(
        [
            local(own_ids - 1),
            local(own_ids),
            local(own_ids + 1),
            local(own_start),
            local(own_start + 1),
            ((own_ids + 1 < block_total) & (next_doc == own_doc)).astype(jnp.int32),
            (own_ids - own_start > 2).astype(jnp.int32),
            jnp.zeros_like(own_ids),
        ],
        axis=1,
    ).reshape(-1)
    picks = local(rand_blocks).reshape(-1)
    spans = jnp.stack(
        [glob_own.astype(jnp.int32), local(own_start), doc_end - own_start, jnp.zeros_like(own_ids)], axis=1
    ).reshape(-1)
    attend, attend_back = attention_calls(row_count, model_width, head_count, buf_blocks * BLOCK)

    def gathered(value):
        return lax.all_gather(value, "ctx", axis=0, tiled=True)

    vectors = (
        query_bias, value_bias, output_bias, first_gain, first_shift, outer_bias, second_gain, second_shift, inner_bias,
    )
    w_qkv = gathered(jnp.concatenate([query_weight, key_weight, value_weight], axis=1).astype(BF))
    vector_all = gathered(jnp.concatenate(vectors).astype(BF)[None, :])
    unit = query_bias.shape[0]
    b_query, b_value, b_output, g_first, s_first, b_outer, g_second, s_second = [
        vector_all[:, i * unit : (i + 1) * unit].reshape(-1).astype(F32) for i in range(8)
    ]
    b_inner = vector_all[:, 8 * unit :].reshape(-1).astype(F32)
    w_late = gathered(jnp.concatenate([output_weight, inner_weight], axis=1).astype(BF))
    w_output, w_inner = w_late[:, :model_width], w_late[:, model_width:]
    w_outer = gathered(outer_weight.astype(BF))

    b_qkv = jnp.concatenate([b_query, jnp.zeros_like(b_query), b_value])
    qkv = (plain_dot(layer_input, w_qkv) + b_qkv).astype(BF)
    query_rows, kv_own = qkv[:, :model_width], qkv[:, model_width:]
    parts = []
    for offset in range(-reach_shards, reach_shards + 1):
        if offset == 0:
            parts.append(kv_own)
        else:
            span_rows = edge_rows(abs(offset), own_blocks)
            start_at = 0 if offset > 0 else row_count - span_rows
            parts.append(passed_along(kv_own[start_at : start_at + span_rows], "ctx", -offset))
    kv_buf = jnp.concatenate(parts, axis=0)

    context_rows = attend(near, picks, spans, query_rows, kv_buf, kv_buf)

    input_float = layer_input.astype(F32)
    resid_one = input_float + plain_dot(context_rows, w_output) + b_output
    normed_one, first_pull = jax.vjp(layer_norm, resid_one, g_first, s_first)
    normed_low = normed_one.astype(BF)
    inner_pre = plain_dot(normed_low, w_inner) + b_inner
    active_f, gelu_pull = jax.vjp(gelu_exact, inner_pre)
    active = active_f.astype(BF)
    resid_two = normed_one + plain_dot(active, w_outer) + b_outer
    normed_two, second_pull = jax.vjp(layer_norm, resid_two, g_second, s_second)
    layer_out = normed_two.astype(BF)

    def scattered(value):
        return lax.psum_scatter(value.astype(BF), "ctx", scatter_dimension=0, tiled=True).astype(F32)

    grad_two, grad_second_gain, grad_second_shift = second_pull(out_grad.astype(F32))
    grad_two_low = grad_two.astype(BF)
    grad_outer_bias = jnp.sum(grad_two_low.astype(F32), axis=0)
    grad_outer_weight = scattered(rows_dot(active, grad_two_low))
    grad_inner = gelu_pull(cols_dot(grad_two_low, w_outer))[0].astype(BF)
    grad_inner_bias = jnp.sum(grad_inner.astype(F32), axis=0)
    grad_inner_weight = scattered(rows_dot(normed_low, grad_inner))
    grad_one = grad_two + cols_dot(grad_inner, w_inner)
    grad_resid_one, grad_first_gain, grad_first_shift = first_pull(grad_one)
    grad_one_low = grad_resid_one.astype(BF)
    grad_output_bias = jnp.sum(grad_one_low.astype(F32), axis=0)
    grad_output_weight = rows_dot(context_rows, grad_one_low)
    context_gradient = cols_dot(grad_one_low, w_output).astype(BF)

    query_low, grad_key_buf, grad_value_buf = attend_back(
        near, picks, spans, query_rows, kv_buf, kv_buf, context_gradient
    )
    own_lower = REACH * BLOCK
    grad_kv_buf = jnp.concatenate([grad_key_buf, grad_value_buf], axis=1)
    kv_total = grad_kv_buf[own_lower : own_lower + row_count].astype(F32)
    lower = 0
    for offset in range(-reach_shards, reach_shards + 1):
        if offset == 0:
            lower += row_count
            continue
        span_rows = edge_rows(abs(offset), own_blocks)
        target = 0 if offset > 0 else row_count - span_rows
        got = passed_along(grad_kv_buf[lower : lower + span_rows], "ctx", offset).astype(F32)
        kv_total = kv_total + jnp.pad(got, ((target, row_count - span_rows - target), (0, 0)))
        lower += span_rows
    qkv_low = jnp.concatenate([query_low, kv_total.astype(BF)], axis=1)
    grad_qkv_weight = rows_dot(layer_input, qkv_low)
    grad_qkv_bias = jnp.sum(qkv_low.astype(F32), axis=0)
    grad_input = grad_resid_one + cols_dot(qkv_low, w_qkv)
    attn_grads = scattered(jnp.concatenate([grad_qkv_weight, grad_output_weight], axis=1))
    vector_grads = jnp.concatenate(
        [
            value.reshape(devices, -1)
            for value in (
                grad_qkv_bias[:model_width], grad_qkv_bias[2 * model_width :], grad_output_bias, grad_first_gain,
                grad_first_shift, grad_outer_bias, grad_second_gain, grad_second_shift, grad_inner_bias,
            )
        ],
        axis=1,
    )
    vector_sums = lax.psum_scatter(vector_grads, "ctx", scatter_dimension=0, tiled=True)[0]
    v_query, v_value, v_output, v_gain1, v_shift1, v_outer, v_gain2, v_shift2 = [
        vector_sums[i * unit : (i + 1) * unit] for i in range(8)
    ]
    v_inner = vector_sums[8 * unit :]
    m = model_width
    return (
        layer_out, grad_input, attn_grads[:, :m], v_query, attn_grads[:, m : 2 * m], attn_grads[:, 2 * m : 3 * m],
        v_value, attn_grads[:, 3 * m :], v_output, v_gain1, v_shift1, grad_inner_weight, v_inner,
        grad_outer_weight, v_outer, v_gain2, v_shift2,
    )


def solution(mesh):
    rows, line = P("ctx", None), P("ctx")
    in_specs = (
        rows, rows, P(), P("ctx", None, None), rows, line, rows, rows, line, rows, line, line, line, rows, line, rows,
        line, line, line,
    )
    out_specs = (
        rows, rows, rows, line, rows, rows, line, rows, line, line, line, rows, line, rows, line, line, line,
    )
    return jax.shard_map(on_device, mesh=mesh, in_specs=in_specs, out_specs=out_specs, check_vma=False)
```

time: 3250 us -> 884 us (0.27); the launches traced: 3200 us -> 876 us
  local copies, waits for them, and re-layouts: 1030 us -> 88.4 us
  other arithmetic: 766 us -> 33.7 us
  matrix products: 515 us -> 92.4 us
  waiting for transfers between devices: 577 us -> 248 us
  Pallas kernels: 0 us -> 124 us
  loops' own time: 38.6 us -> 0 us
    scatter-add x64 -> x0, other arithmetic: 613 us -> none  [the longest x24 355 us: scatter_heads(): summed.at[glob_range.reshape(-1)]]
    dynamic_update_slice x63 -> x0, local copies, waits for them, and re-layouts: 431 us -> none  [the longest x12 191 us: head_backward(): lax.dynamic_update_slice_in_dim(grad_values, dv_head, column, 1)]
    dot_general x154 -> x4, matrix products: 341 us -> 46.6 us  [plain_dot(): return jnp.dot(left, right, preferred_element_type=F32)]
    reduce_scatter x3 -> x2, waiting for transfers between devices: 283 us -> 0.01 us  [scattered(): lax.psum_scatter(value.astype(BF), 'ctx', scatter_dimension=0, tiled=True)]
    gather x138 -> x0, local copies, waits for them, and re-layouts: 224 us -> none  [the longest x48 96 us: gather_heads(): lax.dynamic_slice_in_dim(head_rows, start_at, span_blocks, 0)]
    pallas_call x0 -> x2, Pallas kernels: none -> 124 us  [the longest x1 75.6 us: on_device(): attend_back(near, picks, spans, query_rows, kv_buf, kv_buf, context_gradi...]
    dynamic_slice x72 -> x0, local copies, waits for them, and re-layouts: 95.9 us -> none  [the longest x24 62.4 us: head_slices(): lax.dynamic_slice_in_dim(value_buf, column, head_dim, 1)]
    reshape x61 -> x12, local copies, waits for them, and re-layouts: 97.3 us -> 9.32 us  [the longest x9 8.95 us: on_device(): value.reshape(devices, -1)]
  transfers between devices with their start and end apart: 36 -> 18, of which waited for: 15 -> 7; matrix products, arithmetic and copies ran while one was open for 64% -> 20% of each run, Pallas kernels for 0% -> 14%
where the time goes in v1:
time: 884 us; the launch traced here: 876 us
  waiting for transfers between devices  248 us (28%)
  starting transfers between devices  159 us (18%)
  Pallas kernels  124 us (14%)
  blocking collectives  116 us (13%)
  matrix products  92.4 us (10%)
  local copies, waits for them, and re-layouts  88.4 us (10%)
  other arithmetic  33.7 us (4%)
  between operations  15.4 us (2%)
    ppermute x12, waiting for transfers between devices, passed_along(): lax.ppermute(value, axis, [(source, source + steps) for source in range(f...  189 us
    ppermute x12, starting transfers between devices, passed_along(): lax.ppermute(value, axis, [(source, source + steps) for source in range(f...  159 us
    unnamed x1, blocking collectives  81.9 us
    pallas_call x1, Pallas kernels, on_device(): attend_back(near, picks, spans, query_rows, kv_buf, kv_buf, context_gradi...  75.6 us
    unnamed x124, local copies, waits for them, and re-layouts  50 us
    pallas_call x1, Pallas kernels, on_device(): context_rows = attend(near, picks, spans, query_rows, kv_buf, kv_buf)  48.1 us
    dot_general x4, matrix products, plain_dot(): return jnp.dot(left, right, preferred_element_type=F32)  46.6 us
    unnamed x7, waiting for transfers between devices  41.3 us
  transfers between devices with their start and end apart: 18, of which 7 were waited for; matrix products, arithmetic and copies ran while one was open for 20% of the time, Pallas kernels for 14%

profile of v1, /device:TPU:6, one launch (start us, length us, event | category | flops | bytes accessed | tf_op | source)
XLA Modules:
  0.0 876.0 jit_solution(16629720580693141582)
XLA Ops:
  18.4 33.7 %all-gather = bf16[32,1,288]{2,1,0:T(2,128)(2,1)S(1)} all-gather(bf16[1,1,288]{2,1,0:T(2,128)(2,1)S(1)} %bitcast.84), channel_id=1, replica_groups=mesh['ctx'=32] {'ctx'}, dimensions={0}, use_global_device_ids=true | all-gather | bytes 19008 | tf_op jit(solution)/shard_map/all_gather | solution.py:362
  54.3 17.4 %all-gather.5.cloned.1.call-done = bf16[768,2304]{1,0:T(8,128)(2,1)} async-done(((bf16[24,2304]{1,0:T(8,128)(2,1)}), bf16[768,2304]{1,0:T(8,128)(2,1)}) %all-gather.5.cloned.1.call-update) | async-done | bytes 3538960 | tf_op jit(solution)/shard_map/all_gather | solution.py:362
  71.6 5.2 fusion.7
  78.6 3.6 collective-permute-start.1
  86.5 4.7 collective-permute-start
  111.5 73.5 %collective-permute-done = bf16[448,1536]{1,0:T(8,128)(2,1)} collective-permute-done((bf16[448,1536]{1,0:T(8,128)(2,1)}, bf16[448,1536]{1,0:T(8,128)(2,1)}, u32[]{:S(2)}, u32[]{:S(2)}) %collective-permute-start) | collective-permute-done | bytes 1376288 | tf_op jit(solution)/shard_map/ppermute | solution.py:28
  185.0 89.9 %collective-permute-start.5 = (bf16[448,1536]{1,0:T(8,128)(2,1)}, bf16[448,1536]{1,0:T(8,128)(2,1)S(1)}, u32[]{:S(2)}, u32[]{:S(2)}) collective-permute-start(bf16[448,1536]{1,0:T(8,128)(2,1)} %get-tuple-element.136), channel_id=1, source_target_pairs={{3,0},{4,1},{5,2},{6,3},{7,4},{8,5},{9,6},{10,7},{11,8},{12,9},{13... | collective-permute-start | bytes 4128776 | tf_op jit(solution)/shard_map/ppermute | solution.py:28
  280.7 3.4 constant_dynamic-update-slice_fusion.4
  285.8 3.2 constant_dynamic-update-slice_fusion.2
  289.0 3.3 constant_dynamic-update-slice_fusion.1
  292.3 3.3 collective-permute-done.5
  296.9 48.1 %attend_forward.1 = bf16[768,768]{1,0:T(8,128)(2,1)S(1)} custom-call(s32[96]{0:T(128)S(1)} %reshape.480.near_ref, s32[432]{0:T(512)S(1)} %reshape.481.rand_ref, s32[48]{0:T(128)S(1)} %reshape.482.glob_ref, bf16[768,768]{1,0:T(8,128)(2,1)S(1)} %slice.204.q_ref, bf16[4736,1536]{1,0:T(8,128)(2,1)} %constant_dynamic-update-slice_fusion.k_ref.v_ref, ...), custom_call_target="tpu_custom_call" | custom-call | flops 2415919104 | bytes 14548992 | tf_op jit(solution)/shard_map/attend_forward/pallas_call | solution.py:391
  350.2 29.3 %multiply_convert_fusion = (bf16[768,3072]{1,0:T(8,128)(2,1)}, f32[768,3072]{1,0:T(8,128)}, f32[768,3072]{1,0:T(8,128)}) fusion(f32[3072]{0:T(1024)S(1)} %copy-done.46, bf16[768,3840]{1,0:T(8,128)(2,1)S(1)} %copy-done.49, f32[768,768]{0,1:T(8,128)S(1)} %get-tuple-element.169, f32[768]{0:T(1024)S(1)} %copy-done.47, f32[768]{0:T(1024)S(1)} %copy-done.37, ...), kind=kOutput, calls=%fused_computation.4 | convolution fusion | flops 3782541312 | bytes 30699520 | tf_op jit(solution)/shard_map/dot_general | solution.py:43
  379.5 9.0 %fusion.44 = (f32[768]{0:T(1024)S(1)}, f32[768,768]{0,1:T(8,128)S(1)}) fusion(f32[768]{0:T(1024)} %reshape.498, bf16[768,3072]{1,0:T(8,128)(2,1)} %get-tuple-element.128, bf16[3072,768]{1,0:T(8,128)(2,1)} %all-gather.9.cloned.1.call-done, f32[768]{0:T(1024)} %reshape.496, f32[768]{0:T(1024)} %reshape.495, f32[768]{0:T(1024)} %copy-done.42, ...), kind=kOutput, calls=%fused_computation.151 | convolution fusion | flops 3628006656 | bytes 14174208 | tf_op jit(solution)/shard_map/dot_general | solution.py:43
  395.8 5.6 convolution_convert_fusion.1
  401.6 12.6 %convert_reduce_fusion = (f32[3072]{0:T(1024)}, bf16[768,3072]{1,0:T(8,128)(2,1)S(1)}) fusion(f32[768,3072]{1,0:T(8,128)} %get-tuple-element.129, f32[768,3072]{1,0:T(8,128)} %get-tuple-element.170, f32[3072]{0:T(1024)} %reshape.497, bf16[768,768]{0,1:T(8,128)(2,1)} %copy-done.11, bf16[3072,768]{1,0:T(8,128)(2,1)} %all-gather.9.cloned.1.call-done), kind=kOutput, calls=%fused_computation.2 | convolution fusion | flops 3663983616 | bytes 29515776 | tf_op jit(solution)/shard_map/dot_general | solution.py:51
  414.3 7.7 multiply_reduce_fusion
  426.9 75.6 %attend_backward.1 = (bf16[768,768]{1,0:T(8,128)(2,1)S(1)}, bf16[4736,768]{1,0:T(8,128)(2,1)}, bf16[4736,768]{1,0:T(8,128)(2,1)}) custom-call(s32[96]{0:T(128)S(1)} %reshape.480.near_ref, s32[432]{0:T(512)S(1)} %reshape.481.rand_ref, s32[48]{0:T(128)S(1)} %reshape.482.glob_ref, bf16[768,768]{1,0:T(8,128)(2,1)S(1)} %slice.204.q_ref, ...), custom_call_target="tpu_custom_call" | custom-call | flops 6039797760 | bytes 29097984 | tf_op jit(solution)/shard_map/attend_backward/pallas_call | solution.py:421
  502.5 6.6 constant_dynamic-update-slice_fusion.8
  509.1 6.0 convolution_convert_fusion.2
  515.2 6.6 constant_dynamic-update-slice_fusion.7
  525.9 4.1 fusion.39
  530.0 20.0 %collective-permute-start.10 = (bf16[768,1536]{1,0:T(8,128)(2,1)S(1)}, bf16[768,1536]{1,0:T(8,128)(2,1)S(1)}, u32[]{:S(2)}, u32[]{:S(2)}) collective-permute-start(bf16[768,1536]{1,0:T(8,128)(2,1)S(1)} %get-tuple-element.133), channel_id=1, source_target_pairs={{0,2},{1,3},{2,4},{3,5},{4,6},{5,7},{6,8},{7,9},{8,10},{9,11},{10,... | collective-permute-start | bytes 7077896 | tf_op jit(solution)/shard_map/ppermute | solution.py:28
  556.3 9.5 %collective-permute-done.11 = bf16[448,1536]{1,0:T(8,128)(2,1)S(1)} collective-permute-done((bf16[448,1536]{1,0:T(8,128)(2,1)S(1)}, bf16[448,1536]{1,0:T(8,128)(2,1)S(1)}, u32[]{:S(2)}, u32[]{:S(2)}) %collective-permute-start.11) | collective-permute-done | bytes 1376288 | tf_op jit(solution)/shard_map/ppermute | solution.py:28
  565.7 25.8 %collective-permute-start.6 = (bf16[448,1536]{1,0:T(8,128)(2,1)S(1)}, bf16[448,1536]{1,0:T(8,128)(2,1)S(1)}, u32[]{:S(2)}, u32[]{:S(2)}) collective-permute-start(bf16[448,1536]{1,0:T(8,128)(2,1)S(1)} %get-tuple-element.130), channel_id=1, source_target_pairs={{3,0},{4,1},{5,2},{6,3},{7,4},{8,5},{9,6},{10,7},{11,8},{12,9},{13... | collective-permute-start | bytes 4128776 | tf_op jit(solution)/shard_map/ppermute | solution.py:28
  592.7 56.7 %collective-permute-done.6 = bf16[448,1536]{1,0:T(8,128)(2,1)S(1)} collective-permute-done((bf16[448,1536]{1,0:T(8,128)(2,1)S(1)}, bf16[448,1536]{1,0:T(8,128)(2,1)S(1)}, u32[]{:S(2)}, u32[]{:S(2)}) %collective-permute-start.6) | collective-permute-done | bytes 1376288 | tf_op jit(solution)/shard_map/ppermute | solution.py:28
  649.4 46.1 %collective-permute-done.9 = bf16[768,1536]{1,0:T(8,128)(2,1)S(1)} collective-permute-done((bf16[768,1536]{1,0:T(8,128)(2,1)S(1)}, bf16[768,1536]{1,0:T(8,128)(2,1)S(1)}, u32[]{:S(2)}, u32[]{:S(2)}) %collective-permute-start.9) | collective-permute-done | bytes 2359328 | tf_op jit(solution)/shard_map/ppermute | solution.py:28
  700.2 3.3 fusion.6
  705.9 6.6 copy.103
  726.1 7.1 add_add_fusion.4
  736.6 81.9 %all-reduce.2 = f32[32,288]{1,0:T(8,128)S(1)} all-reduce(f32[32,288]{1,0:T(8,128)S(1)} %concatenate.73), channel_id=3, replica_groups=mesh['ctx'=32] {'ctx'}, use_global_device_ids=true, to_apply=%region_21.22.clone | all-reduce | flops 9216 | bytes 73728
  823.0 41.2 %reduce-scatter.10.cloned.1.call-done = bf16[24,3072]{1,0:T(8,128)(2,1)} async-done(((bf16[768,3072]{1,0:T(8,128)(2,1)}), bf16[24,3072]{1,0:T(8,128)(2,1)}) %reduce-scatter.10.cloned.1.call-update) | async-done | bytes 147472
  (234 shorter events, 109.6 us)
Async XLA Ops:
  7.2 64.5 %all-gather.5.cloned.1.call-start = ((), (), s32[]{:S(2)}) async-start(), calls=%async_computation.3 | async-start | bytes 3649536 | tf_op jit(solution)/shard_map/all_gather | solution.py:362
  10.6 334.5 %all-gather.7.cloned.1.call-start = ((), (), s32[]{:S(2)}) async-start(), calls=%async_computation.4 | async-start | bytes 6082560 | tf_op jit(solution)/shard_map/all_gather | solution.py:362
  13.2 366.3 %all-gather.9.cloned.1.call-start = ((), (), s32[]{:S(2)}) async-start(), calls=%async_computation.5 | async-start | bytes 4866048 | tf_op jit(solution)/shard_map/all_gather | solution.py:362
  14.9 804.7 %reduce-scatter.8.cloned.1.call-start = ((), (), s32[]{:S(2)}) async-start(), calls=%async_computation.7 | async-start | bytes 4866048 | tf_op jit(solution)/shard_map/reduce_scatter | solution.py:405
  78.6 198.8 %collective-permute-start.1 = (bf16[768,1536]{1,0:T(8,128)(2,1)}, bf16[768,1536]{1,0:T(8,128)(2,1)}, u32[]{:S(2)}, u32[]{:S(2)}) collective-permute-start(bf16[768,1536]{1,0:T(8,128)(2,1)} %slice.206), channel_id=1, source_target_pairs={{0,2},{1,3},{2,4},{3,5},{4,6},{5,7},{6,8},{7,9},{8,10},{9,11},{10,... | collective-permute-start | bytes 7077896 | tf_op jit(solution)/shard_map/ppermute | solution.py:28
  82.8 197.9 %collective-permute-start.2 = (bf16[768,1536]{1,0:T(8,128)(2,1)}, bf16[768,1536]{1,0:T(8,128)(2,1)}, u32[]{:S(2)}, u32[]{:S(2)}) collective-permute-start(bf16[768,1536]{1,0:T(8,128)(2,1)} %slice.206), channel_id=1, source_target_pairs={{0,1},{1,2},{2,3},{3,4},{4,5},{5,6},{6,7},{7,8},{8,9},{9,10},{10,1... | collective-permute-start | bytes 7077896 | tf_op jit(solution)/shard_map/ppermute | solution.py:28
  86.5 22.4 %copy-start.12 = (bf16[768,768]{1,0:T(8,128)(2,1)S(1)}, bf16[768,768]{1,0:T(8,128)(2,1)}, u32[]{:S(2)}) copy-start(bf16[768,768]{1,0:T(8,128)(2,1)} %param.20) | copy-start | bytes 3538948
  86.5 98.5 %collective-permute-start = (bf16[448,1536]{1,0:T(8,128)(2,1)}, bf16[448,1536]{1,0:T(8,128)(2,1)}, u32[]{:S(2)}, u32[]{:S(2)}) collective-permute-start(bf16[448,1536]{1,0:T(8,128)(2,1)} %get-tuple-element.137), channel_id=1, source_target_pairs={{0,3},{1,4},{2,5},{3,6},{4,7},{5,8},{6,9},{7,10},{8,11},{9,12},{10... | collective-permute-start | bytes 4128776 | tf_op jit(solution)/shard_map/ppermute | solution.py:28
  92.1 193.7 %collective-permute-start.3 = (bf16[768,1536]{1,0:T(8,128)(2,1)}, bf16[768,1536]{1,0:T(8,128)(2,1)}, u32[]{:S(2)}, u32[]{:S(2)}) collective-permute-start(bf16[768,1536]{1,0:T(8,128)(2,1)} %slice.206), channel_id=1, source_target_pairs={{1,0},{2,1},{3,2},{4,3},{5,4},{6,5},{7,6},{8,7},{9,8},{10,9},{11,1... | collective-permute-start | bytes 7077896 | tf_op jit(solution)/shard_map/ppermute | solution.py:28
  94.0 195.0 %collective-permute-start.4 = (bf16[768,1536]{1,0:T(8,128)(2,1)}, bf16[768,1536]{1,0:T(8,128)(2,1)}, u32[]{:S(2)}, u32[]{:S(2)}) collective-permute-start(bf16[768,1536]{1,0:T(8,128)(2,1)} %slice.206), channel_id=1, source_target_pairs={{2,0},{3,1},{4,2},{5,3},{6,4},{7,5},{8,6},{9,7},{10,8},{11,9},{12,... | collective-permute-start | bytes 7077896 | tf_op jit(solution)/shard_map/ppermute | solution.py:28
  185.0 110.7 %collective-permute-start.5 = (bf16[448,1536]{1,0:T(8,128)(2,1)}, bf16[448,1536]{1,0:T(8,128)(2,1)S(1)}, u32[]{:S(2)}, u32[]{:S(2)}) collective-permute-start(bf16[448,1536]{1,0:T(8,128)(2,1)} %get-tuple-element.136), channel_id=1, source_target_pairs={{3,0},{4,1},{5,2},{6,3},{7,4},{8,5},{9,6},{10,7},{11,8},{12,9},{13... | collective-permute-start | bytes 4128776 | tf_op jit(solution)/shard_map/ppermute | solution.py:28
  401.5 419.8 %reduce-scatter.6.cloned.1.call-start = ((), (), s32[]{:S(2)}) async-start(), calls=%async_computation.6 | async-start | bytes 4866048 | tf_op jit(solution)/shard_map/reduce_scatter | solution.py:405
  401.5 12.7 %copy-start.1 = (f32[768,768]{0,1:T(8,128)S(1)}, f32[768,768]{0,1:T(8,128)}, u32[]{:S(2)}) copy-start(f32[768,768]{0,1:T(8,128)} %copy-done) | copy-start | bytes 7077892
  401.5 12.7 %copy-start.7 = (f32[768,768]{0,1:T(8,128)S(1)}, f32[768,768]{0,1:T(8,128)}, u32[]{:S(2)}) copy-start(f32[768,768]{0,1:T(8,128)} %copy-done.6) | copy-start | bytes 7077892
  401.5 12.7 %copy-start.26 = (f32[768]{0:T(1024)S(1)}, f32[768]{0:T(1024)}, u32[]{:S(2)}) copy-start(f32[768]{0:T(1024)} %copy-done.25) | copy-start | bytes 9220
  401.6 12.7 %copy-start.28 = (f32[768]{0:T(1024)S(1)}, f32[768]{0:T(1024)}, u32[]{:S(2)}) copy-start(f32[768]{0:T(1024)} %copy-done.27) | copy-start | bytes 9220
  401.6 12.7 %copy-start.30 = (f32[768]{0:T(1024)S(1)}, f32[768]{0:T(1024)}, u32[]{:S(2)}) copy-start(f32[768]{0:T(1024)} %copy-done.29) | copy-start | bytes 9220
  401.6 12.7 %copy-start.32 = (f32[768]{0:T(1024)S(1)}, f32[768]{0:T(1024)}, u32[]{:S(2)}) copy-start(f32[768]{0:T(1024)} %copy-done.31) | copy-start | bytes 9220
  401.6 12.7 %copy-start.38 = (f32[768]{0:T(1024)S(1)}, f32[768]{0:T(1024)}, u32[]{:S(2)}) copy-start(f32[768]{0:T(1024)} %reshape.495) | copy-start | bytes 9220
  401.6 12.7 %copy-start.43 = (f32[768]{0:T(1024)S(1)}, f32[768]{0:T(1024)}, u32[]{:S(2)}) copy-start(f32[768]{0:T(1024)} %copy-done.42) | copy-start | bytes 9220
  401.6 12.7 %copy-start.45 = (f32[768]{0:T(1024)S(1)}, f32[768]{0:T(1024)}, u32[]{:S(2)}) copy-start(f32[768]{0:T(1024)} %copy-done.44) | copy-start | bytes 9220
  515.1 349.0 %reduce-scatter.10.cloned.1.call-start = ((), (), s32[]{:S(2)}) async-start(), calls=%async_computation.8 | async-start | bytes 4866048
  523.8 67.8 %copy-start.10 = (bf16[768,768]{0,1:T(8,128)(2,1)S(1)}, bf16[768,768]{0,1:T(8,128)(2,1)}, u32[]{:S(2)}) copy-start(bf16[768,768]{0,1:T(8,128)(2,1)} %copy-done.9) | copy-start | bytes 3538948
  523.8 41.9 %collective-permute-start.11 = (bf16[448,1536]{1,0:T(8,128)(2,1)S(1)}, bf16[448,1536]{1,0:T(8,128)(2,1)S(1)}, u32[]{:S(2)}, u32[]{:S(2)}) collective-permute-start(bf16[448,1536]{1,0:T(8,128)(2,1)S(1)} %get-tuple-element.131), channel_id=1, source_target_pairs={{0,3},{1,4},{2,5},{3,6},{4,7},{5,8},{6,9},{7,10},{8,11},{9,12},{10... | collective-permute-start | bytes 4128776 | tf_op jit(solution)/shard_map/ppermute | solution.py:28
  530.0 119.4 %collective-permute-start.10 = (bf16[768,1536]{1,0:T(8,128)(2,1)S(1)}, bf16[768,1536]{1,0:T(8,128)(2,1)S(1)}, u32[]{:S(2)}, u32[]{:S(2)}) collective-permute-start(bf16[768,1536]{1,0:T(8,128)(2,1)S(1)} %get-tuple-element.133), channel_id=1, source_target_pairs={{0,2},{1,3},{2,4},{3,5},{4,6},{5,7},{6,8},{7,9},{8,10},{9,11},{10,... | collective-permute-start | bytes 7077896 | tf_op jit(solution)/shard_map/ppermute | solution.py:28
  550.0 99.4 %collective-permute-start.7 = (bf16[768,1536]{1,0:T(8,128)(2,1)S(1)}, bf16[768,1536]{1,0:T(8,128)(2,1)S(1)}, u32[]{:S(2)}, u32[]{:S(2)}) collective-permute-start(bf16[768,1536]{1,0:T(8,128)(2,1)S(1)} %get-tuple-element.132), channel_id=1, source_target_pairs={{2,0},{3,1},{4,2},{5,3},{6,4},{7,5},{8,6},{9,7},{10,8},{11,9},{12,... | collective-permute-start | bytes 7077896 | tf_op jit(solution)/shard_map/ppermute | solution.py:28
  551.9 97.4 %collective-permute-start.8 = (bf16[768,1536]{1,0:T(8,128)(2,1)S(1)}, bf16[768,1536]{1,0:T(8,128)(2,1)S(1)}, u32[]{:S(2)}, u32[]{:S(2)}) collective-permute-start(bf16[768,1536]{1,0:T(8,128)(2,1)S(1)} %get-tuple-element.135), channel_id=1, source_target_pairs={{1,0},{2,1},{3,2},{4,3},{5,4},{6,5},{7,6},{8,7},{9,8},{10,9},{11,1... | collective-permute-start | bytes 7077896 | tf_op jit(solution)/shard_map/ppermute | solution.py:28
  553.9 141.7 %collective-permute-start.9 = (bf16[768,1536]{1,0:T(8,128)(2,1)S(1)}, bf16[768,1536]{1,0:T(8,128)(2,1)S(1)}, u32[]{:S(2)}, u32[]{:S(2)}) collective-permute-start(bf16[768,1536]{1,0:T(8,128)(2,1)S(1)} %get-tuple-element.134), channel_id=1, source_target_pairs={{0,1},{1,2},{2,3},{3,4},{4,5},{5,6},{6,7},{7,8},{8,9},{9,10},{10,1... | collective-permute-start | bytes 7077896 | tf_op jit(solution)/shard_map/ppermute | solution.py:28
  565.7 83.6 %collective-permute-start.6 = (bf16[448,1536]{1,0:T(8,128)(2,1)S(1)}, bf16[448,1536]{1,0:T(8,128)(2,1)S(1)}, u32[]{:S(2)}, u32[]{:S(2)}) collective-permute-start(bf16[448,1536]{1,0:T(8,128)(2,1)S(1)} %get-tuple-element.130), channel_id=1, source_target_pairs={{3,0},{4,1},{5,2},{6,3},{7,4},{8,5},{9,6},{10,7},{11,8},{12,9},{13... | collective-permute-start | bytes 4128776 | tf_op jit(solution)/shard_map/ppermute | solution.py:28
  592.7 107.5 %copy-start.13 = (bf16[768,768]{1,0:T(8,128)(2,1)S(1)}, bf16[768,768]{1,0:T(8,128)(2,1)}, u32[]{:S(2)}) copy-start(bf16[768,768]{1,0:T(8,128)(2,1)} %param.19) | copy-start | bytes 3538948
  712.5 13.6 %copy-start.5 = (f32[768,768]{0,1:T(8,128)S(1)}, f32[768,768]{0,1:T(8,128)}, u32[]{:S(2)}) copy-start(f32[768,768]{0,1:T(8,128)} %copy-done.4) | copy-start | bytes 7077892
  712.5 13.6 %copy-start.41 = (f32[768]{0:T(1024)S(1)}, f32[768]{0:T(1024)}, u32[]{:S(2)}) copy-start(f32[768]{0:T(1024)} %copy-done.40) | copy-start | bytes 9220
  (39 other events, 148.5 us)
Sparse Core Ops, SparseCore 0:
  11.5 60.1 all-gather.4
  75.1 154.5 all-gather.6
  233.2 143.8 all-gather.8
  401.6 125.9 reduce-scatter.7
  532.9 218.7 reduce-scatter.5
  757.1 107.0 reduce-scatter.9

commit v2 on v1

--- a/solution.py
+++ b/solution.py
@@ -22,12 +22,6 @@
 F32 = jnp.float32
 
 
-def passed_along(value, axis, steps):
-    count = lax.axis_size(axis)
-    first, last = (max(0, -steps), min(count, count - steps))
-    return lax.ppermute(value, axis, [(source, source + steps) for source in range(first, last)])
-
-
 def layer_norm(hidden, scale_gain, shift_vec):
     row_mean = jnp.mean(hidden, axis=-1, keepdims=True)
     centred = hidden - row_mean
@@ -49,10 +43,6 @@
 
 def cols_dot(left, right):
     return lax.dot_general(left, right, (((1,), (1,)), ((), ())), preferred_element_type=F32)
-
-
-def edge_rows(distance, own_blocks):
-    return BLOCK * min(own_blocks, DOC_MAX - 1 - (distance - 1) * own_blocks)
 
 
 def doc_layout(doc_starts, block_ids):
@@ -63,6 +53,446 @@
     return (doc_ids, first_block)
 
 
+def link_orders(count):
+    bits = count.bit_length() - 1
+    assert count == 1 << bits and bits >= 4, count
+    high = list(range(bits - 1, 2, -1))
+    return [[1] + high + [2, 0], [1, 2] + high + [0], [1] + high[:-1] + [2] + high[-1:] + [0]]
+
+
+def bit_of(index, bit):
+    return (index // (1 << bit)) % 2
+
+
+def across(index, bit):
+    return index + (1 << bit) * (1 - 2 * bit_of(index, bit))
+
+
+def place_of(index, order):
+    return sum(bit_of(index, bit) * (1 << k) for k, bit in enumerate(order))
+
+
+def remote(source, target, send_sem, recv_sem, device):
+    return pltpu.make_async_remote_copy(
+        src_ref=source, dst_ref=target, send_sem=send_sem, recv_sem=recv_sem, device_id=(device,),
+        device_id_type=pl.DeviceIdType.MESH,
+    )
+
+
+def halo_sizes(own_rows):
+    far = REACH * BLOCK - 2 * own_rows
+    assert 0 < far <= own_rows, own_rows
+    return far, [0] + [far + own_rows * i for i in range(6)]
+
+
+def halo_links(me, count):
+    odd = me % 2
+    partner = me - 3 + 6 * odd
+    return odd, me >= 2, me < count - 2, (partner >= 0) & (partner < count), partner
+
+
+def greet(me, bits, count):
+    barrier = pltpu.get_barrier_semaphore()
+
+    def hello(device):
+        pl.semaphore_signal(barrier, inc=1, device_id=(device,), device_id_type=pl.DeviceIdType.MESH)
+
+    _, has_before, has_after, has_far, partner = halo_links(me, count)
+    for bit in range(bits):
+        hello(across(me, bit))
+
+    @pl.when(has_before)
+    def _():
+        hello(me - 2)
+
+    @pl.when(has_after)
+    def _():
+        hello(me + 2)
+
+    @pl.when(has_far)
+    def _():
+        hello(partner)
+
+    expected = bits + has_before.astype(jnp.int32) + has_after.astype(jnp.int32) + has_far.astype(jnp.int32)
+    pl.semaphore_wait(barrier, expected)
+
+
+def gather_kernel(
+    count, wq_ref, wk_ref, wv_ref, v_ref, x_ref, w_out, v_out, x_out, low_w, low_v, buf_a, buf_b, buf_c, buf_v, zeros, local_sem, out_sem, send_sem,
+    recv_sem, halo_send, halo_recv, fill_sem,
+):
+    me = lax.axis_index("ctx")
+    orders = link_orders(count)
+    bits = len(orders[0])
+    width = wq_ref.shape[1]
+    low_w[:, :width] = wq_ref[...].astype(BF)
+    for i in range(width // LANES):
+        start = width + 2 * i * LANES
+        low_w[:, start : start + LANES] = wk_ref[:, i * LANES : (i + 1) * LANES].astype(BF)
+        low_w[:, start + LANES : start + 2 * LANES] = wv_ref[:, i * LANES : (i + 1) * LANES].astype(BF)
+    low_v[...] = v_ref[...].astype(BF)
+    orders = orders + [orders[0]]
+    bufs = [buf_a, buf_b, buf_c, buf_v]
+    sources = [low_w.at[:, pl.ds(i * width, width)] for i in range(3)] + [low_v]
+    places = [place_of(me, order) for order in orders]
+    full = x_ref.shape[0]
+    part, piece = halo_sizes(full)
+    odd, has_before, has_after, has_far, partner = halo_links(me, count)
+    sibling = across(me, 0)
+
+    def rows(start, size):
+        return x_out.at[pl.ds(pl.multiple_of(start, BLOCK), size), :]
+
+    def halo(index, source, target, device):
+        return remote(source, target, halo_send.at[index], halo_recv.at[index], device)
+
+    zeros[...] = jnp.zeros_like(zeros)
+    keep_own = pltpu.make_async_copy(x_ref, rows(piece[3], full), local_sem.at[4])
+    keep_own.start()
+    greet(me, bits, count)
+    for i in range(4):
+        pltpu.make_async_copy(sources[i], bufs[i].at[places[i]], local_sem.at[i]).start()
+
+    after = halo(0, x_ref, rows(piece[1], full), me + 2)
+    before = halo(1, x_ref, rows(piece[5], full), me - 2)
+    far_rows = x_ref.at[pl.ds(pl.multiple_of(odd * (full - part), BLOCK), part), :]
+    far = halo(2, far_rows, rows((1 - odd) * piece[6], part), partner)
+    own = halo(3, x_ref, rows(piece[2] + odd * (piece[4] - piece[2]), full), sibling)
+    wide = halo(
+        4, rows(piece[5] + odd * (piece[1] - piece[5]), full), rows(piece[4] + odd * (piece[2] - piece[4]), full), sibling
+    )
+    edge_from = (piece[1] + full - part) * (1 - odd) + piece[5] * odd
+    edge = halo(5, rows(edge_from, part), rows(piece[6] * odd, part), sibling)
+    has_wide = jnp.where(odd == 1, has_before, has_after)
+    has_edge = jnp.where(odd == 1, has_after, has_before)
+
+    for i in range(4):
+        pltpu.make_async_copy(sources[i], bufs[i].at[places[i]], local_sem.at[i]).wait()
+    copies = [own]
+    for k in range(bits):
+        stage = []
+        for i in range(4):
+            held = bufs[i].at[pl.ds((places[i] // (1 << k)) * (1 << k), 1 << k)]
+            copy = remote(held, held, send_sem.at[i, k], recv_sem.at[i, k], across(me, orders[i][k]))
+            copy.start()
+            stage.append(copy)
+        for copy in stage:
+            copy.wait_recv()
+        copies += stage
+        if k == 0:
+            own.start()
+            pl.when(has_after)(after.start)
+            pl.when(has_before)(before.start)
+            pl.when(has_far)(far.start)
+
+    def put(j, carry):
+        for i in range(3):
+            pltpu.make_async_copy(
+                bufs[i].at[place_of(j, orders[i])], w_out.at[j, :, pl.ds(i * width, width)], out_sem.at[i]
+            ).start()
+        pltpu.make_async_copy(buf_v.at[place_of(j, orders[3])], v_out.at[j], out_sem.at[3]).start()
+        return carry
+
+    lax.fori_loop(0, count, put, 0)
+
+    @pl.when(has_before)
+    def _():
+        halo(0, x_ref, rows(piece[1], full), sibling).wait_recv()
+
+    @pl.when(has_after)
+    def _():
+        halo(1, x_ref, rows(piece[5], full), sibling).wait_recv()
+
+    @pl.when(has_wide)
+    def _():
+        wide.start()
+
+    @pl.when(has_edge)
+    def _():
+        edge.start()
+
+    def fill(missing, start, size):
+        @pl.when(missing)
+        def _():
+            copy = pltpu.make_async_copy(zeros.at[pl.ds(0, size), :], rows(start, size), fill_sem.at[0])
+            copy.start()
+            copy.wait()
+
+    fill(jnp.logical_not(has_before), piece[1], full)
+    fill(jnp.logical_not(has_after), piece[5], full)
+    gets_wide = jnp.where(odd == 1, has_after, has_before)
+    gets_edge = jnp.where(odd == 1, has_before, has_after)
+    wide_at = piece[2] + odd * (piece[4] - piece[2])
+    edge_at = piece[6] * (1 - odd)
+    far_at = piece[6] * odd
+    own_at = piece[4] + odd * (piece[2] - piece[4])
+    fill(jnp.logical_not(gets_wide), wide_at, full)
+    fill(jnp.logical_not(gets_edge), edge_at, part)
+    fill(jnp.logical_not(has_far), far_at, part)
+    halo(3, x_ref, rows(own_at, full), sibling).wait_recv()
+
+    @pl.when(has_far)
+    def _():
+        halo(2, far_rows, rows(far_at, part), sibling).wait_recv()
+
+    @pl.when(gets_wide)
+    def _():
+        halo(4, x_ref, rows(wide_at, full), sibling).wait_recv()
+
+    @pl.when(gets_edge)
+    def _():
+        halo(5, far_rows, rows(edge_at, part), sibling).wait_recv()
+
+    for copy in copies:
+        copy.wait_send()
+    for exists, copy in ((has_after, after), (has_before, before), (has_far, far), (has_wide, wide), (has_edge, edge)):
+        pl.when(exists)(copy.wait_send)
+    keep_own.wait()
+    for i in range(3):
+        pltpu.make_async_copy(bufs[i], w_out.at[:, :, pl.ds(i * width, width)], out_sem.at[i]).wait()
+    pltpu.make_async_copy(buf_v, v_out, out_sem.at[3]).wait()
+
+
+def gather_weights(query, key, value, vectors, own, count):
+    rows, columns = query.shape[0], 3 * query.shape[1]
+    bits = count.bit_length() - 1
+    vmem, any_space = pl.BlockSpec(memory_space=pltpu.VMEM), pl.BlockSpec(memory_space=pl.ANY)
+    return pl.pallas_call(
+        functools.partial(gather_kernel, count),
+        out_shape=(
+            jax.ShapeDtypeStruct((count, rows, columns), BF),
+            jax.ShapeDtypeStruct((count,) + vectors.shape, BF),
+            jax.ShapeDtypeStruct((own.shape[0] + 2 * REACH * BLOCK, own.shape[1]), BF),
+        ),
+        in_specs=[vmem] * 5,
+        out_specs=[any_space, any_space, any_space],
+        scratch_shapes=[pltpu.VMEM((rows, columns), BF), pltpu.VMEM(vectors.shape, BF)]
+        + [pltpu.VMEM((count, rows, columns // 3), BF)] * 3
+        + [
+            pltpu.VMEM((count,) + vectors.shape, BF),
+            pltpu.VMEM(own.shape, BF),
+            pltpu.SemaphoreType.DMA((5,)),
+            pltpu.SemaphoreType.DMA((4,)),
+            pltpu.SemaphoreType.DMA((4, bits)),
+            pltpu.SemaphoreType.DMA((4, bits)),
+            pltpu.SemaphoreType.DMA((6,)),
+            pltpu.SemaphoreType.DMA((6,)),
+            pltpu.SemaphoreType.DMA((1,)),
+        ],
+        compiler_params=pltpu.CompilerParams(
+            collective_id=0, has_side_effects=True, vmem_limit_bytes=60 * 1024 * 1024
+        ),
+        cost_estimate=pl.CostEstimate(flops=0, bytes_accessed=200_000_000, transcendentals=0),
+        name="gather_weights",
+    )(query, key, value, vectors, own)
+
+
+def reduce_kernel(
+    count, q_ref, kv_ref, v_ref, x_ref, wq_out, wk_out, wv_out, v_out, x_out, buf_a, buf_b, buf_c, got_a, got_b, got_c, sum_v, got_v,
+    left, mid, right, e_own, e_wide, e_edge, e_far, from_after, from_before, load_sem, send_sem, recv_sem, halo_send,
+    halo_recv,
+):
+    me = lax.axis_index("ctx")
+    orders = link_orders(count)
+    bits = len(orders[0])
+    bufs, gots = [buf_a, buf_b, buf_c], [got_a, got_b, got_c]
+    width = q_ref.shape[2]
+    full = left.shape[0]
+    part, piece = halo_sizes(full)
+    odd, has_before, has_after, has_far, partner = halo_links(me, count)
+    sibling = across(me, 0)
+
+    def rows(start, size):
+        return x_ref.at[pl.ds(pl.multiple_of(start, BLOCK), size), :]
+
+    def halo(index, source, target, device):
+        return remote(source, target, halo_send.at[index], halo_recv.at[index], device)
+
+    loads = [
+        pltpu.make_async_copy(rows(piece[1], full), left, load_sem.at[4]),
+        pltpu.make_async_copy(rows(piece[3], full), mid, load_sem.at[5]),
+        pltpu.make_async_copy(rows(piece[5], full), right, load_sem.at[6]),
+    ]
+    for copy in loads:
+        copy.start()
+
+    def load(j, carry):
+        pltpu.make_async_copy(q_ref.at[j], bufs[0].at[place_of(j, orders[0])], load_sem.at[0]).start()
+        for i in (1, 2):
+            pltpu.make_async_copy(
+                kv_ref.at[j, :, pl.ds((i - 1) * width, width)], bufs[i].at[place_of(j, orders[i])], load_sem.at[i]
+            ).start()
+        return carry
+
+    lax.fori_loop(0, count, load, 0)
+    first_sum = pltpu.make_async_copy(v_ref, sum_v.at[0], load_sem.at[3])
+    first_sum.start()
+    greet(me, bits, count)
+
+    swaps = [
+        halo(3, rows(piece[2] + odd * (piece[4] - piece[2]), full), e_wide, sibling),
+        halo(4, rows(piece[6] * (1 - odd), part), e_edge, sibling),
+        halo(5, rows(piece[4] + odd * (piece[2] - piece[4]), full), e_own, sibling),
+    ]
+    for copy in swaps:
+        copy.start()
+    far = halo(2, rows(piece[6] * odd, part), e_far, partner)
+
+    @pl.when(has_far)
+    def _():
+        far.start()
+
+    for copy in loads:
+        copy.wait()
+    swaps[0].wait_recv()
+    swaps[1].wait_recv()
+
+    def add_into(target, start, source, size):
+        def add(j, carry):
+            at = pl.ds(pl.multiple_of(start + j * BLOCK, BLOCK), BLOCK)
+            total = target[at, :].astype(F32) + source[pl.ds(pl.multiple_of(j * BLOCK, BLOCK), BLOCK), :].astype(F32)
+            target[at, :] = total.astype(target.dtype)
+            return carry
+
+        lax.fori_loop(0, size // BLOCK, add, 0)
+
+    @pl.when(odd == 0)
+    def _():
+        add_into(left, full - part, e_edge, part)
+        add_into(right, 0, e_wide, full)
+
+    @pl.when(odd == 1)
+    def _():
+        add_into(left, 0, e_wide, full)
+        add_into(right, 0, e_edge, part)
+
+    before = halo(0, left, from_after, me - 2)
+    after = halo(1, right, from_before, me + 2)
+
+    @pl.when(has_before)
+    def _():
+        before.start()
+
+    @pl.when(has_after)
+    def _():
+        after.start()
+
+    for i in range(3):
+        source = q_ref if i == 0 else kv_ref.at[:, :, pl.ds((i - 1) * width, width)]
+        pltpu.make_async_copy(source, bufs[i], load_sem.at[i]).wait()
+    first_sum.wait()
+    places = [place_of(me, order) for order in orders]
+    copies = []
+    for k in range(bits):
+        bit = bits - 1 - k
+        half = 1 << bit
+        offset = count - 2 * half
+        stage = []
+        for i in range(3):
+            keep = (places[i] // half) * half
+            give = keep + half * (1 - 2 * bit_of(places[i], bit))
+            copy = remote(
+                bufs[i].at[pl.ds(give, half)], gots[i].at[pl.ds(offset, half)], send_sem.at[i, k], recv_sem.at[i, k],
+                across(me, orders[i][bit]),
+            )
+            copy.start()
+            stage.append(copy)
+        copy = remote(sum_v.at[k], got_v.at[k], send_sem.at[3, k], recv_sem.at[3, k], across(me, orders[0][bit]))
+        copy.start()
+        stage.append(copy)
+        for i in range(3):
+            stage[i].wait_recv()
+            keep = (places[i] // half) * half
+            if k == bits - 1:
+                total = bufs[i][keep].astype(F32) + gots[i][offset].astype(F32)
+                if i == 0:
+                    wq_out[...] = total
+                else:
+                    for j in range(width // LANES):
+                        place = ((i - 1) * width // LANES + j) // 2 * LANES
+                        target = wv_out if ((i - 1) * width // LANES + j) % 2 else wk_out
+                        target[:, place : place + LANES] = total[:, j * LANES : (j + 1) * LANES]
+            else:
+
+                def add(j, carry, i=i, keep=keep, offset=offset):
+                    total = bufs[i][keep + j].astype(F32) + gots[i][offset + j].astype(F32)
+                    bufs[i][keep + j] = total.astype(BF)
+                    return carry
+
+                lax.fori_loop(0, half, add, 0)
+        stage[3].wait_recv()
+        if k == bits - 1:
+            v_out[...] = sum_v[k] + got_v[k]
+        else:
+            sum_v[k + 1] = sum_v[k] + got_v[k]
+        copies += stage
+
+    swaps[2].wait_recv()
+
+    def start_sum(j, carry):
+        at = pl.ds(pl.multiple_of(j * BLOCK, BLOCK), BLOCK)
+        x_out[at, :] = mid[at, :].astype(F32) + e_own[at, :].astype(F32)
+        return carry
+
+    lax.fori_loop(0, full // BLOCK, start_sum, 0)
+
+    @pl.when(has_far)
+    def _():
+        far.wait_recv()
+        add_into(x_out, odd * (full - part), e_far, part)
+
+    @pl.when(has_after)
+    def _():
+        before.wait_recv()
+        add_into(x_out, 0, from_after, full)
+
+    @pl.when(has_before)
+    def _():
+        after.wait_recv()
+        add_into(x_out, 0, from_before, full)
+
+    for copy in copies + swaps:
+        copy.wait_send()
+    for exists, copy in ((has_after, after), (has_before, before), (has_far, far)):
+        pl.when(exists)(copy.wait_send)
+
+
+def reduce_grads(query_grads, kv_grads, vectors, halo_grads, own_rows, count):
+    _, rows, columns = query_grads.shape
+    bits = count.bit_length() - 1
+    vmem, any_space = pl.BlockSpec(memory_space=pltpu.VMEM), pl.BlockSpec(memory_space=pl.ANY)
+    slabs = pltpu.VMEM((count, rows, columns), BF)
+    stages = pltpu.VMEM((bits,) + vectors.shape, F32)
+    part, _ = halo_sizes(own_rows)
+    whole, piece = pltpu.VMEM((own_rows, columns), BF), pltpu.VMEM((part, columns), BF)
+    return pl.pallas_call(
+        functools.partial(reduce_kernel, count),
+        out_shape=(
+            jax.ShapeDtypeStruct((rows, columns), F32),
+            jax.ShapeDtypeStruct((rows, columns), F32),
+            jax.ShapeDtypeStruct((rows, columns), F32),
+            jax.ShapeDtypeStruct(vectors.shape, F32),
+            jax.ShapeDtypeStruct((own_rows, columns), F32),
+        ),
+        in_specs=[any_space, any_space, vmem, any_space],
+        out_specs=[vmem] * 5,
+        scratch_shapes=[slabs] * 6
+        + [stages, stages, whole, whole, whole, whole, whole, piece, piece, whole, whole]
+        + [
+            pltpu.SemaphoreType.DMA((7,)),
+            pltpu.SemaphoreType.DMA((4, bits)),
+            pltpu.SemaphoreType.DMA((4, bits)),
+            pltpu.SemaphoreType.DMA((6,)),
+            pltpu.SemaphoreType.DMA((6,)),
+        ],
+        compiler_params=pltpu.CompilerParams(
+            collective_id=1, has_side_effects=True, vmem_limit_bytes=60 * 1024 * 1024
+        ),
+        cost_estimate=pl.CostEstimate(flops=0, bytes_accessed=200_000_000, transcendentals=0),
+        name="reduce_grads",
+    )(query_grads, kv_grads, vectors, halo_grads)
+
+
 def low_half():
     return lax.broadcasted_iota(jnp.int32, (BLOCK, LANES), 1) < LANES // 2
 
@@ -77,8 +507,11 @@
     return jnp.where(low_half(), rows[:BLOCK], rows[BLOCK:])
 
 
-def block_at(ref, position):
-    return ref[pl.ds(pl.multiple_of(position * BLOCK, BLOCK), BLOCK), :]
+KEY, VALUE = slice(0, LANES), slice(LANES, 2 * LANES)
+
+
+def block_at(ref, position, side):
+    return ref[pl.ds(pl.multiple_of(position * BLOCK, BLOCK), BLOCK), side]
 
 
 def slots_of(near_ref, rand_ref, block, pair, heads):
@@ -88,10 +521,10 @@
     return shared, chosen
 
 
-def slot_rows(ref, shared, chosen):
+def slot_rows(ref, side, shared, chosen):
     half = low_half()
-    parts = [block_at(ref, i) for i in shared]
-    parts += [jnp.where(half, block_at(ref, a), block_at(ref, b)) for a, b in chosen]
+    parts = [block_at(ref, i, side) for i in shared]
+    parts += [jnp.where(half, block_at(ref, a, side), block_at(ref, b, side)) for a, b in chosen]
     return jnp.concatenate(parts, axis=0)
 
 
@@ -101,7 +534,7 @@
     return after, lead
 
 
-def forward_kernel(heads, own_blocks, near_ref, rand_ref, glob_ref, q_ref, k_ref, v_ref, o_ref, s_ref):
+def forward_kernel(heads, own_blocks, near_ref, rand_ref, glob_ref, q_ref, kv_ref, o_ref, s_ref):
     pair = pl.program_id(0)
     slot_id = lax.broadcasted_iota(jnp.int32, (1, WIDE), 1) // BLOCK
 
@@ -109,12 +542,12 @@
         rows = pl.ds(pl.multiple_of(block * BLOCK, BLOCK), BLOCK)
         shared, chosen = slots_of(near_ref, rand_ref, block, pair, heads)
         queries = split_pair(q_ref[rows, :] * 0.125)
-        scores = cols_dot(queries, slot_rows(k_ref, shared, chosen))
+        scores = cols_dot(queries, slot_rows(kv_ref, KEY, shared, chosen))
         after, lead = slot_bias(near_ref, block)
         scores = scores + jnp.where(slot_id == 2, after, jnp.where(slot_id == 4, lead, 0.0))
         weights = jnp.exp(scores - jnp.max(scores, axis=1, keepdims=True))
         probs = weights * (1.0 / jnp.sum(weights, axis=1, keepdims=True))
-        mixed = plain_dot(probs.astype(BF), slot_rows(v_ref, shared, chosen))
+        mixed = plain_dot(probs.astype(BF), slot_rows(kv_ref, VALUE, shared, chosen))
         o_ref[rows, :] = join_pair(mixed).astype(BF)
         return carry
 
@@ -131,7 +564,7 @@
 
             def score(step, top):
                 at = pl.ds(pl.multiple_of((first + step * SLOTS) * BLOCK, BLOCK), WIDE)
-                scores = cols_dot(queries, k_ref[at, :])
+                scores = cols_dot(queries, kv_ref[at, KEY])
                 scores = jnp.where(slot_id < length - step * SLOTS, scores, masked_score)
                 s_ref[step] = scores
                 return jnp.maximum(top, jnp.max(scores, axis=1, keepdims=True))
@@ -144,7 +577,7 @@
                 weights = jnp.exp(s_ref[step] - top)
                 return (
                     total + jnp.sum(weights, axis=1, keepdims=True),
-                    acc + plain_dot(weights.astype(BF), v_ref[at, :]),
+                    acc + plain_dot(weights.astype(BF), kv_ref[at, VALUE]),
                 )
 
             total, acc = lax.fori_loop(
@@ -158,8 +591,8 @@
 
 
 def backward_kernel(
-    heads, own_blocks, near_ref, rand_ref, glob_ref, q_ref, k_ref, v_ref, c_ref,
-    dq_ref, dk_ref, dv_ref, dk_acc, dv_acc, s_ref, p_ref,
+    heads, own_blocks, near_ref, rand_ref, glob_ref, q_ref, kv_ref, c_ref,
+    dq_ref, dkv_ref, sum_ref, dk_acc, dv_acc, s_ref, p_ref,
 ):
     pair = pl.program_id(0)
     dk_acc[...] = jnp.zeros_like(dk_acc)
@@ -183,7 +616,7 @@
         queries = split_pair(q_ref[rows, :] * 0.125)
         slope = c_ref[rows, :]
         slope = split_pair(jnp.where(glob_ref[block * 4] > 0, jnp.zeros_like(slope), slope))
-        keys = slot_rows(k_ref, shared, chosen)
+        keys = slot_rows(kv_ref, KEY, shared, chosen)
         scores = cols_dot(keys, queries)
         after, lead = slot_bias(near_ref, block)
         scores = jnp.concatenate(
@@ -198,7 +631,7 @@
         )
         weights = jnp.exp(scores - jnp.max(scores, axis=0, keepdims=True))
         probs = weights * (1.0 / jnp.sum(weights, axis=0, keepdims=True))
-        dprobs = cols_dot(slot_rows(v_ref, shared, chosen), slope)
+        dprobs = cols_dot(slot_rows(kv_ref, VALUE, shared, chosen), slope)
         inner = jnp.sum(probs * dprobs, axis=0, keepdims=True)
         dscores = (probs * (dprobs - inner)).astype(BF)
         dq_ref[rows, :] = (join_pair(rows_dot(dscores, keys)) * 0.125).astype(BF)
@@ -221,10 +654,10 @@
 
             def score(step, top):
                 at = pl.ds(pl.multiple_of((first + step * SLOTS) * BLOCK, BLOCK), WIDE)
-                scores = cols_dot(k_ref[at, :], queries)
+                scores = cols_dot(kv_ref[at, KEY], queries)
                 scores = jnp.where(slot_id < length - step * SLOTS, scores, masked_score)
                 s_ref[step] = scores
-                p_ref[step] = cols_dot(v_ref[at, :], slope)
+                p_ref[step] = cols_dot(kv_ref[at, VALUE], slope)
                 return jnp.maximum(top, jnp.max(scores, axis=0, keepdims=True))
 
             top = lax.fori_loop(0, chunks, score, jnp.full((1, LANES), masked_score, F32))
@@ -249,7 +682,7 @@
                 dscores = (probs * (p_ref[step] - inner)).astype(BF)
                 dk_acc[at, :] += plain_dot(dscores, queries)
                 dv_acc[at, :] += plain_dot(probs.astype(BF), slope)
-                return dq_sum + rows_dot(dscores, k_ref[at, :])
+                return dq_sum + rows_dot(dscores, kv_ref[at, KEY])
 
             dq_sum = lax.fori_loop(0, chunks, spread, jnp.zeros((LANES, LANES), F32))
             dq_ref[rows, :] = (join_pair(dq_sum) * 0.125).astype(BF)
@@ -257,16 +690,18 @@
         return carry
 
     lax.fori_loop(0, own_blocks, whole, 0)
-    dk_ref[...] = dk_acc[...].astype(BF)
-    dv_ref[...] = dv_acc[...].astype(BF)
+    dkv_ref[:, KEY] = dk_acc[...].astype(BF)
+    dv_low = dv_acc[...].astype(BF)
+    dkv_ref[:, VALUE] = dv_low
+    sum_ref[0:1, :] = jnp.sum(dq_ref[...].astype(F32), axis=0, keepdims=True)
+    sum_ref[1:2, :] = jnp.sum(dv_low.astype(F32), axis=0, keepdims=True)
 
 
 def attention_calls(row_count, model_width, heads, buf_rows):
     own_blocks = row_count // BLOCK
     pairs = heads // 2
     own = lambda: pl.BlockSpec((row_count, LANES), lambda p, *_: (0, p))
-    keys = lambda: pl.BlockSpec((buf_rows, LANES), lambda p, *_: (0, p))
-    values = lambda: pl.BlockSpec((buf_rows, LANES), lambda p, *_: (0, p + pairs))
+    both = lambda: pl.BlockSpec((buf_rows, 2 * LANES), lambda p, *_: (0, p))
     params = lambda: pltpu.CompilerParams(vmem_limit_bytes=48 * 1024 * 1024)
     forward = pl.pallas_call(
         functools.partial(forward_kernel, heads, own_blocks),
@@ -274,7 +709,7 @@
         grid_spec=pltpu.PrefetchScalarGridSpec(
             num_scalar_prefetch=3,
             grid=(pairs,),
-            in_specs=[own(), keys(), values()],
+            in_specs=[own(), both()],
             out_specs=own(),
             scratch_shapes=[pltpu.VMEM((CHUNKS, LANES, WIDE), F32)],
         ),
@@ -289,14 +724,14 @@
         functools.partial(backward_kernel, heads, own_blocks),
         out_shape=(
             jax.ShapeDtypeStruct((row_count, model_width), BF),
-            jax.ShapeDtypeStruct((buf_rows, model_width), BF),
-            jax.ShapeDtypeStruct((buf_rows, model_width), BF),
+            jax.ShapeDtypeStruct((buf_rows, 2 * model_width), BF),
+            jax.ShapeDtypeStruct((2, model_width), F32),
         ),
         grid_spec=pltpu.PrefetchScalarGridSpec(
             num_scalar_prefetch=3,
             grid=(pairs,),
-            in_specs=[own(), keys(), values(), own()],
-            out_specs=[own(), keys(), keys()],
+            in_specs=[own(), both(), own()],
+            out_specs=[own(), both(), pl.BlockSpec((2, LANES), lambda p, *_: (0, p))],
             scratch_shapes=[
                 pltpu.VMEM((buf_rows, LANES), F32),
                 pltpu.VMEM((buf_rows, LANES), F32),
@@ -314,6 +749,12 @@
     return forward, backward
 
 
+def interleaved(one, two):
+    return jnp.concatenate(
+        [side[..., i : i + LANES] for i in range(0, one.shape[-1], LANES) for side in (one, two)], axis=-1
+    )
+
+
 def on_device(
     layer_input, out_grad, doc_starts, rand_blocks, query_weight, query_bias, key_weight, value_weight,
     value_bias, output_weight, output_bias, first_gain, first_shift, inner_weight, inner_bias,
@@ -323,7 +764,6 @@
     head_count = rand_blocks.shape[1]
     devices = lax.axis_size("ctx")
     own_blocks = row_count // BLOCK
-    reach_shards = (REACH - 1 + own_blocks) // own_blocks
     buf_blocks = 2 * REACH + own_blocks
     own_first = lax.axis_index("ctx") * own_blocks
     buf_first = own_first - REACH
@@ -357,38 +797,37 @@
         [glob_own.astype(jnp.int32), local(own_start), doc_end - own_start, jnp.zeros_like(own_ids)], axis=1
     ).reshape(-1)
     attend, attend_back = attention_calls(row_count, model_width, head_count, buf_blocks * BLOCK)
+    m = model_width
+    unit = query_bias.shape[0]
+    weight_rows = query_weight.shape[0]
 
     def gathered(value):
         return lax.all_gather(value, "ctx", axis=0, tiled=True)
 
-    vectors = (
-        query_bias, value_bias, output_bias, first_gain, first_shift, outer_bias, second_gain, second_shift, inner_bias,
-    )
-    w_qkv = gathered(jnp.concatenate([query_weight, key_weight, value_weight], axis=1).astype(BF))
-    vector_all = gathered(jnp.concatenate(vectors).astype(BF)[None, :])
-    unit = query_bias.shape[0]
+    vectors = jnp.concatenate(
+        [
+            query_bias, value_bias, output_bias, first_gain, first_shift, outer_bias, second_gain, second_shift,
+            inner_bias,
+        ]
+    )
+    lane_pad = -vectors.shape[0] % LANES
+    first_all, vector_all, x_buf = gather_weights(
+        query_weight, key_weight, value_weight, jnp.pad(vectors, (0, lane_pad))[None, :], layer_input, devices
+    )
+    w_qkv = first_all.reshape(m, 3 * m)
+    vector_all = vector_all[:, 0].astype(F32)
     b_query, b_value, b_output, g_first, s_first, b_outer, g_second, s_second = [
-        vector_all[:, i * unit : (i + 1) * unit].reshape(-1).astype(F32) for i in range(8)
+        vector_all[:, i * unit : (i + 1) * unit].reshape(-1) for i in range(8)
     ]
-    b_inner = vector_all[:, 8 * unit :].reshape(-1).astype(F32)
+    b_inner = vector_all[:, 8 * unit : 8 * unit + inner_bias.shape[0]].reshape(-1)
     w_late = gathered(jnp.concatenate([output_weight, inner_weight], axis=1).astype(BF))
-    w_output, w_inner = w_late[:, :model_width], w_late[:, model_width:]
+    w_output, w_inner = w_late[:, :m], w_late[:, m:]
     w_outer = gathered(outer_weight.astype(BF))
-
-    b_qkv = jnp.concatenate([b_query, jnp.zeros_like(b_query), b_value])
-    qkv = (plain_dot(layer_input, w_qkv) + b_qkv).astype(BF)
-    query_rows, kv_own = qkv[:, :model_width], qkv[:, model_width:]
-    parts = []
-    for offset in range(-reach_shards, reach_shards + 1):
-        if offset == 0:
-            parts.append(kv_own)
-        else:
-            span_rows = edge_rows(abs(offset), own_blocks)
-            start_at = 0 if offset > 0 else row_count - span_rows
-            parts.append(passed_along(kv_own[start_at : start_at + span_rows], "ctx", -offset))
-    kv_buf = jnp.concatenate(parts, axis=0)
-
-    context_rows = attend(near, picks, spans, query_rows, kv_buf, kv_buf)
+    w_query, w_kv = w_qkv[:, :m], w_qkv[:, m:]
+
+    query_rows = (plain_dot(layer_input, w_query) + b_query).astype(BF)
+    kv_buf = (plain_dot(x_buf, w_kv) + interleaved(jnp.zeros_like(b_value), b_value)).astype(BF)
+    context_rows = attend(near, picks, spans, query_rows, kv_buf)
 
     input_float = layer_input.astype(F32)
     resid_one = input_float + plain_dot(context_rows, w_output) + b_output
@@ -402,63 +841,70 @@
     layer_out = normed_two.astype(BF)
 
     def scattered(value):
-        return lax.psum_scatter(value.astype(BF), "ctx", scatter_dimension=0, tiled=True).astype(F32)
+        return lax.psum_scatter(value, "ctx", scatter_dimension=0, tiled=True).astype(F32)
 
     grad_two, grad_second_gain, grad_second_shift = second_pull(out_grad.astype(F32))
     grad_two_low = grad_two.astype(BF)
     grad_outer_bias = jnp.sum(grad_two_low.astype(F32), axis=0)
-    grad_outer_weight = scattered(rows_dot(active, grad_two_low))
+    grad_outer_weight = rows_dot(active, grad_two_low).astype(BF)
     grad_inner = gelu_pull(cols_dot(grad_two_low, w_outer))[0].astype(BF)
     grad_inner_bias = jnp.sum(grad_inner.astype(F32), axis=0)
-    grad_inner_weight = scattered(rows_dot(normed_low, grad_inner))
+    grad_inner_weight = rows_dot(normed_low, grad_inner).astype(BF)
     grad_one = grad_two + cols_dot(grad_inner, w_inner)
     grad_resid_one, grad_first_gain, grad_first_shift = first_pull(grad_one)
     grad_one_low = grad_resid_one.astype(BF)
     grad_output_bias = jnp.sum(grad_one_low.astype(F32), axis=0)
-    grad_output_weight = rows_dot(context_rows, grad_one_low)
+    grad_output_weight = rows_dot(context_rows, grad_one_low).astype(BF)
+    slabs = lambda value: value.reshape(devices, -1, m)
+    hidden_blocks = grad_inner_weight.shape[1] // m
+    late_grads = scattered(
+        jnp.concatenate(
+            [slabs(grad_outer_weight), slabs(grad_output_weight)]
+            + [slabs(grad_inner_weight[:, i * m : (i + 1) * m]) for i in range(hidden_blocks)],
+            axis=1,
+        )
+    )[0]
+    outer_rows = outer_weight.shape[0]
+    grad_outer_weight = late_grads[:outer_rows]
+    late_grads = late_grads[outer_rows:].reshape(1 + hidden_blocks, weight_rows, m)
+    grad_output_weight = late_grads[0]
+    grad_inner_weight = jnp.concatenate([late_grads[1 + i] for i in range(hidden_blocks)], axis=1)
     context_gradient = cols_dot(grad_one_low, w_output).astype(BF)
 
-    query_low, grad_key_buf, grad_value_buf = attend_back(
-        near, picks, spans, query_rows, kv_buf, kv_buf, context_gradient
-    )
-    own_lower = REACH * BLOCK
-    grad_kv_buf = jnp.concatenate([grad_key_buf, grad_value_buf], axis=1)
-    kv_total = grad_kv_buf[own_lower : own_lower + row_count].astype(F32)
-    lower = 0
-    for offset in range(-reach_shards, reach_shards + 1):
-        if offset == 0:
-            lower += row_count
-            continue
-        span_rows = edge_rows(abs(offset), own_blocks)
-        target = 0 if offset > 0 else row_count - span_rows
-        got = passed_along(grad_kv_buf[lower : lower + span_rows], "ctx", offset).astype(F32)
-        kv_total = kv_total + jnp.pad(got, ((target, row_count - span_rows - target), (0, 0)))
-        lower += span_rows
-    qkv_low = jnp.concatenate([query_low, kv_total.astype(BF)], axis=1)
-    grad_qkv_weight = rows_dot(layer_input, qkv_low)
-    grad_qkv_bias = jnp.sum(qkv_low.astype(F32), axis=0)
-    grad_input = grad_resid_one + cols_dot(qkv_low, w_qkv)
-    attn_grads = scattered(jnp.concatenate([grad_qkv_weight, grad_output_weight], axis=1))
-    vector_grads = jnp.concatenate(
+    query_low, kv_low, attn_sums = attend_back(near, picks, spans, query_rows, kv_buf, context_gradient)
+    grad_x_buf = cols_dot(kv_low, w_kv).astype(BF)
+    grad_vectors = jnp.concatenate(
         [
-            value.reshape(devices, -1)
-            for value in (
-                grad_qkv_bias[:model_width], grad_qkv_bias[2 * model_width :], grad_output_bias, grad_first_gain,
-                grad_first_shift, grad_outer_bias, grad_second_gain, grad_second_shift, grad_inner_bias,
-            )
+            attn_sums,
+            jnp.stack(
+                [
+                    grad_output_bias, grad_first_gain, grad_first_shift, grad_outer_bias, grad_second_gain,
+                    grad_second_shift,
+                ]
+            ),
+            grad_inner_bias.reshape(-1, m),
         ],
-        axis=1,
-    )
-    vector_sums = lax.psum_scatter(vector_grads, "ctx", scatter_dimension=0, tiled=True)[0]
-    v_query, v_value, v_output, v_gain1, v_shift1, v_outer, v_gain2, v_shift2 = [
-        vector_sums[i * unit : (i + 1) * unit] for i in range(8)
-    ]
-    v_inner = vector_sums[8 * unit :]
-    m = model_width
+        axis=0,
+    )
+    grad_query_weight, grad_key_weight, grad_value_weight, sums, halo_part = reduce_grads(
+        rows_dot(layer_input, query_low).astype(BF).reshape(devices, -1, m),
+        rows_dot(x_buf, kv_low).astype(BF).reshape(devices, -1, 2 * m),
+        grad_vectors,
+        grad_x_buf,
+        row_count,
+        devices,
+    )
+    grad_input = grad_resid_one + cols_dot(query_low, w_query) + halo_part
+    me = lax.axis_index("ctx")
+    own_sums = lax.dynamic_slice_in_dim(sums[:8], me * unit, unit, 1)
+    v_query, v_value, v_output, v_gain1, v_shift1, v_outer, v_gain2, v_shift2 = [own_sums[i] for i in range(8)]
+    inner_unit = inner_bias.shape[0]
+    inner_at = me * inner_unit
+    v_inner = lax.dynamic_slice(sums, (8 + inner_at // m, inner_at % m), (1, inner_unit))[0]
     return (
-        layer_out, grad_input, attn_grads[:, :m], v_query, attn_grads[:, m : 2 * m], attn_grads[:, 2 * m : 3 * m],
-        v_value, attn_grads[:, 3 * m :], v_output, v_gain1, v_shift1, grad_inner_weight, v_inner,
-        grad_outer_weight, v_outer, v_gain2, v_shift2,
+        layer_out, grad_input, grad_query_weight, v_query, grad_key_weight, grad_value_weight, v_value,
+        grad_output_weight, v_output, v_gain1, v_shift1, grad_inner_weight, v_inner, grad_outer_weight, v_outer,
+        v_gain2, v_shift2,
     )
 
 

time: 884 us -> 524 us (0.59)
  waiting for transfers between devices: 248 us -> 0.07 us
  Pallas kernels: 124 us -> 320 us
  starting transfers between devices: 159 us -> 0.12 us
  blocking collectives: 116 us -> 0 us
  local copies, waits for them, and re-layouts: 88.4 us -> 30 us
  matrix products: 92.4 us -> 138 us
  other arithmetic: 33.7 us -> 13.3 us
    pallas_call x2 -> x4, Pallas kernels: 124 us -> 320 us  [the longest x1 92.3 us: gather_weights(): pl.pallas_call(functools.partial(gather_kernel, count), out_shape=(jax.Sh...]
    ppermute x12 -> x0, waiting for transfers between devices: 189 us -> none  [passed_along(): lax.ppermute(value, axis, [(source, source + steps) for source in range(f...]
    ppermute x12 -> x0, starting transfers between devices: 159 us -> none  [passed_along(): lax.ppermute(value, axis, [(source, source + steps) for source in range(f...]
    unnamed x1 -> x0, blocking collectives: 81.9 us -> none
    unnamed x7 -> x3, waiting for transfers between devices: 41.3 us -> 0.05 us
    unnamed x124 -> x94, local copies, waits for them, and re-layouts: 50 us -> 12.5 us
    all_gather x1 -> x0, blocking collectives: 33.7 us -> none  [gathered(): return lax.all_gather(value, 'ctx', axis=0, tiled=True)]
    dot_general x4 -> x5, matrix products: 16 us -> 34.4 us  [rows_dot(): lax.dot_general(left, right, (((0,), (0,)), ((), ())), preferred_element_...]
  transfers between devices with their start and end apart: 18 -> 3, of which waited for: 7 -> 0; matrix products, arithmetic and copies ran while one was open for 20% -> 22% of each run, Pallas kernels for 14% -> 62%
where the time goes in v2:
time: 524 us; the launch traced here: 517 us
  Pallas kernels  320 us (61%)
  matrix products  138 us (26%)
  local copies, waits for them, and re-layouts  30 us (6%)
  between operations  14.9 us (3%)
  other arithmetic  13.3 us (3%)
    pallas_call x1, Pallas kernels, gather_weights(): pl.pallas_call(functools.partial(gather_kernel, count), out_shape=(jax.Sh...  92.3 us
    pallas_call x1, Pallas kernels, reduce_grads(): pl.pallas_call(functools.partial(reduce_kernel, count), out_shape=(jax.Sh...  88.9 us
    pallas_call x1, Pallas kernels, on_device(): attend_back(near, picks, spans, query_rows, kv_buf, context_gradient)  85.7 us
    dot_general x5, matrix products, plain_dot(): return jnp.dot(left, right, preferred_element_type=F32)  58 us
    pallas_call x1, Pallas kernels, on_device(): context_rows = attend(near, picks, spans, query_rows, kv_buf)  53.4 us
    dot_general x5, matrix products, cols_dot(): lax.dot_general(left, right, (((1,), (1,)), ((), ())), preferred_element_...  45.7 us
    dot_general x5, matrix products, rows_dot(): lax.dot_general(left, right, (((0,), (0,)), ((), ())), preferred_element_...  34.4 us
    unnamed x94, local copies, waits for them, and re-layouts  12.5 us
  transfers between devices with their start and end apart: 3, of which 0 were waited for; matrix products, arithmetic and copies ran while one was open for 22% of the time, Pallas kernels for 62%

profile of v2, /device:TPU:6, one launch (start us, length us, event | category | flops | bytes accessed | tf_op | source)
XLA Modules:
  0.0 517.0 jit_solution(10962567885577234643)
XLA Ops:
  9.9 1.6 convert_element_type.129
  13.0 92.3 %gather_weights.1 = (bf16[32,24,2304]{2,1,0:T(8,128)(2,1)}, bf16[32,1,384]{2,1,0:T(2,128)(2,1)}, bf16[4736,768]{1,0:T(8,128)(2,1)}) custom-call(f32[24,768]{1,0:T(8,128)} %wq_ref.1, f32[24,768]{1,0:T(8,128)} %wk_ref.1, f32[24,768]{1,0:T(8,128)} %wv_ref.1, f32[1,384]{1,0:T(1,128)} %broadcast_in_dim.46.v_ref, bf16[768,768]{1,0:T(8,128)(2,1)} %x_ref.1), custom_call_target="tpu_custom_call" | custom-call | bytes 200000000 | tf_op jit(solution)/shard_map/gather_weights/pallas_call | solution.py:260
  106.7 17.6 %add_convert_fusion.kv_ref = bf16[4736,1536]{1,0:T(8,128)(2,1)} fusion(bf16[4736,768]{1,0:T(8,128)(2,1)} %get-tuple-element.30, f32[1536]{0:T(1024)S(1)} %constant_dynamic-update-slice_fusion.7, bf16[768,2304]{1,0:T(8,128)(2,1)} %bitcast.97), kind=kOutput, calls=%fused_computation | convolution fusion | flops 11188174848 | bytes 24188928 | tf_op jit(solution)/shard_map/dot_general | solution.py:37
  129.6 2.4 fusion.19.q_ref
  132.0 53.4 %attend_forward.1 = bf16[768,768]{1,0:T(8,128)(2,1)S(1)} custom-call(s32[96]{0:T(128)S(1)} %reshape.298.near_ref, s32[432]{0:T(512)S(1)} %reshape.299.rand_ref, s32[48]{0:T(128)S(1)} %reshape.300.glob_ref, bf16[768,768]{1,0:T(8,128)(2,1)S(1)} %fusion.19.q_ref, bf16[4736,1536]{1,0:T(8,128)(2,1)} %add_convert_fusion.kv_ref), custom_call_target="tpu_custom_call" | custom-call | flops 2415919104 | bytes 14548992 | tf_op jit(solution)/shard_map/attend_forward/pallas_call | solution.py:830
  185.5 2.6 fusion.41
  189.6 26.7 %multiply_convert_fusion = (bf16[768,3072]{1,0:T(8,128)(2,1)}, f32[768,3072]{1,0:T(8,128)}, f32[768,3072]{1,0:T(8,128)}) fusion(f32[3072]{0:T(1024)S(1)} %copy-done.24, bf16[768,3840]{1,0:T(8,128)(2,1)S(1)} %copy-done.32, f32[768,768]{1,0:T(8,128)S(1)} %get-tuple-element.93, f32[768]{0:T(1024)S(1)} %copy-done.27, f32[768]{0:T(1024)S(1)} %copy-done.11, ...), kind=kOutput, calls=%fused_computation.5 | convolution fusion | flops 3782541312 | bytes 30699520 | tf_op jit(solution)/shard_map/dot_general | solution.py:37
  216.4 8.6 %fusion.42 = (f32[768]{0:T(1024)S(1)}, f32[768,768]{1,0:T(8,128)S(1)}) fusion(f32[768]{0:T(1024)S(1)} %copy-done.29, bf16[768,3072]{1,0:T(8,128)(2,1)} %get-tuple-element.59, bf16[3072,768]{1,0:T(8,128)(2,1)} %all-gather.5.cloned.1.call-done, f32[768]{0:T(1024)S(1)} %copy-done.28, f32[768]{0:T(1024)S(1)} %copy-done.12, f32[768]{0:T(1024)S(1)} %fusion.27, ...), kind=kOutput, calls=%fused_computation.145 | convolution fusion | flops 3628006656 | bytes 14174208 | tf_op jit(solution)/shard_map/dot_general | solution.py:37
  225.4 1.5 fusion.13
  226.9 2.1 fusion.37
  229.9 4.5 convolution_convert_fusion.2
  234.4 13.8 %convert_reduce_fusion = (f32[3072]{0:T(1024)}, bf16[768,3072]{1,0:T(8,128)(2,1)}) fusion(f32[768,3072]{1,0:T(8,128)} %get-tuple-element.60, f32[768,3072]{1,0:T(8,128)} %get-tuple-element.94, f32[3072]{0:T(1024)S(1)} %copy-done.25, bf16[768,768]{1,0:T(8,128)(2,1)S(1)} %get-tuple-element.52, bf16[3072,768]{1,0:T(8,128)(2,1)} %all-gather.5.cloned.1.call-done), kind=kOutput, calls=%fused_computation.3 | convolution fusion | flops 3663983616 | bytes 29515776 | tf_op jit(solution)/shard_map/dot_general | solution.py:45
  248.2 7.2 %convolution_convert_fusion.1 = bf16[768,3072]{1,0:T(8,128)(2,1)S(1)} fusion(bf16[768,3072]{1,0:T(8,128)(2,1)} %get-tuple-element.50, f32[768,768]{1,0:T(8,128)S(1)} %copy-done.2, f32[768]{0:T(1024)S(1)} %copy-done.28, f32[768]{0:T(1024)S(1)} %copy-done.12, f32[768]{0:T(1024)S(1)} %fusion.27, f32[768]{0:T(1024)S(1)} %broadcast_multiply_fusion.1), kind=kOutput, calls=%fused_computation.20 | convolution fusion | flops 3629187072 | bytes 11808768 | tf_op jit(solution)/shard_map/dot_general | solution.py:41
  255.4 7.5 %multiply_reduce_fusion = (f32[768]{0:T(1024)}, f32[768]{0:T(1024)S(1)}, f32[768]{0:T(1024)}, f32[768,768]{1,0:T(8,128)S(1)}) fusion(f32[768,768]{1,0:T(8,128)S(1)} %copy-done.2, f32[768]{0:T(1024)S(1)} %fusion.27, f32[768]{0:T(1024)S(1)} %broadcast_multiply_fusion.1, f32[768]{0:T(1024)S(1)} %copy-done.12, bf16[768,3072]{1,0:T(8,128)(2,1)S(1)} %copy-done.34, ...), kind=kOutput, calls=%fused_computation.37 | convolution fusion | flops 3629774592 | bytes 16536576 | tf_op jit(solution)/shard_map/dot_general | solution.py:45
  264.1 1.1 copy-done
  266.1 1.1 convolution_convert_fusion.4
  267.2 2.4 constant_dynamic-update-slice_fusion.6
  269.7 1.1 constant_dynamic-update-slice_fusion.5
  270.8 1.1 constant_dynamic-update-slice_fusion.4
  271.9 1.2 constant_dynamic-update-slice_fusion.3
  273.0 1.1 constant_dynamic-update-slice_fusion.2
  274.1 1.1 constant_dynamic-update-slice_fusion.1
  280.1 2.4 convolution_convert_fusion.6.c_ref
  282.6 85.7 %attend_backward.1 = (bf16[768,768]{1,0:T(8,128)(2,1)S(1)}, bf16[4736,1536]{1,0:T(8,128)(2,1)}, f32[2,768]{1,0:T(2,128)S(1)}) custom-call(s32[96]{0:T(128)S(1)} %reshape.298.near_ref, s32[432]{0:T(512)S(1)} %reshape.299.rand_ref, s32[48]{0:T(128)S(1)} %reshape.300.glob_ref, bf16[768,768]{1,0:T(8,128)(2,1)S(1)} %fusion.19.q_ref, ...), custom_call_target="tpu_custom_call" | custom-call | flops 6039797760 | bytes 29097984 | tf_op jit(solution)/shard_map/attend_backward/pallas_call | solution.py:874
  368.4 1.3 concatenate.22.v_ref
  369.6 3.6 convolution_convert_fusion.5
  373.2 18.1 %convolution_convert_fusion.3 = bf16[768,1536]{1,0:T(8,128)(2,1)} fusion(bf16[4736,768]{1,0:T(8,128)(2,1)} %get-tuple-element.30, bf16[4736,1536]{1,0:T(8,128)(2,1)} %get-tuple-element.32), kind=kOutput, calls=%fused_computation.31 | convolution fusion | flops 11174805504 | bytes 24182784 | tf_op jit(solution)/shard_map/dot_general | solution.py:41
  391.3 16.7 %convolution_convert_fusion.x_ref = bf16[4736,768]{1,0:T(8,128)(2,1)} fusion(bf16[4736,1536]{1,0:T(8,128)(2,1)} %get-tuple-element.32, bf16[768,2304]{1,0:T(8,128)(2,1)S(1)} %bitcast.100), kind=kOutput, calls=%fused_computation.19 | convolution fusion | flops 11177263104 | bytes 24182784 | tf_op jit(solution)/shard_map/dot_general | solution.py:45
  408.0 88.9 %reduce_grads.1 = (f32[24,768]{1,0:T(8,128)}, f32[24,768]{1,0:T(8,128)}, f32[24,768]{1,0:T(8,128)}, f32[12,768]{1,0:T(8,128)}, f32[768,768]{1,0:T(8,128)}) custom-call(bf16[32,24,768]{2,1,0:T(8,128)(2,1)} %bitcast.94, bf16[32,24,1536]{2,1,0:T(8,128)(2,1)} %bitcast.92, f32[12,768]{1,0:T(8,128)} %concatenate.22.v_ref, ...), custom_call_target="tpu_custom_call" | custom-call | bytes 200000000 | tf_op jit(solution)/shard_map/reduce_grads/pallas_call | solution.py:468
  497.7 1.3 dynamic-slice_bitcast_fusion
  499.6 5.3 %add_add_fusion.2 = f32[768,768]{1,0:T(8,128)} fusion(f32[768,768]{1,0:T(8,128)} %get-tuple-element.34, f32[768,768]{1,0:T(8,128)} %copy-done, bf16[768,768]{1,0:T(8,128)(2,1)S(1)} %get-tuple-element.31, f32[768]{0:T(1024)S(1)} %negate_multiply_fusion.1, bf16[768,2304]{1,0:T(8,128)(2,1)} %bitcast.99), kind=kOutput, calls=%fused_computation.39 | convolution fusion | flops 907739136 | bytes 9440256 | tf_op jit(solution)/shard_map/dot_general | solution.py:45
  504.9 1.0 convert_element_type.146
  (161 shorter events, 25.6 us)
Async XLA Ops:
  7.2 178.3 %all-gather.3.cloned.1.call-start = ((), (), s32[]{:S(2)}) async-start(), calls=%async_computation.1 | async-start | bytes 6082560 | tf_op jit(solution)/shard_map/all_gather | solution.py:805
  9.8 206.5 %all-gather.5.cloned.1.call-start = ((), (), s32[]{:S(2)}) async-start(), calls=%async_computation.2 | async-start | bytes 4866048 | tf_op jit(solution)/shard_map/all_gather | solution.py:805
  11.5 493.4 %reduce-scatter.2.cloned.1.call-start = ((), (), s32[]{:S(2)}) async-start(), calls=%async_computation.3 | async-start | bytes 10948608 | tf_op jit(solution)/shard_map/reduce_scatter | solution.py:844
  106.6 17.7 %copy-start.33 = (s32[24]{0:T(128)S(1)}, s32[24]{0:T(128)}, u32[]{:S(2)}) copy-start(s32[24]{0:T(128)} %param.21) | copy-start | bytes 292
  106.6 18.4 %copy-start.10 = (s32[12,12,3]{1,2,0:T(4,128)S(1)}, s32[12,12,3]{1,2,0:T(4,128)}, u32[]{:S(2)}) copy-start(s32[12,12,3]{1,2,0:T(4,128)} %param.22) | copy-start | bytes 5188
  106.7 23.0 %copy-start.4 = (bf16[768,768]{1,0:T(8,128)(2,1)S(1)}, bf16[768,768]{1,0:T(8,128)(2,1)}, u32[]{:S(2)}) copy-start(bf16[768,768]{1,0:T(8,128)(2,1)} %x_ref.1) | copy-start | bytes 3538948
  185.5 4.1 copy-start.11
  185.5 4.1 copy-start.24
  185.5 4.1 copy-start.27
  185.5 4.1 copy-start.32
  189.6 26.8 %copy-start.12 = (f32[768]{0:T(1024)S(1)}, f32[768]{0:T(1024)}, u32[]{:S(2)}) copy-start(f32[768]{0:T(1024)} %mul.153) | copy-start | bytes 9220
  189.6 26.8 %copy-start.28 = (f32[768]{0:T(1024)S(1)}, f32[768]{0:T(1024)}, u32[]{:S(2)}) copy-start(f32[768]{0:T(1024)} %add.243) | copy-start | bytes 9220
  189.6 26.8 %copy-start.29 = (f32[768]{0:T(1024)S(1)}, f32[768]{0:T(1024)}, u32[]{:S(2)}) copy-start(f32[768]{0:T(1024)} %add.250) | copy-start | bytes 9220
  216.4 9.0 %copy-start.3 = (bf16[768,768]{1,0:T(8,128)(2,1)S(1)}, bf16[768,768]{1,0:T(8,128)(2,1)}, u32[]{:S(2)}) copy-start(bf16[768,768]{1,0:T(8,128)(2,1)} %param.20) | copy-start | bytes 3538948
  226.9 3.0 slice-start
  229.9 4.5 copy-start.25
  234.4 13.8 %copy-start.2 = (f32[768,768]{1,0:T(8,128)S(1)}, f32[768,768]{1,0:T(8,128)}, u32[]{:S(2)}) copy-start(f32[768,768]{1,0:T(8,128)} %copy-done.1) | copy-start | bytes 7077892
  248.2 7.2 %copy-start.34 = (bf16[768,3072]{1,0:T(8,128)(2,1)S(1)}, bf16[768,3072]{1,0:T(8,128)(2,1)}, u32[]{:S(2)}) copy-start(bf16[768,3072]{1,0:T(8,128)(2,1)} %get-tuple-element.50) | copy-start | bytes 14155780
  275.3 3.1 copy-start.31
  275.3 3.6 copy-start.30
  275.3 4.2 copy-start.17
  282.5 85.8 %copy-start.9 = (f32[4,768]{1,0:T(4,128)S(1)}, f32[4,768]{1,0:T(4,128)}, u32[]{:S(2)}) copy-start(f32[4,768]{1,0:T(4,128)} %reshape.309) | copy-start | bytes 36868
  282.5 85.8 %copy-start.18 = (f32[1,768]{1,0:T(1,128)S(1)}, f32[1,768]{1,0:T(1,128)}, u32[]{:S(2)}) copy-start(f32[1,768]{1,0:T(1,128)} %reshape.307) | copy-start | bytes 9220
  282.5 85.8 %copy-start.19 = (f32[1,768]{1,0:T(1,128)S(1)}, f32[1,768]{1,0:T(1,128)}, u32[]{:S(2)}) copy-start(f32[1,768]{1,0:T(1,128)} %reshape.308) | copy-start | bytes 9220
  282.5 85.8 %copy-start.20 = (f32[1,768]{1,0:T(1,128)S(1)}, f32[1,768]{1,0:T(1,128)}, u32[]{:S(2)}) copy-start(f32[1,768]{1,0:T(1,128)} %stack.11) | copy-start | bytes 9220
  282.5 85.8 %copy-start.21 = (f32[1,768]{1,0:T(1,128)S(1)}, f32[1,768]{1,0:T(1,128)}, u32[]{:S(2)}) copy-start(f32[1,768]{1,0:T(1,128)} %reshape.305) | copy-start | bytes 9220
  282.5 85.8 %copy-start.22 = (f32[1,768]{1,0:T(1,128)S(1)}, f32[1,768]{1,0:T(1,128)}, u32[]{:S(2)}) copy-start(f32[1,768]{1,0:T(1,128)} %reshape.306) | copy-start | bytes 9220
  282.6 85.8 %copy-start.23 = (f32[1,768]{1,0:T(1,128)S(1)}, f32[1,768]{1,0:T(1,128)}, u32[]{:S(2)}) copy-start(f32[1,768]{1,0:T(1,128)} %stack.10) | copy-start | bytes 9220
  373.2 18.1 %copy-start.5 = (bf16[32,24,2304]{2,1,0:T(8,128)(2,1)S(1)}, bf16[32,24,2304]{2,1,0:T(8,128)(2,1)}, u32[]{:S(2)}) copy-start(bf16[32,24,2304]{2,1,0:T(8,128)(2,1)} %get-tuple-element.28) | copy-start | bytes 10616836
  499.6 8.5 %copy-start.8 = (f32[24,768]{1,0:T(8,128)S(1)}, f32[24,768]{1,0:T(8,128)}, u32[]{:S(2)}) copy-start(f32[24,768]{1,0:T(8,128)} %get-tuple-element.121) | copy-start | bytes 221188
  499.6 9.1 %copy-start.7 = (f32[24,768]{1,0:T(8,128)S(1)}, f32[24,768]{1,0:T(8,128)}, u32[]{:S(2)}) copy-start(f32[24,768]{1,0:T(8,128)} %get-tuple-element.123) | copy-start | bytes 221188
  499.6 9.8 %copy-start.6 = (f32[24,768]{1,0:T(8,128)S(1)}, f32[24,768]{1,0:T(8,128)}, u32[]{:S(2)}) copy-start(f32[24,768]{1,0:T(8,128)} %get-tuple-element.124) | copy-start | bytes 221188
  (8 other events, 14.1 us)
Sparse Core Ops, SparseCore 0:
  11.5 111.1 all-gather.2
  126.1 63.8 all-gather.4
  275.5 164.5 reduce-scatter.1

commit v3 on v2

--- a/solution.py
+++ b/solution.py
@@ -29,8 +29,10 @@
     return centred * lax.rsqrt(variance + norm_eps) * scale_gain + shift_vec
 
 
-def gelu_exact(inner_pre):
-    return jax.nn.gelu(inner_pre, approximate=False)
+def gelu_and_slope(inner_pre):
+    below = 0.5 + 0.5 * lax.erf(inner_pre * math.sqrt(0.5))
+    density = jnp.exp(-0.5 * inner_pre * inner_pre) * (1.0 / math.sqrt(2.0 * math.pi))
+    return (inner_pre * below, below + inner_pre * density)
 
 
 def plain_dot(left, right):
@@ -534,24 +536,35 @@
     return after, lead
 
 
+def masked(scores, near_ref, block):
+    after, lead = slot_bias(near_ref, block)
+    return jnp.concatenate(
+        [
+            scores[: 2 * BLOCK],
+            scores[2 * BLOCK : 3 * BLOCK] + after,
+            scores[3 * BLOCK : 4 * BLOCK],
+            scores[4 * BLOCK : 5 * BLOCK] + lead,
+            scores[5 * BLOCK :],
+        ],
+        axis=0,
+    )
+
+
 def forward_kernel(heads, own_blocks, near_ref, rand_ref, glob_ref, q_ref, kv_ref, o_ref, s_ref):
     pair = pl.program_id(0)
-    slot_id = lax.broadcasted_iota(jnp.int32, (1, WIDE), 1) // BLOCK
 
     def regular(block, carry):
         rows = pl.ds(pl.multiple_of(block * BLOCK, BLOCK), BLOCK)
         shared, chosen = slots_of(near_ref, rand_ref, block, pair, heads)
         queries = split_pair(q_ref[rows, :] * 0.125)
-        scores = cols_dot(queries, slot_rows(kv_ref, KEY, shared, chosen))
-        after, lead = slot_bias(near_ref, block)
-        scores = scores + jnp.where(slot_id == 2, after, jnp.where(slot_id == 4, lead, 0.0))
-        weights = jnp.exp(scores - jnp.max(scores, axis=1, keepdims=True))
-        probs = weights * (1.0 / jnp.sum(weights, axis=1, keepdims=True))
-        mixed = plain_dot(probs.astype(BF), slot_rows(kv_ref, VALUE, shared, chosen))
+        scores = masked(cols_dot(slot_rows(kv_ref, KEY, shared, chosen), queries), near_ref, block)
+        weights = jnp.exp(scores - jnp.max(scores, axis=0, keepdims=True))
+        probs = weights * (1.0 / jnp.sum(weights, axis=0, keepdims=True))
+        mixed = rows_dot(probs.astype(BF), slot_rows(kv_ref, VALUE, shared, chosen))
         o_ref[rows, :] = join_pair(mixed).astype(BF)
         return carry
 
-    lax.fori_loop(0, own_blocks, regular, 0, unroll=4)
+    lax.fori_loop(0, own_blocks, regular, 0, unroll=own_blocks)
 
     def whole(block, carry):
         @pl.when(glob_ref[block * 4] > 0)
@@ -559,31 +572,30 @@
             rows = pl.ds(pl.multiple_of(block * BLOCK, BLOCK), BLOCK)
             first = glob_ref[block * 4 + 1]
             length = glob_ref[block * 4 + 2]
-            chunks = (length + SLOTS - 1) // SLOTS
             queries = split_pair(q_ref[rows, :] * 0.125)
+            slot_id = lax.broadcasted_iota(jnp.int32, (WIDE, LANES), 0) // BLOCK
 
             def score(step, top):
                 at = pl.ds(pl.multiple_of((first + step * SLOTS) * BLOCK, BLOCK), WIDE)
-                scores = cols_dot(queries, kv_ref[at, KEY])
+                scores = cols_dot(kv_ref[at, KEY], queries)
                 scores = jnp.where(slot_id < length - step * SLOTS, scores, masked_score)
                 s_ref[step] = scores
-                return jnp.maximum(top, jnp.max(scores, axis=1, keepdims=True))
-
-            top = lax.fori_loop(0, chunks, score, jnp.full((LANES, 1), masked_score, F32))
+                return jnp.maximum(top, jnp.max(scores, axis=0, keepdims=True))
+
+            top = lax.fori_loop(0, CHUNKS, score, jnp.full((1, LANES), masked_score, F32), unroll=True)
 
             def mix(step, kept):
                 total, acc = kept
                 at = pl.ds(pl.multiple_of((first + step * SLOTS) * BLOCK, BLOCK), WIDE)
                 weights = jnp.exp(s_ref[step] - top)
                 return (
-                    total + jnp.sum(weights, axis=1, keepdims=True),
-                    acc + plain_dot(weights.astype(BF), kv_ref[at, VALUE]),
+                    total + jnp.sum(weights, axis=0, keepdims=True),
+                    acc + rows_dot(weights.astype(BF), kv_ref[at, VALUE]),
                 )
 
-            total, acc = lax.fori_loop(
-                0, chunks, mix, (jnp.zeros((LANES, 1), F32), jnp.zeros((LANES, LANES), F32))
-            )
-            o_ref[rows, :] = join_pair(acc * (1.0 / total)).astype(BF)
+            total, acc = lax.fori_loop(0, CHUNKS, mix, (jnp.zeros((1, LANES), F32), jnp.zeros((LANES, LANES), F32)), unroll=True)
+            scale = jnp.transpose(jnp.broadcast_to(1.0 / total, (LANES, LANES)))
+            o_ref[rows, :] = join_pair(acc * scale).astype(BF)
 
         return carry
 
@@ -617,18 +629,7 @@
         slope = c_ref[rows, :]
         slope = split_pair(jnp.where(glob_ref[block * 4] > 0, jnp.zeros_like(slope), slope))
         keys = slot_rows(kv_ref, KEY, shared, chosen)
-        scores = cols_dot(keys, queries)
-        after, lead = slot_bias(near_ref, block)
-        scores = jnp.concatenate(
-            [
-                scores[: 2 * BLOCK],
-                scores[2 * BLOCK : 3 * BLOCK] + after,
-                scores[3 * BLOCK : 4 * BLOCK],
-                scores[4 * BLOCK : 5 * BLOCK] + lead,
-                scores[5 * BLOCK :],
-            ],
-            axis=0,
-        )
+        scores = masked(cols_dot(keys, queries), near_ref, block)
         weights = jnp.exp(scores - jnp.max(scores, axis=0, keepdims=True))
         probs = weights * (1.0 / jnp.sum(weights, axis=0, keepdims=True))
         dprobs = cols_dot(slot_rows(kv_ref, VALUE, shared, chosen), slope)
@@ -639,7 +640,7 @@
         add_rows(dv_acc, shared, chosen, plain_dot(probs.astype(BF), slope))
         return carry
 
-    lax.fori_loop(0, own_blocks, regular, 0, unroll=2)
+    lax.fori_loop(0, own_blocks, regular, 0, unroll=6)
 
     def whole(block, carry):
         @pl.when(glob_ref[block * 4] > 0)
@@ -647,7 +648,6 @@
             rows = pl.ds(pl.multiple_of(block * BLOCK, BLOCK), BLOCK)
             first = glob_ref[block * 4 + 1]
             length = glob_ref[block * 4 + 2]
-            chunks = (length + SLOTS - 1) // SLOTS
             queries = split_pair(q_ref[rows, :] * 0.125)
             slope = split_pair(c_ref[rows, :])
             slot_id = lax.broadcasted_iota(jnp.int32, (WIDE, LANES), 0) // BLOCK
@@ -660,7 +660,7 @@
                 p_ref[step] = cols_dot(kv_ref[at, VALUE], slope)
                 return jnp.maximum(top, jnp.max(scores, axis=0, keepdims=True))
 
-            top = lax.fori_loop(0, chunks, score, jnp.full((1, LANES), masked_score, F32))
+            top = lax.fori_loop(0, CHUNKS, score, jnp.full((1, LANES), masked_score, F32), unroll=True)
 
             def weigh(step, kept):
                 total, inner = kept
@@ -672,7 +672,7 @@
                 )
 
             zero_row = jnp.zeros((1, LANES), F32)
-            total, inner = lax.fori_loop(0, chunks, weigh, (zero_row, zero_row))
+            total, inner = lax.fori_loop(0, CHUNKS, weigh, (zero_row, zero_row), unroll=True)
             scale = 1.0 / total
             inner = inner * scale
 
@@ -684,7 +684,7 @@
                 dv_acc[at, :] += plain_dot(probs.astype(BF), slope)
                 return dq_sum + rows_dot(dscores, kv_ref[at, KEY])
 
-            dq_sum = lax.fori_loop(0, chunks, spread, jnp.zeros((LANES, LANES), F32))
+            dq_sum = lax.fori_loop(0, CHUNKS, spread, jnp.zeros((LANES, LANES), F32), unroll=True)
             dq_ref[rows, :] = (join_pair(dq_sum) * 0.125).astype(BF)
 
         return carry
@@ -711,7 +711,7 @@
             grid=(pairs,),
             in_specs=[own(), both()],
             out_specs=own(),
-            scratch_shapes=[pltpu.VMEM((CHUNKS, LANES, WIDE), F32)],
+            scratch_shapes=[pltpu.VMEM((CHUNKS, WIDE, LANES), F32)],
         ),
         compiler_params=params(),
         cost_estimate=pl.CostEstimate(
@@ -834,8 +834,8 @@
     normed_one, first_pull = jax.vjp(layer_norm, resid_one, g_first, s_first)
     normed_low = normed_one.astype(BF)
     inner_pre = plain_dot(normed_low, w_inner) + b_inner
-    active_f, gelu_pull = jax.vjp(gelu_exact, inner_pre)
-    active = active_f.astype(BF)
+    active, active_slope = gelu_and_slope(inner_pre)
+    active, active_slope = lax.optimization_barrier((active.astype(BF), active_slope))
     resid_two = normed_one + plain_dot(active, w_outer) + b_outer
     normed_two, second_pull = jax.vjp(layer_norm, resid_two, g_second, s_second)
     layer_out = normed_two.astype(BF)
@@ -847,7 +847,7 @@
     grad_two_low = grad_two.astype(BF)
     grad_outer_bias = jnp.sum(grad_two_low.astype(F32), axis=0)
     grad_outer_weight = rows_dot(active, grad_two_low).astype(BF)
-    grad_inner = gelu_pull(cols_dot(grad_two_low, w_outer))[0].astype(BF)
+    grad_inner = (cols_dot(grad_two_low, w_outer) * active_slope).astype(BF)
     grad_inner_bias = jnp.sum(grad_inner.astype(F32), axis=0)
     grad_inner_weight = rows_dot(normed_low, grad_inner).astype(BF)
     grad_one = grad_two + cols_dot(grad_inner, w_inner)

time: 524 us -> 476 us (0.908)
  Pallas kernels: 320 us -> 269 us
  matrix products: 138 us -> 114 us
  waiting for transfers between devices: 0.07 us -> 20.9 us
    pallas_call x1, Pallas kernels: 53.4 us -> 25.9 us  [on_device(): context_rows = attend(near, picks, spans, query_rows, kv_buf)]
    all_gather x2, waiting for transfers between devices: 0.02 us -> 20.8 us  [gathered(): return lax.all_gather(value, 'ctx', axis=0, tiled=True)]
    dot_general x5, matrix products: 58 us -> 37.6 us  [plain_dot(): return jnp.dot(left, right, preferred_element_type=F32)]
    pallas_call x1, Pallas kernels: 85.7 us -> 70 us  [on_device(): attend_back(near, picks, spans, query_rows, kv_buf, context_gradient)]
    pallas_call x1, Pallas kernels: 88.9 us -> 83 us  [reduce_grads(): pl.pallas_call(functools.partial(reduce_kernel, count), out_shape=(jax.Sh...]
    unnamed x94 -> x88, local copies, waits for them, and re-layouts: 12.5 us -> 14.9 us
  transfers between devices with their start and end apart: 3 -> 3, of which waited for: 0 -> 1; matrix products, arithmetic and copies ran while one was open for 22% -> 20% of each run, Pallas kernels for 62% -> 58%
where the time goes in v3:
time: 476 us; the launch traced here: 466 us
  Pallas kernels  269 us (57%)
  matrix products  114 us (24%)
  local copies, waits for them, and re-layouts  32.4 us (7%)
  waiting for transfers between devices  20.9 us (4%)
  other arithmetic  14.9 us (3%)
  between operations  14.6 us (3%)
    pallas_call x1, Pallas kernels, gather_weights(): pl.pallas_call(functools.partial(gather_kernel, count), out_shape=(jax.Sh...  90.5 us
    pallas_call x1, Pallas kernels, reduce_grads(): pl.pallas_call(functools.partial(reduce_kernel, count), out_shape=(jax.Sh...  83 us
    pallas_call x1, Pallas kernels, on_device(): attend_back(near, picks, spans, query_rows, kv_buf, context_gradient)  70 us
    dot_general x5, matrix products, cols_dot(): lax.dot_general(left, right, (((1,), (1,)), ((), ())), preferred_element_...  42.3 us
    dot_general x5, matrix products, plain_dot(): return jnp.dot(left, right, preferred_element_type=F32)  37.6 us
    dot_general x5, matrix products, rows_dot(): lax.dot_general(left, right, (((0,), (0,)), ((), ())), preferred_element_...  34 us
    pallas_call x1, Pallas kernels, on_device(): context_rows = attend(near, picks, spans, query_rows, kv_buf)  25.9 us
    all_gather x2, waiting for transfers between devices, gathered(): return lax.all_gather(value, 'ctx', axis=0, tiled=True)  20.8 us
  transfers between devices with their start and end apart: 3, of which 1 were waited for; matrix products, arithmetic and copies ran while one was open for 20% of the time, Pallas kernels for 58%

profile of v3, /device:TPU:6, one launch (start us, length us, event | category | flops | bytes accessed | tf_op | source)
XLA Modules:
  0.0 466.2 jit_solution(10257392855348797553)
XLA Ops:
  10.0 1.6 convert_element_type.129
  15.6 90.5 %gather_weights.1 = (bf16[32,24,2304]{2,1,0:T(8,128)(2,1)}, bf16[32,1,384]{2,1,0:T(2,128)(2,1)}, bf16[4736,768]{1,0:T(8,128)(2,1)}) custom-call(f32[24,768]{1,0:T(8,128)} %wq_ref.1, f32[24,768]{1,0:T(8,128)} %wk_ref.1, f32[24,768]{1,0:T(8,128)} %wv_ref.1, f32[1,384]{1,0:T(1,128)} %broadcast_in_dim.46.v_ref, bf16[768,768]{1,0:T(8,128)(2,1)} %x_ref.1), custom_call_target="tpu_custom_call" | custom-call | bytes 200000000 | tf_op jit(solution)/shard_map/gather_weights/pallas_call | solution.py:262
  111.6 2.5 fusion.17.q_ref
  114.2 2.1 copy-done.29
  116.3 14.3 %add_convert_fusion.kv_ref = bf16[4736,1536]{1,0:T(8,128)(2,1)} fusion(bf16[4736,768]{1,0:T(8,128)(2,1)S(1)} %copy-done.29, f32[1536]{0:T(1024)S(1)} %constant_dynamic-update-slice_fusion.7, bf16[768,2304]{1,0:T(8,128)(2,1)S(1)} %bitcast.99), kind=kOutput, calls=%fused_computation | convolution fusion | flops 11188174848 | bytes 24190976 | tf_op jit(solution)/shard_map/dot_general | solution.py:39
  130.6 25.9 %attend_forward.1 = bf16[768,768]{1,0:T(8,128)(2,1)S(1)} custom-call(s32[96]{0:T(128)S(1)} %reshape.298.near_ref, s32[432]{0:T(512)S(1)} %reshape.299.rand_ref, s32[48]{0:T(128)S(1)} %reshape.300.glob_ref, bf16[768,768]{1,0:T(8,128)(2,1)S(1)} %fusion.17.q_ref, bf16[4736,1536]{1,0:T(8,128)(2,1)} %add_convert_fusion.kv_ref), custom_call_target="tpu_custom_call" | custom-call | flops 2415919104 | bytes 14548992 | tf_op jit(solution)/shard_map/attend_forward/pallas_call | solution.py:830
  156.5 2.6 fusion.38
  160.1 9.6 %fusion.3 = (f32[768,3072]{1,0:T(8,128)}, bf16[768,3072]{1,0:T(8,128)(2,1)}) fusion(f32[3072]{0:T(1024)S(1)} %copy-done.23, bf16[768,3840]{1,0:T(8,128)(2,1)S(1)} %copy-done.30, f32[768,768]{1,0:T(8,128)S(1)} %get-tuple-element.95, f32[768]{0:T(1024)S(1)} %copy-done.25, f32[768]{0:T(1024)S(1)} %copy-done.11, f32[768]{0:T(1024)S(1)} %fusion.25, ...), kind=kOutput, calls=%fused_computation.5 | convolution fusion | flops 3652780032 | bytes 21262336 | tf_op jit(solution)/shard_map/dot_general | solution.py:39
  169.7 20.8 %all-gather.5.cloned.1.call-done = bf16[3072,768]{1,0:T(8,128)(2,1)} async-done(((bf16[96,768]{1,0:T(8,128)(2,1)}), bf16[3072,768]{1,0:T(8,128)(2,1)}) %all-gather.5.cloned.1.call-update) | async-done | bytes 4718608 | tf_op jit(solution)/shard_map/all_gather | solution.py:805
  190.5 8.5 %fusion.39 = (f32[768]{0:T(1024)S(1)}, f32[768,768]{1,0:T(8,128)S(1)}) fusion(f32[768]{0:T(1024)S(1)} %copy-done.26, bf16[768,3072]{1,0:T(8,128)(2,1)} %get-tuple-element.33, bf16[3072,768]{1,0:T(8,128)(2,1)} %all-gather.5.cloned.1.call-done, f32[768]{0:T(1024)S(1)} %copy-done.25, f32[768]{0:T(1024)S(1)} %copy-done.11, f32[768]{0:T(1024)S(1)} %fusion.25, ...), kind=kOutput, calls=%fused_computation.136 | convolution fusion | flops 3628006656 | bytes 14174208 | tf_op jit(solution)/shard_map/dot_general | solution.py:39
  200.3 1.5 fusion.11
  201.8 2.1 fusion.35
  204.8 4.2 convolution_convert_fusion.2
  209.1 10.0 %convert_reduce_fusion = (f32[3072]{0:T(1024)}, bf16[768,3072]{1,0:T(8,128)(2,1)}) fusion(f32[768,3072]{1,0:T(8,128)} %get-tuple-element.34, bf16[768,768]{1,0:T(8,128)(2,1)S(1)} %get-tuple-element.54, bf16[3072,768]{1,0:T(8,128)(2,1)} %all-gather.5.cloned.1.call-done), kind=kOutput, calls=%fused_computation.6 | convolution fusion | flops 3633312768 | bytes 20066304 | tf_op jit(solution)/shard_map/dot_general | solution.py:47
  219.1 7.1 %convolution_convert_fusion.1 = bf16[768,3072]{1,0:T(8,128)(2,1)S(1)} fusion(bf16[768,3072]{1,0:T(8,128)(2,1)} %get-tuple-element.100, f32[768,768]{1,0:T(8,128)S(1)} %copy-done.2, f32[768]{0:T(1024)S(1)} %copy-done.25, f32[768]{0:T(1024)S(1)} %copy-done.11, f32[768]{0:T(1024)S(1)} %fusion.25, f32[768]{0:T(1024)S(1)} %broadcast_multiply_fusion.1), kind=kOutput, calls=%fused_computation.11 | convolution fusion | flops 3629187072 | bytes 11808768 | tf_op jit(solution)/shard_map/dot_general | solution.py:43
  226.2 7.4 %multiply_reduce_fusion = (f32[768]{0:T(1024)}, f32[768]{0:T(1024)S(1)}, f32[768]{0:T(1024)}, f32[768,768]{1,0:T(8,128)S(1)}) fusion(f32[768,768]{1,0:T(8,128)S(1)} %copy-done.2, f32[768]{0:T(1024)S(1)} %fusion.25, f32[768]{0:T(1024)S(1)} %broadcast_multiply_fusion.1, f32[768]{0:T(1024)S(1)} %copy-done.11, bf16[768,3072]{1,0:T(8,128)(2,1)S(1)} %copy-done.31, ...), kind=kOutput, calls=%fused_computation.28 | convolution fusion | flops 3629774592 | bytes 16536576 | tf_op jit(solution)/shard_map/dot_general | solution.py:47
  236.8 1.1 convolution_convert_fusion.4
  237.9 2.5 constant_dynamic-update-slice_fusion.6
  240.4 1.2 constant_dynamic-update-slice_fusion.5
  241.5 1.1 constant_dynamic-update-slice_fusion.4
  242.7 1.1 constant_dynamic-update-slice_fusion.3
  243.8 1.1 constant_dynamic-update-slice_fusion.2
  244.9 1.1 constant_dynamic-update-slice_fusion.1
  250.9 2.4 convolution_convert_fusion.6.c_ref
  253.4 70.0 %attend_backward.1 = (bf16[768,768]{1,0:T(8,128)(2,1)S(1)}, bf16[4736,1536]{1,0:T(8,128)(2,1)}, f32[2,768]{1,0:T(2,128)S(1)}) custom-call(s32[96]{0:T(128)S(1)} %reshape.298.near_ref, s32[432]{0:T(512)S(1)} %reshape.299.rand_ref, s32[48]{0:T(128)S(1)} %reshape.300.glob_ref, bf16[768,768]{1,0:T(8,128)(2,1)S(1)} %fusion.17.q_ref, ...), custom_call_target="tpu_custom_call" | custom-call | flops 6039797760 | bytes 29097984 | tf_op jit(solution)/shard_map/attend_backward/pallas_call | solution.py:874
  323.4 1.3 concatenate.22.v_ref
  324.7 3.5 convolution_convert_fusion.5
  328.1 18.1 %convolution_convert_fusion.3 = bf16[768,1536]{1,0:T(8,128)(2,1)} fusion(bf16[4736,768]{1,0:T(8,128)(2,1)} %get-tuple-element.32, bf16[4736,1536]{1,0:T(8,128)(2,1)} %get-tuple-element.36), kind=kOutput, calls=%fused_computation.22 | convolution fusion | flops 11174805504 | bytes 24182784 | tf_op jit(solution)/shard_map/dot_general | solution.py:43
  346.2 17.2 %convolution_convert_fusion.x_ref = bf16[4736,768]{1,0:T(8,128)(2,1)} fusion(bf16[4736,1536]{1,0:T(8,128)(2,1)} %get-tuple-element.36, bf16[768,2304]{1,0:T(8,128)(2,1)S(1)} %bitcast.100), kind=kOutput, calls=%fused_computation.10 | convolution fusion | flops 11177263104 | bytes 24182784 | tf_op jit(solution)/shard_map/dot_general | solution.py:47
  363.4 83.0 %reduce_grads.1 = (f32[24,768]{1,0:T(8,128)}, f32[24,768]{1,0:T(8,128)}, f32[24,768]{1,0:T(8,128)}, f32[12,768]{1,0:T(8,128)}, f32[768,768]{1,0:T(8,128)}) custom-call(bf16[32,24,768]{2,1,0:T(8,128)(2,1)} %bitcast.94, bf16[32,24,1536]{2,1,0:T(8,128)(2,1)} %bitcast.92, f32[12,768]{1,0:T(8,128)} %concatenate.22.v_ref, ...), custom_call_target="tpu_custom_call" | custom-call | bytes 200000000 | tf_op jit(solution)/shard_map/reduce_grads/pallas_call | solution.py:470
  447.2 1.3 dynamic-slice_bitcast_fusion
  449.1 5.3 %add_add_fusion.2 = f32[768,768]{1,0:T(8,128)} fusion(f32[768,768]{1,0:T(8,128)} %get-tuple-element.38, f32[768,768]{1,0:T(8,128)} %copy-done, bf16[768,768]{1,0:T(8,128)(2,1)S(1)} %get-tuple-element.35, f32[768]{0:T(1024)S(1)} %negate_multiply_fusion, bf16[768,2304]{1,0:T(8,128)(2,1)} %bitcast.98), kind=kOutput, calls=%fused_computation.30 | convolution fusion | flops 907739136 | bytes 9440256 | tf_op jit(solution)/shard_map/dot_general | solution.py:47
  (155 shorter events, 29.4 us)
Async XLA Ops:
  7.2 104.4 %copy-start.4 = (bf16[768,768]{1,0:T(8,128)(2,1)S(1)}, bf16[768,768]{1,0:T(8,128)(2,1)}, u32[]{:S(2)}) copy-start(bf16[768,768]{1,0:T(8,128)(2,1)} %x_ref.1) | copy-start | bytes 3538948
  7.2 149.3 %all-gather.3.cloned.1.call-start = ((), (), s32[]{:S(2)}) async-start(), calls=%async_computation.1 | async-start | bytes 6082560 | tf_op jit(solution)/shard_map/all_gather | solution.py:805
  9.9 180.6 %all-gather.5.cloned.1.call-start = ((), (), s32[]{:S(2)}) async-start(), calls=%async_computation.2 | async-start | bytes 4866048 | tf_op jit(solution)/shard_map/all_gather | solution.py:805
  11.6 442.8 %reduce-scatter.2.cloned.1.call-start = ((), (), s32[]{:S(2)}) async-start(), calls=%async_computation.3 | async-start | bytes 10948608 | tf_op jit(solution)/shard_map/reduce_scatter | solution.py:844
  111.6 2.6 copy-start.5
  111.6 4.7 %copy-start.29 = (bf16[4736,768]{1,0:T(8,128)(2,1)S(1)}, bf16[4736,768]{1,0:T(8,128)(2,1)}, u32[]{:S(2)}) copy-start(bf16[4736,768]{1,0:T(8,128)(2,1)} %get-tuple-element.32) | copy-start | bytes 21823492
  156.5 3.1 copy-start.30
  159.1 10.5 %copy-start.1 = (f32[768,768]{1,0:T(8,128)}, f32[768,768]{1,0:T(8,128)S(1)}, u32[]{:S(2)}) copy-start(f32[768,768]{1,0:T(8,128)S(1)} %get-tuple-element.95) | copy-start | bytes 7077892
  160.1 30.4 %copy-start.26 = (f32[768]{0:T(1024)S(1)}, f32[768]{0:T(1024)}, u32[]{:S(2)}) copy-start(f32[768]{0:T(1024)} %add.258) | copy-start | bytes 9220
  199.0 1.3 copy-start.3
  199.5 2.4 copy-start.12
  201.8 3.0 slice-start
  201.8 3.0 slice-start.1
  209.1 10.0 %copy-start.2 = (f32[768,768]{1,0:T(8,128)S(1)}, f32[768,768]{1,0:T(8,128)}, u32[]{:S(2)}) copy-start(f32[768,768]{1,0:T(8,128)} %copy-done.1) | copy-start | bytes 7077892
  219.1 7.1 %copy-start.31 = (bf16[768,3072]{1,0:T(8,128)(2,1)S(1)}, bf16[768,3072]{1,0:T(8,128)(2,1)}, u32[]{:S(2)}) copy-start(bf16[768,3072]{1,0:T(8,128)(2,1)} %get-tuple-element.100) | copy-start | bytes 14155780
  234.5 1.4 copy-start
  246.0 1.9 copy-start.15
  246.0 2.5 copy-start.24
  246.0 3.1 copy-start.28
  246.1 3.6 copy-start.27
  246.1 4.2 copy-start.16
  253.3 70.1 %copy-start.10 = (f32[4,768]{1,0:T(4,128)S(1)}, f32[4,768]{1,0:T(4,128)}, u32[]{:S(2)}) copy-start(f32[4,768]{1,0:T(4,128)} %reshape.309) | copy-start | bytes 36868
  253.3 70.1 %copy-start.17 = (f32[1,768]{1,0:T(1,128)S(1)}, f32[1,768]{1,0:T(1,128)}, u32[]{:S(2)}) copy-start(f32[1,768]{1,0:T(1,128)} %reshape.307) | copy-start | bytes 9220
  253.3 70.0 %copy-start.18 = (f32[1,768]{1,0:T(1,128)S(1)}, f32[1,768]{1,0:T(1,128)}, u32[]{:S(2)}) copy-start(f32[1,768]{1,0:T(1,128)} %reshape.308) | copy-start | bytes 9220
  253.3 70.0 %copy-start.19 = (f32[1,768]{1,0:T(1,128)S(1)}, f32[1,768]{1,0:T(1,128)}, u32[]{:S(2)}) copy-start(f32[1,768]{1,0:T(1,128)} %stack.11) | copy-start | bytes 9220
  253.3 70.0 %copy-start.20 = (f32[1,768]{1,0:T(1,128)S(1)}, f32[1,768]{1,0:T(1,128)}, u32[]{:S(2)}) copy-start(f32[1,768]{1,0:T(1,128)} %reshape.305) | copy-start | bytes 9220
  253.3 70.0 %copy-start.21 = (f32[1,768]{1,0:T(1,128)S(1)}, f32[1,768]{1,0:T(1,128)}, u32[]{:S(2)}) copy-start(f32[1,768]{1,0:T(1,128)} %reshape.306) | copy-start | bytes 9220
  253.4 70.0 %copy-start.22 = (f32[1,768]{1,0:T(1,128)S(1)}, f32[1,768]{1,0:T(1,128)}, u32[]{:S(2)}) copy-start(f32[1,768]{1,0:T(1,128)} %stack.10) | copy-start | bytes 9220
  328.1 18.1 %copy-start.6 = (bf16[32,24,2304]{2,1,0:T(8,128)(2,1)S(1)}, bf16[32,24,2304]{2,1,0:T(8,128)(2,1)}, u32[]{:S(2)}) copy-start(bf16[32,24,2304]{2,1,0:T(8,128)(2,1)} %get-tuple-element.30) | copy-start | bytes 10616836
  454.4 3.2 copy-start.9
  454.4 3.8 copy-start.8
  454.4 4.5 copy-start.7
  (5 other events, 4.6 us)
Sparse Core Ops, SparseCore 0:
  11.5 112.4 all-gather.2
  127.4 63.0 all-gather.4
  246.2 155.7 reduce-scatter.1

commit v4 on v3

--- a/solution.py
+++ b/solution.py
@@ -820,9 +820,19 @@
         vector_all[:, i * unit : (i + 1) * unit].reshape(-1) for i in range(8)
     ]
     b_inner = vector_all[:, 8 * unit : 8 * unit + inner_bias.shape[0]].reshape(-1)
-    w_late = gathered(jnp.concatenate([output_weight, inner_weight], axis=1).astype(BF))
-    w_output, w_inner = w_late[:, :m], w_late[:, m:]
-    w_outer = gathered(outer_weight.astype(BF))
+    outer_rows = outer_weight.shape[0]
+    hidden_blocks = inner_weight.shape[1] // m
+    late = gathered(
+        jnp.concatenate(
+            [outer_weight, output_weight] + [inner_weight[:, i * m : (i + 1) * m] for i in range(hidden_blocks)], axis=0
+        ).astype(BF)[None]
+    )
+    w_outer = late[:, :outer_rows].reshape(-1, m)
+    w_output, *w_inner = [
+        late[:, outer_rows + i * weight_rows : outer_rows + (i + 1) * weight_rows].reshape(m, m)
+        for i in range(1 + hidden_blocks)
+    ]
+    w_inner = jnp.concatenate(w_inner, axis=1)
     w_query, w_kv = w_qkv[:, :m], w_qkv[:, m:]
 
     query_rows = (plain_dot(layer_input, w_query) + b_query).astype(BF)
@@ -856,7 +866,6 @@
     grad_output_bias = jnp.sum(grad_one_low.astype(F32), axis=0)
     grad_output_weight = rows_dot(context_rows, grad_one_low).astype(BF)
     slabs = lambda value: value.reshape(devices, -1, m)
-    hidden_blocks = grad_inner_weight.shape[1] // m
     late_grads = scattered(
         jnp.concatenate(
             [slabs(grad_outer_weight), slabs(grad_output_weight)]
@@ -864,7 +873,6 @@
             axis=1,
         )
     )[0]
-    outer_rows = outer_weight.shape[0]
     grad_outer_weight = late_grads[:outer_rows]
     late_grads = late_grads[outer_rows:].reshape(1 + hidden_blocks, weight_rows, m)
     grad_output_weight = late_grads[0]

time: 476 us -> 476 us (level)
  waiting for transfers between devices: 20.9 us -> 0.07 us
  Pallas kernels: 269 us -> 286 us
  local copies, waits for them, and re-layouts: 32.4 us -> 46 us
  matrix products: 114 us -> 106 us
    pallas_call x1, Pallas kernels: 83 us -> 117 us  [reduce_grads(): pl.pallas_call(functools.partial(reduce_kernel, count), out_shape=(jax.Sh...]
    all_gather x2 -> x1, waiting for transfers between devices: 20.8 us -> 0.02 us  [gathered(): return lax.all_gather(value, 'ctx', axis=0, tiled=True)]
    pallas_call x1, Pallas kernels: 70 us -> 52.1 us  [on_device(): attend_back(near, picks, spans, query_rows, kv_buf, context_gradient)]
    pallas_call x1, Pallas kernels: 90.5 us -> 101 us  [gather_weights(): pl.pallas_call(functools.partial(gather_kernel, count), out_shape=(jax.Sh...]
    pallas_call x1, Pallas kernels: 25.9 us -> 16.8 us  [on_device(): context_rows = attend(near, picks, spans, query_rows, kv_buf)]
    slice x0 -> x2, local copies, waits for them, and re-layouts: none -> 7.54 us  [the longest x1 4.36 us: on_device(): w_outer = late[:, :outer_rows].reshape(-1, m)]
    dot_general x5, matrix products: 37.6 us -> 32.1 us  [plain_dot(): return jnp.dot(left, right, preferred_element_type=F32)]
    unnamed x88 -> x93, local copies, waits for them, and re-layouts: 14.9 us -> 16 us
  transfers between devices with their start and end apart: 3 -> 2, of which waited for: 1 -> 0; matrix products, arithmetic and copies ran while one was open for 20% -> 18% of each run, Pallas kernels for 58% -> 61%
where the time goes in v4:
time: 476 us; the launch traced here: 467 us
  Pallas kernels  286 us (60%)
  matrix products  106 us (22%)
  local copies, waits for them, and re-layouts  46 us (10%)
  between operations  15.2 us (3%)
  other arithmetic  13.5 us (3%)
    pallas_call x1, Pallas kernels, reduce_grads(): pl.pallas_call(functools.partial(reduce_kernel, count), out_shape=(jax.Sh...  117 us
    pallas_call x1, Pallas kernels, gather_weights(): pl.pallas_call(functools.partial(gather_kernel, count), out_shape=(jax.Sh...  101 us
    pallas_call x1, Pallas kernels, on_device(): attend_back(near, picks, spans, query_rows, kv_buf, context_gradient)  52.1 us
    dot_general x5, matrix products, cols_dot(): lax.dot_general(left, right, (((1,), (1,)), ((), ())), preferred_element_...  41 us
    dot_general x5, matrix products, rows_dot(): lax.dot_general(left, right, (((0,), (0,)), ((), ())), preferred_element_...  32.9 us
    dot_general x5, matrix products, plain_dot(): return jnp.dot(left, right, preferred_element_type=F32)  32.1 us
    pallas_call x1, Pallas kernels, on_device(): context_rows = attend(near, picks, spans, query_rows, kv_buf)  16.8 us
    unnamed x93, local copies, waits for them, and re-layouts  16 us
  transfers between devices with their start and end apart: 2, of which 0 were waited for; matrix products, arithmetic and copies ran while one was open for 18% of the time, Pallas kernels for 61%

profile of v4, /device:TPU:6, one launch (start us, length us, event | category | flops | bytes accessed | tf_op | source)
XLA Modules:
  0.0 467.0 jit_solution(11438928425108876672)
XLA Ops:
  15.0 100.6 %gather_weights.1 = (bf16[32,24,2304]{2,1,0:T(8,128)(2,1)}, bf16[32,1,384]{2,1,0:T(2,128)(2,1)}, bf16[4736,768]{1,0:T(8,128)(2,1)}) custom-call(f32[24,768]{1,0:T(8,128)} %wq_ref.1, f32[24,768]{1,0:T(8,128)} %wk_ref.1, f32[24,768]{1,0:T(8,128)} %wv_ref.1, f32[1,384]{1,0:T(1,128)} %broadcast_in_dim.47.v_ref, bf16[768,768]{1,0:T(8,128)(2,1)} %x_ref.1), custom_call_target="tpu_custom_call" | custom-call | bytes 200000000 | tf_op jit(solution)/shard_map/gather_weights/pallas_call | solution.py:262
  121.0 2.5 fusion.11.q_ref
  123.6 2.0 copy-done.30
  125.6 14.3 %add_convert_fusion.kv_ref = bf16[4736,1536]{1,0:T(8,128)(2,1)} fusion(bf16[4736,768]{1,0:T(8,128)(2,1)S(1)} %copy-done.30, f32[1536]{0:T(1024)S(1)} %constant_dynamic-update-slice_fusion.7, bf16[768,2304]{1,0:T(8,128)(2,1)S(1)} %bitcast.139), kind=kOutput, calls=%fused_computation | convolution fusion | flops 11188174848 | bytes 24190976 | tf_op jit(solution)/shard_map/dot_general | solution.py:39
  139.9 16.8 %attend_forward.1 = bf16[768,768]{1,0:T(8,128)(2,1)S(1)} custom-call(s32[96]{0:T(128)S(1)} %reshape.403.near_ref, s32[432]{0:T(512)S(1)} %reshape.404.rand_ref, s32[48]{0:T(128)S(1)} %reshape.405.glob_ref, bf16[768,768]{1,0:T(8,128)(2,1)S(1)} %fusion.11.q_ref, bf16[4736,1536]{1,0:T(8,128)(2,1)} %add_convert_fusion.kv_ref), custom_call_target="tpu_custom_call" | custom-call | flops 2415919104 | bytes 14548992 | tf_op jit(solution)/shard_map/attend_forward/pallas_call | solution.py:840
  156.7 3.2 fusion.35
  159.9 1.2 fusion.38
  162.0 10.0 %fusion.3 = (f32[768,3072]{1,0:T(8,128)}, bf16[768,3072]{1,0:T(8,128)(2,1)S(1)}) fusion(f32[3072]{0:T(1024)S(1)} %copy-done.26, bf16[768,768]{1,0:T(8,128)(2,1)S(1)} %bitcast.127, bf16[768,768]{1,0:T(8,128)(2,1)S(1)} %bitcast.129, bf16[768,768]{1,0:T(8,128)(2,1)S(1)} %bitcast.131, bf16[768,768]{1,0:T(8,128)(2,1)S(1)} %bitcast.125, ...), kind=kOutput, calls=%fused_computation.5 | convolution fusion | flops 3671654400 | bytes 21258240 | tf_op jit(solution)/shard_map/dot_general | solution.py:39
  172.1 4.4 slice.221
  176.5 4.1 fusion.39
  181.8 1.4 fusion.7
  183.3 2.2 fusion.34
  187.4 4.3 convolution_convert_fusion.2
  191.7 8.9 %convert_reduce_fusion = (f32[3072]{0:T(1024)}, bf16[768,3072]{1,0:T(8,128)(2,1)}) fusion(f32[768,3072]{1,0:T(8,128)} %get-tuple-element.34, bf16[768,768]{1,0:T(8,128)(2,1)} %copy-done.8, bf16[3072,768]{1,0:T(8,128)(2,1)S(1)} %bitcast.121), kind=kOutput, calls=%fused_computation.6 | convolution fusion | flops 3633312768 | bytes 20066304 | tf_op jit(solution)/shard_map/dot_general | solution.py:47
  200.6 8.8 %multiply_reduce_fusion = (f32[768]{0:T(1024)}, f32[768]{0:T(1024)S(1)}, f32[768]{0:T(1024)}, f32[768,768]{1,0:T(8,128)S(1)}) fusion(f32[768,768]{1,0:T(8,128)S(1)} %get-tuple-element.100, f32[768]{0:T(1024)S(1)} %fusion.22, f32[768]{0:T(1024)S(1)} %broadcast_multiply_fusion.1, f32[768]{0:T(1024)S(1)} %copy-done.18, ...), kind=kOutput, calls=%fused_computation.25 | convolution fusion | flops 3648648960 | bytes 16536576 | tf_op jit(solution)/shard_map/dot_general | solution.py:47
  209.5 5.2 %convolution_convert_fusion.1 = bf16[768,3072]{1,0:T(8,128)(2,1)S(1)} fusion(bf16[768,3072]{1,0:T(8,128)(2,1)S(1)} %copy-done.31, f32[768,768]{1,0:T(8,128)S(1)} %get-tuple-element.100, f32[768]{0:T(1024)S(1)} %copy-done.27, f32[768]{0:T(1024)S(1)} %copy-done.18, f32[768]{0:T(1024)S(1)} %fusion.22, f32[768]{0:T(1024)S(1)} %broadcast_multiply_fusion.1), kind=kOutput, calls=%fused_computation.11 | convolution fusion | flops 3629187072 | bytes 11808768 | tf_op jit(solution)/shard_map/dot_general | solution.py:43
  219.0 2.5 constant_dynamic-update-slice_fusion.6
  227.2 1.4 reshape.418
  228.6 1.3 reshape.419
  229.8 1.3 stack.11
  231.1 1.3 reshape.420
  232.4 1.3 reshape.416
  233.7 1.3 reshape.417
  235.0 1.3 stack.10
  237.4 52.1 %attend_backward.1 = (bf16[768,768]{1,0:T(8,128)(2,1)S(1)}, bf16[4736,1536]{1,0:T(8,128)(2,1)}, f32[2,768]{1,0:T(2,128)S(1)}) custom-call(s32[96]{0:T(128)S(1)} %reshape.403.near_ref, s32[432]{0:T(512)S(1)} %reshape.404.rand_ref, s32[48]{0:T(128)S(1)} %reshape.405.glob_ref, bf16[768,768]{1,0:T(8,128)(2,1)S(1)} %fusion.11.q_ref, ...), custom_call_target="tpu_custom_call" | custom-call | flops 6039797760 | bytes 29097984 | tf_op jit(solution)/shard_map/attend_backward/pallas_call | solution.py:882
  289.6 1.3 concatenate.51.v_ref
  290.9 3.4 convolution_convert_fusion.5
  294.3 18.9 %convolution_convert_fusion.3 = bf16[768,1536]{1,0:T(8,128)(2,1)} fusion(bf16[4736,768]{1,0:T(8,128)(2,1)} %get-tuple-element.32, bf16[4736,1536]{1,0:T(8,128)(2,1)} %get-tuple-element.36), kind=kOutput, calls=%fused_computation.19 | convolution fusion | flops 11174805504 | bytes 24182784 | tf_op jit(solution)/shard_map/dot_general | solution.py:43
  313.2 16.8 %convolution_convert_fusion.x_ref = bf16[4736,768]{1,0:T(8,128)(2,1)} fusion(bf16[4736,1536]{1,0:T(8,128)(2,1)} %get-tuple-element.36, bf16[768,2304]{1,0:T(8,128)(2,1)S(1)} %bitcast.140), kind=kOutput, calls=%fused_computation.10 | convolution fusion | flops 11177263104 | bytes 24182784 | tf_op jit(solution)/shard_map/dot_general | solution.py:47
  330.0 116.6 %reduce_grads.1 = (f32[24,768]{1,0:T(8,128)}, f32[24,768]{1,0:T(8,128)}, f32[24,768]{1,0:T(8,128)}, f32[12,768]{1,0:T(8,128)}, f32[768,768]{1,0:T(8,128)}) custom-call(bf16[32,24,768]{2,1,0:T(8,128)(2,1)} %bitcast.134, bf16[32,24,1536]{2,1,0:T(8,128)(2,1)} %bitcast.122, f32[12,768]{1,0:T(8,128)} %concatenate.51.v_ref, ...), custom_call_target="tpu_custom_call" | custom-call | bytes 200000000 | tf_op jit(solution)/shard_map/reduce_grads/pallas_call | solution.py:470
  447.4 1.3 dynamic-slice_bitcast_fusion
  449.3 5.3 %add_add_fusion.2 = f32[768,768]{1,0:T(8,128)} fusion(f32[768,768]{1,0:T(8,128)} %get-tuple-element.38, f32[768,768]{1,0:T(8,128)} %copy-done, bf16[768,768]{1,0:T(8,128)(2,1)S(1)} %get-tuple-element.35, f32[768]{0:T(1024)S(1)} %negate_multiply_fusion, bf16[768,2304]{1,0:T(8,128)(2,1)} %bitcast.138), kind=kOutput, calls=%fused_computation.27 | convolution fusion | flops 907739136 | bytes 9440256 | tf_op jit(solution)/shard_map/dot_general | solution.py:47
  (159 shorter events, 34.6 us)
Async XLA Ops:
  7.2 113.8 %copy-start.9 = (bf16[768,768]{1,0:T(8,128)(2,1)S(1)}, bf16[768,768]{1,0:T(8,128)(2,1)}, u32[]{:S(2)}) copy-start(bf16[768,768]{1,0:T(8,128)(2,1)} %x_ref.1) | copy-start | bytes 3538948
  7.2 149.5 %all-gather.2.cloned.1.call-start = ((), (), s32[]{:S(2)}) async-start(), calls=%async_computation.1 | async-start | bytes 10948608 | tf_op jit(solution)/shard_map/all_gather | solution.py:805
  11.0 443.6 %reduce-scatter.2.cloned.1.call-start = ((), (), s32[]{:S(2)}) async-start(), calls=%async_computation.2 | async-start | bytes 10948608 | tf_op jit(solution)/shard_map/reduce_scatter | solution.py:854
  121.0 2.5 copy-start.12
  121.0 4.6 copy-start.30
  156.7 3.3 copy-start.10
  156.7 3.2 copy-start.29
  159.9 1.7 copy-start.2
  159.9 1.7 copy-start.3
  159.9 1.8 copy-start.4
  159.9 2.1 copy-start.5
  172.1 4.4 copy-start.32
  172.1 4.4 copy-start.28
  180.6 1.3 copy-start.1
  181.0 2.3 copy-start.19
  183.3 4.2 slice-start
  183.3 4.1 slice-start.1
  200.6 8.8 %copy-start.31 = (bf16[768,3072]{1,0:T(8,128)(2,1)S(1)}, bf16[768,3072]{1,0:T(8,128)(2,1)}, u32[]{:S(2)}) copy-start(bf16[768,3072]{1,0:T(8,128)(2,1)} %get-tuple-element.105) | copy-start | bytes 14155780
  215.6 1.4 copy-start
  217.9 1.1 copy-start.6
  227.1 9.1 %copy-start.7 = (bf16[768,768]{1,0:T(8,128)(2,1)S(1)}, bf16[768,768]{1,0:T(8,128)(2,1)}, u32[]{:S(2)}) copy-start(bf16[768,768]{1,0:T(8,128)(2,1)} %copy-done.6) | copy-start | bytes 3538948
  237.3 52.2 %copy-start.17 = (f32[4,768]{1,0:T(4,128)S(1)}, f32[4,768]{1,0:T(4,128)}, u32[]{:S(2)}) copy-start(f32[4,768]{1,0:T(4,128)} %reshape.420) | copy-start | bytes 36868
  237.4 52.2 %copy-start.20 = (f32[1,768]{1,0:T(1,128)S(1)}, f32[1,768]{1,0:T(1,128)}, u32[]{:S(2)}) copy-start(f32[1,768]{1,0:T(1,128)} %reshape.418) | copy-start | bytes 9220
  237.4 52.2 %copy-start.21 = (f32[1,768]{1,0:T(1,128)S(1)}, f32[1,768]{1,0:T(1,128)}, u32[]{:S(2)}) copy-start(f32[1,768]{1,0:T(1,128)} %reshape.419) | copy-start | bytes 9220
  237.4 52.2 %copy-start.22 = (f32[1,768]{1,0:T(1,128)S(1)}, f32[1,768]{1,0:T(1,128)}, u32[]{:S(2)}) copy-start(f32[1,768]{1,0:T(1,128)} %stack.11) | copy-start | bytes 9220
  237.4 52.2 %copy-start.23 = (f32[1,768]{1,0:T(1,128)S(1)}, f32[1,768]{1,0:T(1,128)}, u32[]{:S(2)}) copy-start(f32[1,768]{1,0:T(1,128)} %reshape.416) | copy-start | bytes 9220
  237.4 52.2 %copy-start.24 = (f32[1,768]{1,0:T(1,128)S(1)}, f32[1,768]{1,0:T(1,128)}, u32[]{:S(2)}) copy-start(f32[1,768]{1,0:T(1,128)} %reshape.417) | copy-start | bytes 9220
  237.4 52.2 %copy-start.25 = (f32[1,768]{1,0:T(1,128)S(1)}, f32[1,768]{1,0:T(1,128)}, u32[]{:S(2)}) copy-start(f32[1,768]{1,0:T(1,128)} %stack.10) | copy-start | bytes 9220
  294.3 18.9 %copy-start.13 = (bf16[32,24,2304]{2,1,0:T(8,128)(2,1)S(1)}, bf16[32,24,2304]{2,1,0:T(8,128)(2,1)}, u32[]{:S(2)}) copy-start(bf16[32,24,2304]{2,1,0:T(8,128)(2,1)} %get-tuple-element.30) | copy-start | bytes 10616836
  454.6 3.2 copy-start.16
  454.6 3.8 copy-start.15
  454.6 4.5 copy-start.14
  (5 other events, 4.4 us)
Sparse Core Ops, SparseCore 0:
  11.5 134.8 all-gather.1
  227.3 186.1 reduce-scatter.1

commit v5 on v4

--- a/solution.py
+++ b/solution.py
@@ -640,7 +640,7 @@
         add_rows(dv_acc, shared, chosen, plain_dot(probs.astype(BF), slope))
         return carry
 
-    lax.fori_loop(0, own_blocks, regular, 0, unroll=6)
+    lax.fori_loop(0, own_blocks, regular, 0, unroll=own_blocks)
 
     def whole(block, carry):
         @pl.when(glob_ref[block * 4] > 0)

time: 476 us -> 475 us (level)
  no operation moved by 1% of the time
where the time goes in v5:
time: 475 us; the launch traced here: 466 us
  Pallas kernels  286 us (60%)
  matrix products  105 us (22%)
  local copies, waits for them, and re-layouts  46 us (10%)
  between operations  15.3 us (3%)
  other arithmetic  13.5 us (3%)
    pallas_call x1, Pallas kernels, reduce_grads(): pl.pallas_call(functools.partial(reduce_kernel, count), out_shape=(jax.Sh...  118 us
    pallas_call x1, Pallas kernels, gather_weights(): pl.pallas_call(functools.partial(gather_kernel, count), out_shape=(jax.Sh...  101 us
    pallas_call x1, Pallas kernels, on_device(): attend_back(near, picks, spans, query_rows, kv_buf, context_gradient)  51.1 us
    dot_general x5, matrix products, cols_dot(): lax.dot_general(left, right, (((1,), (1,)), ((), ())), preferred_element_...  41 us
    dot_general x5, matrix products, plain_dot(): return jnp.dot(left, right, preferred_element_type=F32)  32.1 us
    dot_general x5, matrix products, rows_dot(): lax.dot_general(left, right, (((0,), (0,)), ((), ())), preferred_element_...  31.9 us
    pallas_call x1, Pallas kernels, on_device(): context_rows = attend(near, picks, spans, query_rows, kv_buf)  16.8 us
    unnamed x93, local copies, waits for them, and re-layouts  16 us
  transfers between devices with their start and end apart: 2, of which 0 were waited for; matrix products, arithmetic and copies ran while one was open for 18% of the time, Pallas kernels for 61%

profile of v5, /device:TPU:6, one launch (start us, length us, event | category | flops | bytes accessed | tf_op | source)
XLA Modules:
  0.0 466.5 jit_solution(13667362505004269713)
XLA Ops:
  15.0 100.6 %gather_weights.1 = (bf16[32,24,2304]{2,1,0:T(8,128)(2,1)}, bf16[32,1,384]{2,1,0:T(2,128)(2,1)}, bf16[4736,768]{1,0:T(8,128)(2,1)}) custom-call(f32[24,768]{1,0:T(8,128)} %wq_ref.1, f32[24,768]{1,0:T(8,128)} %wk_ref.1, f32[24,768]{1,0:T(8,128)} %wv_ref.1, f32[1,384]{1,0:T(1,128)} %broadcast_in_dim.47.v_ref, bf16[768,768]{1,0:T(8,128)(2,1)} %x_ref.1), custom_call_target="tpu_custom_call" | custom-call | bytes 200000000 | tf_op jit(solution)/shard_map/gather_weights/pallas_call | solution.py:262
  121.0 2.5 fusion.11.q_ref
  123.6 2.0 copy-done.30
  125.6 14.3 %add_convert_fusion.kv_ref = bf16[4736,1536]{1,0:T(8,128)(2,1)} fusion(bf16[4736,768]{1,0:T(8,128)(2,1)S(1)} %copy-done.30, f32[1536]{0:T(1024)S(1)} %constant_dynamic-update-slice_fusion.7, bf16[768,2304]{1,0:T(8,128)(2,1)S(1)} %bitcast.139), kind=kOutput, calls=%fused_computation | convolution fusion | flops 11188174848 | bytes 24190976 | tf_op jit(solution)/shard_map/dot_general | solution.py:39
  139.9 16.8 %attend_forward.1 = bf16[768,768]{1,0:T(8,128)(2,1)S(1)} custom-call(s32[96]{0:T(128)S(1)} %reshape.403.near_ref, s32[432]{0:T(512)S(1)} %reshape.404.rand_ref, s32[48]{0:T(128)S(1)} %reshape.405.glob_ref, bf16[768,768]{1,0:T(8,128)(2,1)S(1)} %fusion.11.q_ref, bf16[4736,1536]{1,0:T(8,128)(2,1)} %add_convert_fusion.kv_ref), custom_call_target="tpu_custom_call" | custom-call | flops 2415919104 | bytes 14548992 | tf_op jit(solution)/shard_map/attend_forward/pallas_call | solution.py:840
  156.7 3.2 fusion.35
  159.9 1.2 fusion.38
  162.0 10.0 %fusion.3 = (f32[768,3072]{1,0:T(8,128)}, bf16[768,3072]{1,0:T(8,128)(2,1)S(1)}) fusion(f32[3072]{0:T(1024)S(1)} %copy-done.26, bf16[768,768]{1,0:T(8,128)(2,1)S(1)} %bitcast.127, bf16[768,768]{1,0:T(8,128)(2,1)S(1)} %bitcast.129, bf16[768,768]{1,0:T(8,128)(2,1)S(1)} %bitcast.131, bf16[768,768]{1,0:T(8,128)(2,1)S(1)} %bitcast.125, ...), kind=kOutput, calls=%fused_computation.5 | convolution fusion | flops 3671654400 | bytes 21258240 | tf_op jit(solution)/shard_map/dot_general | solution.py:39
  172.1 4.4 slice.221
  176.5 4.1 fusion.39
  181.8 1.4 fusion.7
  183.3 2.2 fusion.34
  187.4 4.3 convolution_convert_fusion.2
  191.7 8.9 %convert_reduce_fusion = (f32[3072]{0:T(1024)}, bf16[768,3072]{1,0:T(8,128)(2,1)}) fusion(f32[768,3072]{1,0:T(8,128)} %get-tuple-element.34, bf16[768,768]{1,0:T(8,128)(2,1)} %copy-done.8, bf16[3072,768]{1,0:T(8,128)(2,1)S(1)} %bitcast.121), kind=kOutput, calls=%fused_computation.6 | convolution fusion | flops 3633312768 | bytes 20066304 | tf_op jit(solution)/shard_map/dot_general | solution.py:47
  200.6 8.8 %multiply_reduce_fusion = (f32[768]{0:T(1024)}, f32[768]{0:T(1024)S(1)}, f32[768]{0:T(1024)}, f32[768,768]{1,0:T(8,128)S(1)}) fusion(f32[768,768]{1,0:T(8,128)S(1)} %get-tuple-element.100, f32[768]{0:T(1024)S(1)} %fusion.22, f32[768]{0:T(1024)S(1)} %broadcast_multiply_fusion.1, f32[768]{0:T(1024)S(1)} %copy-done.18, ...), kind=kOutput, calls=%fused_computation.25 | convolution fusion | flops 3648648960 | bytes 16536576 | tf_op jit(solution)/shard_map/dot_general | solution.py:47
  209.5 5.2 %convolution_convert_fusion.1 = bf16[768,3072]{1,0:T(8,128)(2,1)S(1)} fusion(bf16[768,3072]{1,0:T(8,128)(2,1)S(1)} %copy-done.31, f32[768,768]{1,0:T(8,128)S(1)} %get-tuple-element.100, f32[768]{0:T(1024)S(1)} %copy-done.27, f32[768]{0:T(1024)S(1)} %copy-done.18, f32[768]{0:T(1024)S(1)} %fusion.22, f32[768]{0:T(1024)S(1)} %broadcast_multiply_fusion.1), kind=kOutput, calls=%fused_computation.11 | convolution fusion | flops 3629187072 | bytes 11808768 | tf_op jit(solution)/shard_map/dot_general | solution.py:43
  219.0 2.5 constant_dynamic-update-slice_fusion.6
  227.2 1.4 reshape.418
  228.6 1.3 reshape.419
  229.8 1.3 stack.11
  231.1 1.3 reshape.420
  232.4 1.3 reshape.416
  233.7 1.3 reshape.417
  235.0 1.3 stack.10
  237.4 51.1 %attend_backward.1 = (bf16[768,768]{1,0:T(8,128)(2,1)S(1)}, bf16[4736,1536]{1,0:T(8,128)(2,1)}, f32[2,768]{1,0:T(2,128)S(1)}) custom-call(s32[96]{0:T(128)S(1)} %reshape.403.near_ref, s32[432]{0:T(512)S(1)} %reshape.404.rand_ref, s32[48]{0:T(128)S(1)} %reshape.405.glob_ref, bf16[768,768]{1,0:T(8,128)(2,1)S(1)} %fusion.11.q_ref, ...), custom_call_target="tpu_custom_call" | custom-call | flops 6039797760 | bytes 29097984 | tf_op jit(solution)/shard_map/attend_backward/pallas_call | solution.py:882
  288.6 1.3 concatenate.51.v_ref
  289.9 3.4 convolution_convert_fusion.5
  293.4 18.0 %convolution_convert_fusion.3 = bf16[768,1536]{1,0:T(8,128)(2,1)} fusion(bf16[4736,768]{1,0:T(8,128)(2,1)} %get-tuple-element.32, bf16[4736,1536]{1,0:T(8,128)(2,1)} %get-tuple-element.36), kind=kOutput, calls=%fused_computation.19 | convolution fusion | flops 11174805504 | bytes 24182784 | tf_op jit(solution)/shard_map/dot_general | solution.py:43
  311.3 16.8 %convolution_convert_fusion.x_ref = bf16[4736,768]{1,0:T(8,128)(2,1)} fusion(bf16[4736,1536]{1,0:T(8,128)(2,1)} %get-tuple-element.36, bf16[768,2304]{1,0:T(8,128)(2,1)S(1)} %bitcast.140), kind=kOutput, calls=%fused_computation.10 | convolution fusion | flops 11177263104 | bytes 24182784 | tf_op jit(solution)/shard_map/dot_general | solution.py:47
  328.1 118.0 %reduce_grads.1 = (f32[24,768]{1,0:T(8,128)}, f32[24,768]{1,0:T(8,128)}, f32[24,768]{1,0:T(8,128)}, f32[12,768]{1,0:T(8,128)}, f32[768,768]{1,0:T(8,128)}) custom-call(bf16[32,24,768]{2,1,0:T(8,128)(2,1)} %bitcast.134, bf16[32,24,1536]{2,1,0:T(8,128)(2,1)} %bitcast.122, f32[12,768]{1,0:T(8,128)} %concatenate.51.v_ref, ...), custom_call_target="tpu_custom_call" | custom-call | bytes 200000000 | tf_op jit(solution)/shard_map/reduce_grads/pallas_call | solution.py:470
  446.9 1.3 dynamic-slice_bitcast_fusion
  448.8 5.3 %add_add_fusion.2 = f32[768,768]{1,0:T(8,128)} fusion(f32[768,768]{1,0:T(8,128)} %get-tuple-element.38, f32[768,768]{1,0:T(8,128)} %copy-done, bf16[768,768]{1,0:T(8,128)(2,1)S(1)} %get-tuple-element.35, f32[768]{0:T(1024)S(1)} %negate_multiply_fusion, bf16[768,2304]{1,0:T(8,128)(2,1)} %bitcast.138), kind=kOutput, calls=%fused_computation.27 | convolution fusion | flops 907739136 | bytes 9440256 | tf_op jit(solution)/shard_map/dot_general | solution.py:47
  (159 shorter events, 34.6 us)
Async XLA Ops:
  7.2 113.8 %copy-start.9 = (bf16[768,768]{1,0:T(8,128)(2,1)S(1)}, bf16[768,768]{1,0:T(8,128)(2,1)}, u32[]{:S(2)}) copy-start(bf16[768,768]{1,0:T(8,128)(2,1)} %x_ref.1) | copy-start | bytes 3538948
  7.2 149.5 %all-gather.2.cloned.1.call-start = ((), (), s32[]{:S(2)}) async-start(), calls=%async_computation.1 | async-start | bytes 10948608 | tf_op jit(solution)/shard_map/all_gather | solution.py:805
  11.0 443.1 %reduce-scatter.2.cloned.1.call-start = ((), (), s32[]{:S(2)}) async-start(), calls=%async_computation.2 | async-start | bytes 10948608 | tf_op jit(solution)/shard_map/reduce_scatter | solution.py:854
  121.0 2.5 copy-start.12
  121.0 4.6 copy-start.30
  156.7 3.3 copy-start.10
  156.7 3.2 copy-start.29
  159.9 1.7 copy-start.2
  159.9 1.7 copy-start.3
  159.9 1.8 copy-start.4
  159.9 2.1 copy-start.5
  172.1 4.4 copy-start.32
  172.1 4.4 copy-start.28
  180.6 1.3 copy-start.1
  181.0 2.3 copy-start.19
  183.3 4.2 slice-start
  183.3 4.1 slice-start.1
  200.6 8.8 %copy-start.31 = (bf16[768,3072]{1,0:T(8,128)(2,1)S(1)}, bf16[768,3072]{1,0:T(8,128)(2,1)}, u32[]{:S(2)}) copy-start(bf16[768,3072]{1,0:T(8,128)(2,1)} %get-tuple-element.105) | copy-start | bytes 14155780
  215.6 1.4 copy-start
  217.9 1.1 copy-start.6
  227.1 9.1 %copy-start.7 = (bf16[768,768]{1,0:T(8,128)(2,1)S(1)}, bf16[768,768]{1,0:T(8,128)(2,1)}, u32[]{:S(2)}) copy-start(bf16[768,768]{1,0:T(8,128)(2,1)} %copy-done.6) | copy-start | bytes 3538948
  237.3 51.2 %copy-start.17 = (f32[4,768]{1,0:T(4,128)S(1)}, f32[4,768]{1,0:T(4,128)}, u32[]{:S(2)}) copy-start(f32[4,768]{1,0:T(4,128)} %reshape.420) | copy-start | bytes 36868
  237.4 51.2 %copy-start.20 = (f32[1,768]{1,0:T(1,128)S(1)}, f32[1,768]{1,0:T(1,128)}, u32[]{:S(2)}) copy-start(f32[1,768]{1,0:T(1,128)} %reshape.418) | copy-start | bytes 9220
  237.4 51.2 %copy-start.21 = (f32[1,768]{1,0:T(1,128)S(1)}, f32[1,768]{1,0:T(1,128)}, u32[]{:S(2)}) copy-start(f32[1,768]{1,0:T(1,128)} %reshape.419) | copy-start | bytes 9220
  237.4 51.2 %copy-start.22 = (f32[1,768]{1,0:T(1,128)S(1)}, f32[1,768]{1,0:T(1,128)}, u32[]{:S(2)}) copy-start(f32[1,768]{1,0:T(1,128)} %stack.11) | copy-start | bytes 9220
  237.4 51.2 %copy-start.23 = (f32[1,768]{1,0:T(1,128)S(1)}, f32[1,768]{1,0:T(1,128)}, u32[]{:S(2)}) copy-start(f32[1,768]{1,0:T(1,128)} %reshape.416) | copy-start | bytes 9220
  237.4 51.2 %copy-start.24 = (f32[1,768]{1,0:T(1,128)S(1)}, f32[1,768]{1,0:T(1,128)}, u32[]{:S(2)}) copy-start(f32[1,768]{1,0:T(1,128)} %reshape.417) | copy-start | bytes 9220
  237.4 51.2 %copy-start.25 = (f32[1,768]{1,0:T(1,128)S(1)}, f32[1,768]{1,0:T(1,128)}, u32[]{:S(2)}) copy-start(f32[1,768]{1,0:T(1,128)} %stack.10) | copy-start | bytes 9220
  293.4 18.0 %copy-start.13 = (bf16[32,24,2304]{2,1,0:T(8,128)(2,1)S(1)}, bf16[32,24,2304]{2,1,0:T(8,128)(2,1)}, u32[]{:S(2)}) copy-start(bf16[32,24,2304]{2,1,0:T(8,128)(2,1)} %get-tuple-element.30) | copy-start | bytes 10616836
  454.1 3.2 copy-start.16
  454.1 3.8 copy-start.15
  454.1 4.5 copy-start.14
  (5 other events, 4.4 us)
Sparse Core Ops, SparseCore 0:
  11.5 134.8 all-gather.1
  227.3 185.9 reduce-scatter.1
